TPU v7x, 256 devices: a whole 4x4x8 slice. The times are simulated.
256 devices in a mesh: ctx: 256 (over y, z, x, core).
Axes of the slice: x: 4, y: 4, z: 8, core: 2. Of those that a mesh axis runs over, the one named last changes fastest.
Arguments:
- queries: bfloat16 [65536, 768], P('ctx'), may hold values from -16 to 16
- keys: bfloat16 [65536, 768], P('ctx'), may hold values from -16 to 16
- values: bfloat16 [65536, 768], P('ctx'), may hold values from -6 to 6
- offsets: int32 [5, 12], replicated, may hold values from 0 to 255, as said below
Outputs:
- attended: bfloat16 [65536, 768], P('ctx')
Inputs may be any that keep to these rules, and one draw needn't show every extreme that they name: offsets[l, h] lies in 0 to min(4 ** l, 256) - 1.
All inputs are finite; a program needn't handle non-finite values.
Results may differ from a plain program's by a relative error of at most 0.0035.
Values may be sent and summed in bfloat16 or wider, within the bound.
No kernel may reach another device: no remote copies, remote signals or barrier semaphores. Data moves between devices by JAX's collectives and lax.ppermute only.
A program may use at most 64 MiB of HBM per device.

v0:
```python
import functools

import jax
import jax.numpy as jnp
from jax import lax
from jax.experimental import pallas as pl
from jax.experimental.pallas import tpu as pltpu
from jax.sharding import PartitionSpec as P

HEADS = 12
PAIRS = 6
LANES = 128
HALF = 64
TOK = 256
WIDTH = 768
NEG = -1e30
SCALE = 0.125
F32 = jnp.float32
BF16 = jnp.bfloat16
SEL = 96
STAT = 16
VMEM = pl.BlockSpec(memory_space=pltpu.VMEM)
SMEM = pl.BlockSpec(memory_space=pltpu.SMEM)


def iota(shape, dim):
    return lax.broadcasted_iota(jnp.int32, shape, dim)


def dot_nt(a, b):
    return lax.dot_general(a, b, (((1,), (1,)), ((), ())), preferred_element_type=F32)


def dot_nn(a, b):
    return jnp.dot(a, b, preferred_element_type=F32)


def lanes_of(pair):
    return slice(pair * LANES, (pair + 1) * LANES)


def split_heads(rows):
    low = iota(rows.shape, 1) < HALF
    zero = jnp.zeros_like(rows)
    return jnp.concatenate([jnp.where(low, rows, zero), jnp.where(low, zero, rows)], 0)


def join_heads(stacked):
    n = stacked.shape[0] // 2
    low = iota((n, LANES), 1) < HALF
    return jnp.where(low, stacked[:n], stacked[n:])


def put_stats(stats, pair, peak, total):
    n = stats.shape[0]
    lane = iota(stats.shape, 1)
    for side in range(2):
        head = 2 * pair + side
        stats = jnp.where(lane == head, peak[side * n:(side + 1) * n], stats)
        stats = jnp.where(lane == STAT + head, total[side * n:(side + 1) * n], stats)
    return stats


def call(body, outs, in_specs, flops, nbytes, grant):
    return pl.pallas_call(
        body,
        compiler_params=pltpu.CompilerParams(vmem_limit_bytes=grant << 20),
        out_shape=outs,
        in_specs=in_specs,
        out_specs=[VMEM] * len(outs),
        cost_estimate=pl.CostEstimate(flops=flops, bytes_accessed=nbytes, transcendentals=0),
    )


def select_kernel(off_ref, q_ref, k_ref, v_ref, q1_ref, near_ref, kv2_ref, f3_ref, f4_ref):
    row = iota((SEL, TOK), 0)
    tok = iota((SEL, TOK), 1)
    base = jnp.where(row < 64, row * 4, jnp.where(row < 80, (row - 64) * 16, (row - 80) * 64))
    base = jnp.where(row < 84, base, 0)
    for pair in range(PAIRS):
        picks = []
        for side in range(2):
            head = 2 * pair + side
            off = jnp.where(
                row < 64,
                off_ref[1, head],
                jnp.where(row < 80, off_ref[2, head], jnp.where(row < 84, off_ref[3, head], off_ref[4, head])),
            )
            hit = (tok == base + off) & (row < 85)
            picks.append(jnp.where(hit, 1.0, 0.0).astype(BF16))
        pick = jnp.concatenate(picks, 0)
        at = lanes_of(pair)
        after = slice(WIDTH + pair * LANES, WIDTH + (pair + 1) * LANES)
        rows = join_heads(dot_nn(pick, q_ref[:, at]) * SCALE).astype(BF16)
        q1_ref[:, at] = rows[0:64]
        near_ref[64:80, at] = rows[64:80]
        near_ref[64:80, after] = rows[80:96]
        for ref, here in ((k_ref, at), (v_ref, after)):
            rows = join_heads(dot_nn(pick, ref[:, at])).astype(BF16)
            near_ref[0:64, here] = rows[0:64]
            kv2_ref[:, here] = rows[64:80]
            f3_ref[:, here] = rows[80:84]
            f4_ref[:, here] = rows[84:85]


def local_kernel(q_ref, k_ref, v_ref, acc_ref, stat_ref):
    half = TOK // 2
    for part in range(2):
        keys = (part + 1) * half
        here = slice(part * half, keys)
        query = iota((2 * half, keys), 0) % half + part * half
        allowed = iota((2 * half, keys), 1) <= query
        stats = jnp.zeros((half, LANES), F32)
        for pair in range(PAIRS):
            at = lanes_of(pair)
            queries = split_heads(q_ref[here, at] * jnp.asarray(SCALE, BF16))
            scores = jnp.where(allowed, dot_nt(queries, k_ref[0:keys, at]), NEG)
            peak = jnp.max(scores, axis=1, keepdims=True)
            weights = jnp.exp(scores - peak)
            total = jnp.sum(weights, axis=1, keepdims=True)
            acc_ref[here, at] = join_heads(dot_nn(weights.astype(BF16), v_ref[0:keys, at]))
            stats = put_stats(stats, pair, peak, total)
        stat_ref[here, :] = stats


def far_kernel(pos_ref, qa_ref, qb_ref, ka_ref, kb_ref, out_ref):
    me = pos_ref[0]
    col = iota((1, 256), 1) & 127
    block = col >> 4
    asker = me ^ ((block & 1) * 2) ^ (((block >> 1) & 1) * 6) ^ (block >> 2)
    q_row = col & 15
    row = iota((32, 1), 0)
    owner = me ^ ((row >> 4) * 8)
    allowed2 = (owner & 15) * 16 + (row & 15) <= (asker & 15) * 16 + q_row
    row = iota((64, 1), 0)
    k_row = row & 7
    owner = me ^ (((row >> 3) & 1) * 32) ^ (((row >> 4) & 1) * 16) ^ ((row >> 5) * 8)
    far_owner = owner ^ ((k_row & 1) * 192) ^ (((k_row >> 1) & 1) * 64)
    q_limit = jnp.where(q_row < 4, (asker & 63) * 4 + q_row, -1)
    third = (owner & 63) * 4 + k_row <= q_limit
    fourth = far_owner <= jnp.where(q_row == 4, asker, -1)
    allowed34 = jnp.where(k_row < 4, third.astype(jnp.int32), fourth.astype(jnp.int32)) > 0
    stat_row = iota((32, 128), 0)
    results = []
    for level, first, allowed in ((0, 0, allowed2), (1, WIDTH, allowed34)):
        low, high = ((32, 48), (0, 32))[level]
        stats = jnp.zeros((32, 128), F32)
        accs = []
        for pair in range(PAIRS):
            at = lanes_of(pair)
            vat = slice(WIDTH + pair * LANES, WIDTH + (pair + 1) * LANES)
            qat = slice(first + pair * LANES, first + (pair + 1) * LANES)
            queries = split_heads(jnp.concatenate([qa_ref[128:192, qat], qb_ref[128:192, qat]], 0))
            keys = jnp.concatenate([ka_ref[low:high, at], kb_ref[low:high, at]], 0)
            values = jnp.concatenate([ka_ref[low:high, vat], kb_ref[low:high, vat]], 0)
            scores = jnp.where(allowed, dot_nt(keys, queries), NEG)
            peak = jnp.max(scores, axis=0, keepdims=True)
            weights = jnp.where(allowed, jnp.exp(scores - peak), 0.0)
            total = jnp.sum(weights, axis=0, keepdims=True)
            acc = lax.dot_general(
                weights.astype(BF16), values, (((0,), (0,)), ((), ())), preferred_element_type=F32
            )
            accs.append(join_heads(acc).astype(BF16))
            for side in range(2):
                here = slice(128 * side, 128 * side + 128)
                stats = jnp.where(stat_row == 2 * pair + side, peak[:, here], stats)
                stats = jnp.where(stat_row == STAT + 2 * pair + side, total[:, here], stats)
        high = stats.astype(BF16).astype(F32)
        mid = (stats - high).astype(BF16).astype(F32)
        low = stats - high - mid
        stats = jnp.concatenate([high, mid, low, jnp.zeros((32, 128), F32)], 0).T.astype(BF16)
        results.append((accs, stats))
    for number in range(8):
        to = (me & 7) ^ ((number & 1) * 2) ^ (((number >> 1) & 1) * 6) ^ (number >> 2)
        for level, begin, rows in ((0, 0, 16), (1, 16, 8)):
            accs, stats = results[level]
            here = slice(number * 16, number * 16 + rows)
            for pair in range(PAIRS):
                out_ref[to, begin:begin + rows, lanes_of(pair)] = accs[pair][here]
            out_ref[to, begin:begin + rows, WIDTH:WIDTH + LANES] = stats[here]


def head_row(off_ref, level, shape, per_lane):
    lane = iota(shape, 1)
    lane = lane if per_lane else lane // HALF
    off = jnp.zeros(shape, jnp.int32)
    for head in range(HEADS):
        off = jnp.where(lane == head, off_ref[level, head], off)
    return off


def near_kernel(off_ref, pos_ref, q1_ref, a1_ref, b1_ref, acc0_ref, stat0_ref, acc_ref, stat_ref):
    me = pos_ref[0]
    col = iota((1, TOK), 1)
    device = me ^ (((col >> 6) & 1) * 2) ^ (col >> 7)
    k_pos = (device & 3) * 64 + (col & 63)
    q_pos = (me & 3) * 64 + (iota((128, 1), 0) & 63)
    allowed = k_pos <= q_pos
    stats = jnp.zeros((64, LANES), F32)
    accs = []
    for pair in range(PAIRS):
        at = lanes_of(pair)
        vat = slice(WIDTH + pair * LANES, WIDTH + (pair + 1) * LANES)
        queries = split_heads(q1_ref[:, at])
        scores = jnp.concatenate([dot_nt(queries, a1_ref[0:128, at]), dot_nt(queries, b1_ref[0:128, at])], 1)
        scores = jnp.where(allowed, scores, NEG)
        peak = jnp.max(scores, axis=1, keepdims=True)
        weights = jnp.exp(scores - peak)
        total = jnp.sum(weights, axis=1, keepdims=True)
        weights = weights.astype(BF16)
        acc = dot_nn(weights[:, 0:128], a1_ref[0:128, vat]) + dot_nn(weights[:, 128:256], b1_ref[0:128, vat])
        accs.append(join_heads(acc))
        stats = put_stats(stats, pair, peak, total)
    lane = iota((TOK, LANES), 1)
    tok = iota((TOK, LANES), 0)
    expand = jnp.where((iota((TOK, 64), 0) >> 2) == iota((TOK, 64), 1), 1.0, 0.0)
    spread = jnp.dot(expand, stats, precision=lax.Precision.HIGHEST, preferred_element_type=F32)
    kept = ((tok & 3) == head_row(off_ref, 1, (1, LANES), True)) & (lane < HEADS)
    stat0 = stat0_ref[...]
    peak0 = jnp.where(lane < HEADS, stat0, 0.0)
    peak1 = jnp.where(kept, spread, NEG)
    best = jnp.maximum(peak0, peak1)
    share0 = jnp.where(lane < HEADS, jnp.exp(peak0 - best), 0.0)
    share1 = jnp.exp(peak1 - best)
    total = share0 * pltpu.roll(stat0, LANES - STAT, 1) + share1 * pltpu.roll(spread, LANES - STAT, 1)
    stat_ref[...] = jnp.where(lane < HEADS, best, pltpu.roll(jnp.where(lane < HEADS, total, 0.0), STAT, 1))
    row_share = lax.dot_general(
        expand, share1, (((0,), (0,)), ((), ())), precision=lax.Precision.HIGHEST, preferred_element_type=F32
    )
    scale0 = over_lanes(share0)
    scale1 = over_lanes(row_share)
    twice = jnp.concatenate([expand.astype(BF16)] * 2, 1)
    for pair in range(PAIRS):
        at = lanes_of(pair)
        high, low = split2(accs[pair] * scale1[:, at])
        rows = dot_nn(twice, jnp.concatenate([high, low], 0))
        lane = iota((1, LANES), 1) >> 6
        off = jnp.where(lane == 0, off_ref[1, 2 * pair], off_ref[1, 2 * pair + 1])
        rows = jnp.where((iota((TOK, LANES), 0) & 3) == off, rows, 0.0)
        acc_ref[:, at] = scale0[:, at] * acc0_ref[:, at] + rows


def split2(value):
    high = value.astype(BF16)
    return high, (value - high.astype(F32)).astype(BF16)


def over_lanes(coeff):
    high, low = split2(coeff)
    lane = iota((2 * LANES, WIDTH), 1) // HALF
    spread = jnp.where((iota((2 * LANES, WIDTH), 0) & (LANES - 1)) == lane, 1.0, 0.0).astype(BF16)
    return dot_nn(jnp.concatenate([high, low], 1), spread)


def final_kernel(off_ref, acc_ref, stat_ref, ret_ref, out_ref):
    lane = iota((24, LANES), 1)
    parts = []
    for number in range(8):
        stats = ret_ref[number, :, WIDTH:WIDTH + LANES].astype(F32)
        parts.append(stats + pltpu.roll(stats, 96, 1) + pltpu.roll(stats, 64, 1))
    peaks = [jnp.where(lane < HEADS, part, NEG) for part in parts]
    peak = functools.reduce(jnp.maximum, peaks)
    factors = [jnp.where(lane < HEADS, jnp.exp(part - peak), 0.0) for part in peaks]
    total = sum(factor * pltpu.roll(part, LANES - STAT, 1) for factor, part in zip(factors, parts))
    spread = over_lanes(jnp.concatenate(factors, 0))
    rows = sum(
        spread[24 * number:24 * number + 24] * ret_ref[number, :, 0:WIDTH].astype(F32) for number in range(8)
    )

    def expanded(value, level):
        if level == 2:
            return jnp.concatenate([jnp.broadcast_to(value[r:r + 1], (16, LANES)) for r in range(16)], 0)
        if level == 3:
            return jnp.concatenate([jnp.broadcast_to(value[16 + r:17 + r], (64, LANES)) for r in range(4)], 0)
        return jnp.broadcast_to(value[20:21], (TOK, LANES))

    lane = iota((TOK, LANES), 1)
    tok = iota((TOK, LANES), 0)
    stat = stat_ref[...]
    level_peaks = [jnp.where(lane < HEADS, stat, 0.0)]
    level_totals = [pltpu.roll(stat, LANES - STAT, 1)]
    for level in (2, 3, 4):
        kept = ((tok & (4**level - 1)) == head_row(off_ref, level, (1, LANES), True)) & (lane < HEADS)
        level_peaks.append(jnp.where(kept, expanded(peak, level), NEG))
        level_totals.append(expanded(total, level))
    best = functools.reduce(jnp.maximum, level_peaks)
    shares = [jnp.where(lane < HEADS, jnp.exp(value - best), 0.0) for value in level_peaks]
    denom = sum(share * value for share, value in zip(shares, level_totals))
    inverse = 1.0 / jnp.where(lane < HEADS, denom, 1.0)
    shares = [share * inverse for share in shares]
    row_shares = [jnp.sum(shares[1][16 * r:16 * r + 16], axis=0, keepdims=True) for r in range(16)]
    row_shares += [jnp.sum(shares[2][64 * r:64 * r + 64], axis=0, keepdims=True) for r in range(4)]
    row_shares += [jnp.sum(shares[3], axis=0, keepdims=True)]
    row_shares += [jnp.zeros((3, LANES), F32)]
    rows = rows * over_lanes(jnp.concatenate(row_shares, 0))
    scale = over_lanes(shares[0])
    hits = [
        iota((4**level, WIDTH), 0) == head_row(off_ref, level, (1, WIDTH), False) for level in (2, 3, 4)
    ]
    for r in range(16):
        here = slice(16 * r, 16 * r + 16)
        inner = slice(16 * (r % 4), 16 * (r % 4) + 16)
        merged = scale[here] * acc_ref[here, :]
        merged = merged + jnp.where(hits[0], rows[r:r + 1], 0.0)
        merged = merged + jnp.where(hits[1][inner], rows[16 + r // 4:17 + r // 4], 0.0)
        merged = merged + jnp.where(hits[2][here], rows[20:21], 0.0)
        out_ref[here, :] = merged.astype(BF16)


def shaped(rows, width, dtype):
    return jax.ShapeDtypeStruct((rows, width), dtype)


def traded(value, mask, count):
    return lax.ppermute(value, "ctx", [(source, source ^ mask) for source in range(count)])


def grown(value, mask, count):
    return jnp.concatenate([value, traded(value, mask, count)], 0)


def program(queries, keys, values, offsets):
    count = lax.axis_size("ctx")
    me = lax.axis_index("ctx").astype(jnp.int32).reshape(1)
    q1, near, kv2, third, fourth = call(
        select_kernel,
        [shaped(64, WIDTH, BF16), shaped(80, 2 * WIDTH, BF16), shaped(16, 2 * WIDTH, BF16),
         shaped(4, 2 * WIDTH, BF16), shaped(1, 2 * WIDTH, BF16)],
        [SMEM] + [VMEM] * 3, 200_000_000, 2_000_000, 12,
    )(offsets, queries, keys, values)
    fourth = grown(fourth, 192, count)
    fourth = grown(fourth, 64, count)
    far = jnp.concatenate([third, fourth], 0)
    far = grown(far, 32, count)
    far = grown(far, 16, count)
    far = jnp.concatenate([far, kv2], 0)
    far_other = traded(far, 8, count)
    near_other = traded(near, 2, count)
    asked = jnp.concatenate([near[64:80], near_other[64:80]], 0)
    asked_other = traded(asked, 6, count)
    both = jnp.concatenate([near[0:64], near_other[0:64], asked, asked_other], 0)
    both_other = traded(both, 1, count)
    acc0, stat0 = call(
        local_kernel, [shaped(TOK, WIDTH, F32), shaped(TOK, LANES, F32)], [VMEM] * 3, 1_000_000_000, 3_000_000, 12,
    )(queries, keys, values)
    (partial,) = call(
        far_kernel, [jax.ShapeDtypeStruct((8, 24, WIDTH + LANES), BF16)], [SMEM] + [VMEM] * 4,
        200_000_000, 600_000, 12,
    )(me, both, both_other, far, far_other)
    groups = [list(range(first, first + 8)) for first in range(0, count, 8)]
    back = lax.all_to_all(partial, "ctx", 0, 0, axis_index_groups=groups)
    acc01, stat01 = call(
        near_kernel, [shaped(TOK, WIDTH, F32), shaped(TOK, LANES, F32)],
        [SMEM, SMEM] + [VMEM] * 5, 600_000_000, 2_000_000, 16,
    )(offsets, me, q1, both, both_other, acc0, stat0)
    (merged,) = call(
        final_kernel, [shaped(TOK, WIDTH, BF16)], [SMEM, VMEM, VMEM, VMEM], 1_000_000_000, 3_000_000, 16,
    )(offsets, acc01, stat01, back)
    return merged


def solution(mesh):
    in_specs = (P("ctx", None), P("ctx", None), P("ctx", None), P())
    return jax.shard_map(program, mesh=mesh, in_specs=in_specs, out_specs=P("ctx", None), check_vma=False)
```

profile of v0, /device:TPU:1, one launch (start us, length us, event | category | flops | bytes accessed | tf_op | source)
XLA Modules:
  0.0 61.1 jit_solution(5738974157055964128)
XLA Ops:
  0.0 1.0 %copy-done = bf16[256,768]{1,0:T(8,128)(2,1)S(1)} copy-done((bf16[256,768]{1,0:T(8,128)(2,1)S(1)}, bf16[256,768]{1,0:T(8,128)(2,1)}, u32[]{:S(2)}) %copy-start) | copy-done | bytes 393240
  1.0 1.0 %copy-done.2 = bf16[256,768]{1,0:T(8,128)(2,1)S(1)} copy-done((bf16[256,768]{1,0:T(8,128)(2,1)S(1)}, bf16[256,768]{1,0:T(8,128)(2,1)}, u32[]{:S(2)}) %copy-start.2) | copy-done | bytes 393240
  2.0 1.0 %copy-done.4 = bf16[256,768]{1,0:T(8,128)(2,1)S(1)} copy-done((bf16[256,768]{1,0:T(8,128)(2,1)S(1)}, bf16[256,768]{1,0:T(8,128)(2,1)}, u32[]{:S(2)}) %copy-start.4) | copy-done | bytes 393240
  3.0 0.7 %copy-done.6 = s32[5,12]{1,0:T(8,128)S(1)} copy-done((s32[5,12]{1,0:T(8,128)S(1)}, s32[5,12]{1,0:T(8,128)}, u32[]{:S(2)}) %copy-start.6) | copy-done | bytes 264
  3.7 1.2 %shard_map.46 = (bf16[64,768]{1,0:T(8,128)(2,1)S(1)}, bf16[80,1536]{1,0:T(8,128)(2,1)S(1)}, bf16[16,1536]{1,0:T(8,128)(2,1)S(1)}, bf16[4,1536]{1,0:T(4,128)(2,1)S(1)}, bf16[1,1536]{1,0:T(2,128)(2,1)S(1)}) custom-call(s32[5,12]{1,0:T(8,128)S(1)} %copy-done.6, bf16[256,768]{1,0:T(8,128)(2,1)S(1)} %copy-done, bf16[256,768]{1,0:T(8,128)(2,1)S(1)} %copy-done.2, ...), custom_call_target="tpu_custom_call" | custom-call | flops 200000000 | bytes 2000000 | tf_op jit(solution)/shard_map/pallas_call | solution.py:325
  4.9 2.1 %collective-permute-start = (bf16[80,1536]{1,0:T(8,128)(2,1)S(1)}, bf16[80,1536]{1,0:T(8,128)(2,1)S(1)}, u32[]{:S(2)}, u32[]{:S(2)}) collective-permute-start(bf16[80,1536]{1,0:T(8,128)(2,1)S(1)} %get-tuple-element.15), channel_id=1, source_target_pairs={{0,2},{1,3},{2,0},{3,1},{4,6},{5,7},{6,4},{7,5},{8,10},{9,11},{10,... | collective-permute-start | bytes 737288 | tf_op jit(solution)/shard_map/ppermute | solution.py:315
  7.0 4.4 %collective-permute-done = bf16[80,1536]{1,0:T(8,128)(2,1)S(1)} collective-permute-done((bf16[80,1536]{1,0:T(8,128)(2,1)S(1)}, bf16[80,1536]{1,0:T(8,128)(2,1)S(1)}, u32[]{:S(2)}, u32[]{:S(2)}) %collective-permute-start) | collective-permute-done | bytes 245792 | tf_op jit(solution)/shard_map/ppermute | solution.py:315
  11.5 3.8 %collective-permute-start.1 = (bf16[32,1536]{1,0:T(8,128)(2,1)S(1)}, bf16[32,1536]{1,0:T(8,128)(2,1)S(1)}, u32[]{:S(2)}, u32[]{:S(2)}) collective-permute-start(bf16[32,1536]{1,0:T(8,128)(2,1)S(1)} %pad_maximum_fusion), channel_id=1, source_target_pairs={{0,6},{1,7},{2,4},{3,5},{4,2},{5,3},{6,0},{7,1},{8,14},{9,15},{10,... | collective-permute-start | bytes 294920 | tf_op jit(solution)/shard_map/ppermute | solution.py:315
  15.3 2.7 %collective-permute-start.3 = (bf16[1,1536]{1,0:T(2,128)(2,1)S(1)}, bf16[1,1536]{1,0:T(2,128)(2,1)S(1)}, u32[]{:S(2)}, u32[]{:S(2)}) collective-permute-start(bf16[1,1536]{1,0:T(2,128)(2,1)S(1)} %get-tuple-element.21), channel_id=1, source_target_pairs={{0,192},{1,193},{2,194},{3,195},{4,196},{5,197},{6,198},{7,199},{8... | collective-permute-start | bytes 9224 | tf_op jit(solution)/shard_map/ppermute | solution.py:315
  18.0 0.0 collective-permute-done.1
  18.0 2.4 %collective-permute-start.2 = (bf16[192,1536]{1,0:T(8,128)(2,1)S(1)}, bf16[192,1536]{1,0:T(8,128)(2,1)S(1)}, u32[]{:S(2)}, u32[]{:S(2)}) collective-permute-start(bf16[192,1536]{1,0:T(8,128)(2,1)S(1)} %constant_dynamic-update-slice_fusion.a1_ref.qa_ref), channel_id=1, source_target_pairs={{0,1},{1,0},{2,3},{3,2},{4,5},{5,4},{6,7},{7,6},{8,9},{9,8},{10,11... | collective-permute-start | bytes 1769480 | tf_op jit(solution)/shard_map/ppermute | solution.py:315
  20.5 0.0 collective-permute-done.3
  20.5 1.2 %collective-permute-start.4 = (bf16[2,1536]{1,0:T(2,128)(2,1)S(1)}, bf16[2,1536]{1,0:T(2,128)(2,1)S(1)}, u32[]{:S(2)}, u32[]{:S(2)}) collective-permute-start(bf16[2,1536]{1,0:T(2,128)(2,1)S(1)} %pad_maximum_fusion.2), channel_id=1, source_target_pairs={{0,64},{1,65},{2,66},{3,67},{4,68},{5,69},{6,70},{7,71},{8,72},{9,... | collective-permute-start | bytes 18440 | tf_op jit(solution)/shard_map/ppermute | solution.py:315
  21.7 1.4 %collective-permute-done.4 = bf16[2,1536]{1,0:T(2,128)(2,1)S(1)} collective-permute-done((bf16[2,1536]{1,0:T(2,128)(2,1)S(1)}, bf16[2,1536]{1,0:T(2,128)(2,1)S(1)}, u32[]{:S(2)}, u32[]{:S(2)}) %collective-permute-start.4) | collective-permute-done | bytes 6176 | tf_op jit(solution)/shard_map/ppermute | solution.py:315
  23.1 6.8 %collective-permute-start.5 = (bf16[8,1536]{1,0:T(8,128)(2,1)S(1)}, bf16[8,1536]{1,0:T(8,128)(2,1)S(1)}, u32[]{:S(2)}, u32[]{:S(2)}) collective-permute-start(bf16[8,1536]{1,0:T(8,128)(2,1)S(1)} %pad_maximum_fusion.1), channel_id=1, source_target_pairs={{0,32},{1,33},{2,34},{3,35},{4,36},{5,37},{6,38},{7,39},{8,40},{9,... | collective-permute-start | bytes 73736 | tf_op jit(solution)/shard_map/ppermute | solution.py:315
  29.9 1.2 %collective-permute-done.5 = bf16[8,1536]{1,0:T(8,128)(2,1)S(1)} collective-permute-done((bf16[8,1536]{1,0:T(8,128)(2,1)S(1)}, bf16[8,1536]{1,0:T(8,128)(2,1)S(1)}, u32[]{:S(2)}, u32[]{:S(2)}) %collective-permute-start.5) | collective-permute-done | bytes 24608 | tf_op jit(solution)/shard_map/ppermute | solution.py:315
  31.1 1.5 %collective-permute-start.6 = (bf16[16,1536]{1,0:T(8,128)(2,1)S(1)}, bf16[16,1536]{1,0:T(8,128)(2,1)S(1)}, u32[]{:S(2)}, u32[]{:S(2)}) collective-permute-start(bf16[16,1536]{1,0:T(8,128)(2,1)S(1)} %concatenate.26), channel_id=1, source_target_pairs={{0,16},{1,17},{2,18},{3,19},{4,20},{5,21},{6,22},{7,23},{8,24},{9,... | collective-permute-start | bytes 147464 | tf_op jit(solution)/shard_map/ppermute | solution.py:315
  32.7 2.4 %collective-permute-done.6 = bf16[16,1536]{1,0:T(8,128)(2,1)S(1)} collective-permute-done((bf16[16,1536]{1,0:T(8,128)(2,1)S(1)}, bf16[16,1536]{1,0:T(8,128)(2,1)S(1)}, u32[]{:S(2)}, u32[]{:S(2)}) %collective-permute-start.6) | collective-permute-done | bytes 49184 | tf_op jit(solution)/shard_map/ppermute | solution.py:315
  35.1 0.1 concatenate.27.ka_ref
  35.2 0.9 %collective-permute-start.7 = (bf16[48,1536]{1,0:T(8,128)(2,1)S(1)}, bf16[48,1536]{1,0:T(8,128)(2,1)S(1)}, u32[]{:S(2)}, u32[]{:S(2)}) collective-permute-start(bf16[48,1536]{1,0:T(8,128)(2,1)S(1)} %concatenate.27.ka_ref), channel_id=1, source_target_pairs={{0,8},{1,9},{2,10},{3,11},{4,12},{5,13},{6,14},{7,15},{8,0},{9,1},... | collective-permute-start | bytes 442376 | tf_op jit(solution)/shard_map/ppermute | solution.py:315
  36.0 3.7 %collective-permute-done.7.kb_ref = bf16[48,1536]{1,0:T(8,128)(2,1)S(1)} collective-permute-done((bf16[48,1536]{1,0:T(8,128)(2,1)S(1)}, bf16[48,1536]{1,0:T(8,128)(2,1)S(1)}, u32[]{:S(2)}, u32[]{:S(2)}) %collective-permute-start.7) | collective-permute-done | bytes 147488 | tf_op jit(solution)/shard_map/ppermute | solution.py:315
  39.8 0.0 collective-permute-done.2.b1_ref.qb_ref
  39.8 2.9 %shard_map.49 = bf16[8,24,896]{2,1,0:T(8,128)(2,1)} custom-call(s32[1]{0:T(128)} %bitcast.pos_ref, bf16[192,1536]{1,0:T(8,128)(2,1)S(1)} %constant_dynamic-update-slice_fusion.a1_ref.qa_ref, bf16[192,1536]{1,0:T(8,128)(2,1)S(1)} %collective-permute-done.2.b1_ref.qb_ref, bf16[48,1536]{1,0:T(8,128)(2,1)S(1)} %concatenate.27.ka_ref, ...), custom_call_target="tpu_custom_call" | custom-call | flops 200000000 | bytes 600000 | tf_op jit(solution)/shard_map/pallas_call | solution.py:346
  42.7 9.0 %all-to-all-start = ((bf16[8,24,896]{2,1,0:T(8,128)(2,1)}), bf16[8,24,896]{2,1,0:T(8,128)(2,1)S(1)}, u32[]{:S(2)}, u32[]{:S(2)}) async-start(bf16[8,24,896]{2,1,0:T(8,128)(2,1)} %shard_map.49), calls=%async_computation | async-start | bytes 688128 | tf_op jit(solution)/shard_map/all_to_all | solution.py:351
  51.7 0.0 copy-done.5
  51.7 0.0 copy-done.1
  51.7 1.3 %shard_map.47 = (f32[256,768]{1,0:T(8,128)S(1)}, f32[256,128]{1,0:T(8,128)S(1)}) custom-call(bf16[256,768]{1,0:T(8,128)(2,1)S(1)} %copy-done.1, bf16[256,768]{1,0:T(8,128)(2,1)S(1)} %copy-done.3, bf16[256,768]{1,0:T(8,128)(2,1)S(1)} %copy-done.5), custom_call_target="tpu_custom_call" | custom-call | flops 1000000000 | bytes 3000000 | tf_op jit(solution)/shard_map/pallas_call | solution.py:343
  53.0 0.0 copy-start.7
  53.0 0.7 %copy-done.7 = s32[5,12]{1,0:T(8,128)S(1)} copy-done((s32[5,12]{1,0:T(8,128)S(1)}, s32[5,12]{1,0:T(8,128)}, u32[]{:S(2)}) %copy-start.7) | copy-done | bytes 264
  53.7 3.2 %shard_map.48 = (f32[256,768]{1,0:T(8,128)S(1)}, f32[256,128]{1,0:T(8,128)S(1)}) custom-call(s32[5,12]{1,0:T(8,128)S(1)} %copy-done.7, s32[1]{0:T(128)} %bitcast.pos_ref, bf16[64,768]{1,0:T(8,128)(2,1)S(1)} %get-tuple-element.14.q1_ref, bf16[192,1536]{1,0:T(8,128)(2,1)S(1)} %constant_dynamic-update-slice_fusion.a1_ref.qa_ref, ...), custom_call_target="tpu_custom_call" | custom-call | flops 600000000 | bytes 2000000 | tf_op jit(solution)/shard_map/pallas_call | solution.py:352
  57.0 2.0 %all-to-all-done.ret_ref = bf16[8,24,896]{2,1,0:T(8,128)(2,1)S(1)} async-done(((bf16[8,24,896]{2,1,0:T(8,128)(2,1)}), bf16[8,24,896]{2,1,0:T(8,128)(2,1)S(1)}, u32[]{:S(2)}, u32[]{:S(2)}) %all-to-all-start) | async-done | bytes 344096 | tf_op jit(solution)/shard_map/all_to_all | solution.py:351
  58.9 2.2 %shard_map.50 = bf16[256,768]{1,0:T(8,128)(2,1)} custom-call(s32[5,12]{1,0:T(8,128)S(1)} %copy-done.7, f32[256,768]{1,0:T(8,128)S(1)} %get-tuple-element.18.acc_ref, f32[256,128]{1,0:T(8,128)S(1)} %get-tuple-element.19.stat_ref, bf16[8,24,896]{2,1,0:T(8,128)(2,1)S(1)} %all-to-all-done.ret_ref), custom_call_target="tpu_custom_call" | custom-call | flops 1000000000 | bytes 3000000 | tf_op jit(solution)/shard_map/pallas_call | solution.py:356
  (17 shorter events, 0.2 us)
Async XLA Ops:
  0.0 1.0 %copy-start = (bf16[256,768]{1,0:T(8,128)(2,1)S(1)}, bf16[256,768]{1,0:T(8,128)(2,1)}, u32[]{:S(2)}) copy-start(bf16[256,768]{1,0:T(8,128)(2,1)} %q_ref.3) | copy-start | bytes 1179652
  1.0 1.0 %copy-start.2 = (bf16[256,768]{1,0:T(8,128)(2,1)S(1)}, bf16[256,768]{1,0:T(8,128)(2,1)}, u32[]{:S(2)}) copy-start(bf16[256,768]{1,0:T(8,128)(2,1)} %k_ref.3) | copy-start | bytes 1179652
  2.0 1.0 %copy-start.4 = (bf16[256,768]{1,0:T(8,128)(2,1)S(1)}, bf16[256,768]{1,0:T(8,128)(2,1)}, u32[]{:S(2)}) copy-start(bf16[256,768]{1,0:T(8,128)(2,1)} %v_ref.3) | copy-start | bytes 1179652
  3.0 0.7 %copy-start.6 = (s32[5,12]{1,0:T(8,128)S(1)}, s32[5,12]{1,0:T(8,128)}, u32[]{:S(2)}) copy-start(s32[5,12]{1,0:T(8,128)} %off_ref.5) | copy-start | bytes 724
  4.9 6.5 %collective-permute-start = (bf16[80,1536]{1,0:T(8,128)(2,1)S(1)}, bf16[80,1536]{1,0:T(8,128)(2,1)S(1)}, u32[]{:S(2)}, u32[]{:S(2)}) collective-permute-start(bf16[80,1536]{1,0:T(8,128)(2,1)S(1)} %get-tuple-element.15), channel_id=1, source_target_pairs={{0,2},{1,3},{2,0},{3,1},{4,6},{5,7},{6,4},{7,5},{8,10},{9,11},{10,... | collective-permute-start | bytes 737288 | tf_op jit(solution)/shard_map/ppermute | solution.py:315
  11.5 6.5 %collective-permute-start.1 = (bf16[32,1536]{1,0:T(8,128)(2,1)S(1)}, bf16[32,1536]{1,0:T(8,128)(2,1)S(1)}, u32[]{:S(2)}, u32[]{:S(2)}) collective-permute-start(bf16[32,1536]{1,0:T(8,128)(2,1)S(1)} %pad_maximum_fusion), channel_id=1, source_target_pairs={{0,6},{1,7},{2,4},{3,5},{4,2},{5,3},{6,0},{7,1},{8,14},{9,15},{10,... | collective-permute-start | bytes 294920 | tf_op jit(solution)/shard_map/ppermute | solution.py:315
  15.3 5.2 %collective-permute-start.3 = (bf16[1,1536]{1,0:T(2,128)(2,1)S(1)}, bf16[1,1536]{1,0:T(2,128)(2,1)S(1)}, u32[]{:S(2)}, u32[]{:S(2)}) collective-permute-start(bf16[1,1536]{1,0:T(2,128)(2,1)S(1)} %get-tuple-element.21), channel_id=1, source_target_pairs={{0,192},{1,193},{2,194},{3,195},{4,196},{5,197},{6,198},{7,199},{8... | collective-permute-start | bytes 9224 | tf_op jit(solution)/shard_map/ppermute | solution.py:315
  18.0 21.7 %collective-permute-start.2 = (bf16[192,1536]{1,0:T(8,128)(2,1)S(1)}, bf16[192,1536]{1,0:T(8,128)(2,1)S(1)}, u32[]{:S(2)}, u32[]{:S(2)}) collective-permute-start(bf16[192,1536]{1,0:T(8,128)(2,1)S(1)} %constant_dynamic-update-slice_fusion.a1_ref.qa_ref), channel_id=1, source_target_pairs={{0,1},{1,0},{2,3},{3,2},{4,5},{5,4},{6,7},{7,6},{8,9},{9,8},{10,11... | collective-permute-start | bytes 1769480 | tf_op jit(solution)/shard_map/ppermute | solution.py:315
  20.5 2.6 %collective-permute-start.4 = (bf16[2,1536]{1,0:T(2,128)(2,1)S(1)}, bf16[2,1536]{1,0:T(2,128)(2,1)S(1)}, u32[]{:S(2)}, u32[]{:S(2)}) collective-permute-start(bf16[2,1536]{1,0:T(2,128)(2,1)S(1)} %pad_maximum_fusion.2), channel_id=1, source_target_pairs={{0,64},{1,65},{2,66},{3,67},{4,68},{5,69},{6,70},{7,71},{8,72},{9,... | collective-permute-start | bytes 18440 | tf_op jit(solution)/shard_map/ppermute | solution.py:315
  23.1 8.0 %collective-permute-start.5 = (bf16[8,1536]{1,0:T(8,128)(2,1)S(1)}, bf16[8,1536]{1,0:T(8,128)(2,1)S(1)}, u32[]{:S(2)}, u32[]{:S(2)}) collective-permute-start(bf16[8,1536]{1,0:T(8,128)(2,1)S(1)} %pad_maximum_fusion.1), channel_id=1, source_target_pairs={{0,32},{1,33},{2,34},{3,35},{4,36},{5,37},{6,38},{7,39},{8,40},{9,... | collective-permute-start | bytes 73736 | tf_op jit(solution)/shard_map/ppermute | solution.py:315
  31.1 4.0 %collective-permute-start.6 = (bf16[16,1536]{1,0:T(8,128)(2,1)S(1)}, bf16[16,1536]{1,0:T(8,128)(2,1)S(1)}, u32[]{:S(2)}, u32[]{:S(2)}) collective-permute-start(bf16[16,1536]{1,0:T(8,128)(2,1)S(1)} %concatenate.26), channel_id=1, source_target_pairs={{0,16},{1,17},{2,18},{3,19},{4,20},{5,21},{6,22},{7,23},{8,24},{9,... | collective-permute-start | bytes 147464 | tf_op jit(solution)/shard_map/ppermute | solution.py:315
  35.2 4.6 %collective-permute-start.7 = (bf16[48,1536]{1,0:T(8,128)(2,1)S(1)}, bf16[48,1536]{1,0:T(8,128)(2,1)S(1)}, u32[]{:S(2)}, u32[]{:S(2)}) collective-permute-start(bf16[48,1536]{1,0:T(8,128)(2,1)S(1)} %concatenate.27.ka_ref), channel_id=1, source_target_pairs={{0,8},{1,9},{2,10},{3,11},{4,12},{5,13},{6,14},{7,15},{8,0},{9,1},... | collective-permute-start | bytes 442376 | tf_op jit(solution)/shard_map/ppermute | solution.py:315
  39.8 11.9 %copy-start.3 = (bf16[256,768]{1,0:T(8,128)(2,1)S(1)}, bf16[256,768]{1,0:T(8,128)(2,1)}, u32[]{:S(2)}) copy-start(bf16[256,768]{1,0:T(8,128)(2,1)} %k_ref.3) | copy-start | bytes 1179652
  39.8 11.9 %copy-start.5 = (bf16[256,768]{1,0:T(8,128)(2,1)S(1)}, bf16[256,768]{1,0:T(8,128)(2,1)}, u32[]{:S(2)}) copy-start(bf16[256,768]{1,0:T(8,128)(2,1)} %v_ref.3) | copy-start | bytes 1179652
  42.7 9.0 %copy-start.1 = (bf16[256,768]{1,0:T(8,128)(2,1)S(1)}, bf16[256,768]{1,0:T(8,128)(2,1)}, u32[]{:S(2)}) copy-start(bf16[256,768]{1,0:T(8,128)(2,1)} %q_ref.3) | copy-start | bytes 1179652
  42.7 16.3 %all-to-all-start = ((bf16[8,24,896]{2,1,0:T(8,128)(2,1)}), bf16[8,24,896]{2,1,0:T(8,128)(2,1)S(1)}, u32[]{:S(2)}, u32[]{:S(2)}) async-start(bf16[8,24,896]{2,1,0:T(8,128)(2,1)} %shard_map.49), calls=%async_computation | async-start | bytes 688128 | tf_op jit(solution)/shard_map/all_to_all | solution.py:351
  53.0 0.7 %copy-start.7 = (s32[5,12]{1,0:T(8,128)S(1)}, s32[5,12]{1,0:T(8,128)}, u32[]{:S(2)}) copy-start(s32[5,12]{1,0:T(8,128)} %off_ref.5) | copy-start | bytes 724
where the time goes:
time: 61.5 us; the launch traced here: 61.1 us
  starting transfers between devices  30.4 us (49%)
  waiting for transfers between devices  15.1 us (25%)
  Pallas kernels  10.8 us (18%)
  local copies, waits for them, and re-layouts  4.51 us (7%)
    ppermute x8, starting transfers between devices, traded(): lax.ppermute(value, 'ctx', [(source, source ^ mask) for source in range(c...  21.4 us
    ppermute x8, waiting for transfers between devices, traded(): lax.ppermute(value, 'ctx', [(source, source ^ mask) for source in range(c...  13.2 us
    all_to_all x1, starting transfers between devices, program(): back = lax.all_to_all(partial, 'ctx', 0, 0, axis_index_groups=groups)  9.01 us
    unnamed x18, local copies, waits for them, and re-layouts  4.39 us
    pallas_call x1, Pallas kernels, program(): call(near_kernel, [shaped(TOK, WIDTH, F32), shaped(TOK, LANES, F32)], [SM...  3.23 us
    pallas_call x1, Pallas kernels, program(): call(far_kernel, [jax.ShapeDtypeStruct((8, 24, WIDTH + LANES), BF16)], [S...  2.9 us
    pallas_call x1, Pallas kernels, program(): call(final_kernel, [shaped(TOK, WIDTH, BF16)], [SMEM, VMEM, VMEM, VMEM],...  2.16 us
    all_to_all x1, waiting for transfers between devices, program(): back = lax.all_to_all(partial, 'ctx', 0, 0, axis_index_groups=groups)  1.98 us
  transfers between devices with their start and end apart: 9, of which 6 were waited for; matrix products, arithmetic and copies ran while one was open for 0% of the time, Pallas kernels for 7%

commit v1 on v0

--- a/solution.py
+++ b/solution.py
@@ -61,9 +61,10 @@
     return stats
 
 
-def call(body, outs, in_specs, flops, nbytes, grant):
+def call(body, outs, in_specs, flops, nbytes, grant, scratch=()):
     return pl.pallas_call(
         body,
+        scratch_shapes=scratch,
         compiler_params=pltpu.CompilerParams(vmem_limit_bytes=grant << 20),
         out_shape=outs,
         in_specs=in_specs,
@@ -72,7 +73,15 @@
     )
 
 
-def select_kernel(off_ref, q_ref, k_ref, v_ref, q1_ref, near_ref, kv2_ref, f3_ref, f4_ref):
+def select_kernel(
+    off_hbm, q_hbm, k_hbm, v_hbm, q1_ref, near_ref, kv2_ref, f3_ref, f4_ref, off_ref, q_ref, k_ref, v_ref, sems
+):
+    pairs = ((off_hbm, off_ref), (q_hbm, q_ref), (k_hbm, k_ref), (v_hbm, v_ref))
+    copies = [pltpu.make_async_copy(src, dst, sems.at[n]) for n, (src, dst) in enumerate(pairs)]
+    for copy in copies:
+        copy.start()
+    for copy in copies:
+        copy.wait()
     row = iota((SEL, TOK), 0)
     tok = iota((SEL, TOK), 1)
     base = jnp.where(row < 64, row * 4, jnp.where(row < 80, (row - 64) * 16, (row - 80) * 64))
@@ -123,37 +132,46 @@
         stat_ref[here, :] = stats
 
 
-def far_kernel(pos_ref, qa_ref, qb_ref, ka_ref, kb_ref, out_ref):
+def far_kernel(pos_ref, qa_ref, qb_ref, ka_ref, kb_ref, kf_ref, out_ref):
     me = pos_ref[0]
+
+    def device_of(block):
+        return me ^ ((block & 1) * 2) ^ (((block >> 1) & 1) * 6) ^ (block >> 2)
+
     col = iota((1, 256), 1) & 127
-    block = col >> 4
-    asker = me ^ ((block & 1) * 2) ^ (((block >> 1) & 1) * 6) ^ (block >> 2)
-    q_row = col & 15
+    asker = device_of(col >> 4)
     row = iota((32, 1), 0)
     owner = me ^ ((row >> 4) * 8)
-    allowed2 = (owner & 15) * 16 + (row & 15) <= (asker & 15) * 16 + q_row
+    allowed2 = (owner & 15) * 16 + (row & 15) <= (asker & 15) * 16 + (col & 15)
+    col = iota((1, 128), 1) & 63
+    asker = device_of(col >> 3)
+    q_row = col & 7
     row = iota((64, 1), 0)
     k_row = row & 7
-    owner = me ^ (((row >> 3) & 1) * 32) ^ (((row >> 4) & 1) * 16) ^ ((row >> 5) * 8)
+    owner = (me - (me & 56)) + (row >> 3) * 8
     far_owner = owner ^ ((k_row & 1) * 192) ^ (((k_row >> 1) & 1) * 64)
-    q_limit = jnp.where(q_row < 4, (asker & 63) * 4 + q_row, -1)
-    third = (owner & 63) * 4 + k_row <= q_limit
+    third = (owner & 63) * 4 + k_row <= jnp.where(q_row < 4, (asker & 63) * 4 + q_row, -1)
     fourth = far_owner <= jnp.where(q_row == 4, asker, -1)
     allowed34 = jnp.where(k_row < 4, third.astype(jnp.int32), fourth.astype(jnp.int32)) > 0
-    stat_row = iota((32, 128), 0)
     results = []
-    for level, first, allowed in ((0, 0, allowed2), (1, WIDTH, allowed34)):
-        low, high = ((32, 48), (0, 32))[level]
-        stats = jnp.zeros((32, 128), F32)
+    for level, rows, allowed in ((0, 16, allowed2), (1, 8, allowed34)):
+        count = 8 * rows
+        stat_row = iota((32, count), 0)
+        stats = jnp.zeros((32, count), F32)
         accs = []
         for pair in range(PAIRS):
             at = lanes_of(pair)
             vat = slice(WIDTH + pair * LANES, WIDTH + (pair + 1) * LANES)
-            qat = slice(first + pair * LANES, first + (pair + 1) * LANES)
-            queries = split_heads(jnp.concatenate([qa_ref[128:192, qat], qb_ref[128:192, qat]], 0))
-            keys = jnp.concatenate([ka_ref[low:high, at], kb_ref[low:high, at]], 0)
-            values = jnp.concatenate([ka_ref[low:high, vat], kb_ref[low:high, vat]], 0)
-            scores = jnp.where(allowed, dot_nt(keys, queries), NEG)
+            if level == 0:
+                queries = jnp.concatenate([qa_ref[128:192, at], qb_ref[128:192, at]], 0)
+                keys = jnp.concatenate([ka_ref[:, at], kb_ref[:, at]], 0)
+                values = jnp.concatenate([ka_ref[:, vat], kb_ref[:, vat]], 0)
+            else:
+                blocks = [ref[128 + 16 * n:136 + 16 * n, vat] for ref in (qa_ref, qb_ref) for n in range(4)]
+                queries = jnp.concatenate(blocks, 0)
+                keys = kf_ref[:, at]
+                values = kf_ref[:, vat]
+            scores = jnp.where(allowed, dot_nt(keys, split_heads(queries)), NEG)
             peak = jnp.max(scores, axis=0, keepdims=True)
             weights = jnp.where(allowed, jnp.exp(scores - peak), 0.0)
             total = jnp.sum(weights, axis=0, keepdims=True)
@@ -162,19 +180,19 @@
             )
             accs.append(join_heads(acc).astype(BF16))
             for side in range(2):
-                here = slice(128 * side, 128 * side + 128)
+                here = slice(count * side, count * side + count)
                 stats = jnp.where(stat_row == 2 * pair + side, peak[:, here], stats)
                 stats = jnp.where(stat_row == STAT + 2 * pair + side, total[:, here], stats)
         high = stats.astype(BF16).astype(F32)
         mid = (stats - high).astype(BF16).astype(F32)
         low = stats - high - mid
-        stats = jnp.concatenate([high, mid, low, jnp.zeros((32, 128), F32)], 0).T.astype(BF16)
+        stats = jnp.concatenate([high, mid, low, jnp.zeros((32, count), F32)], 0).T.astype(BF16)
         results.append((accs, stats))
     for number in range(8):
-        to = (me & 7) ^ ((number & 1) * 2) ^ (((number >> 1) & 1) * 6) ^ (number >> 2)
+        to = device_of(number) & 7
         for level, begin, rows in ((0, 0, 16), (1, 16, 8)):
             accs, stats = results[level]
-            here = slice(number * 16, number * 16 + rows)
+            here = slice(number * rows, number * rows + rows)
             for pair in range(PAIRS):
                 out_ref[to, begin:begin + rows, lanes_of(pair)] = accs[pair][here]
             out_ref[to, begin:begin + rows, WIDTH:WIDTH + LANES] = stats[here]
@@ -326,15 +344,16 @@
         select_kernel,
         [shaped(64, WIDTH, BF16), shaped(80, 2 * WIDTH, BF16), shaped(16, 2 * WIDTH, BF16),
          shaped(4, 2 * WIDTH, BF16), shaped(1, 2 * WIDTH, BF16)],
-        [SMEM] + [VMEM] * 3, 200_000_000, 2_000_000, 12,
-    )(offsets, queries, keys, values)
+        [pl.BlockSpec(memory_space=pltpu.HBM)] * 4, 200_000_000, 2_000_000, 12,
+        [pltpu.SMEM((5, HEADS), jnp.int32)] + [pltpu.VMEM((TOK, WIDTH), BF16)] * 3 + [pltpu.SemaphoreType.DMA((4,))],
+    )(*[pltpu.with_memory_space_constraint(a, pltpu.HBM) for a in (offsets, queries, keys, values)])
     fourth = grown(fourth, 192, count)
     fourth = grown(fourth, 64, count)
     far = jnp.concatenate([third, fourth], 0)
-    far = grown(far, 32, count)
-    far = grown(far, 16, count)
-    far = jnp.concatenate([far, kv2], 0)
-    far_other = traded(far, 8, count)
+    lines = [[first + step for step in range(0, 64, 8)] for first in range(count) if not first & 56]
+    far = jnp.broadcast_to(far[None], (8, 8, 2 * WIDTH))
+    far = lax.all_to_all(far, "ctx", 0, 0, axis_index_groups=lines).reshape(64, 2 * WIDTH)
+    kv2_other = traded(kv2, 8, count)
     near_other = traded(near, 2, count)
     asked = jnp.concatenate([near[64:80], near_other[64:80]], 0)
     asked_other = traded(asked, 6, count)
@@ -344,9 +363,9 @@
         local_kernel, [shaped(TOK, WIDTH, F32), shaped(TOK, LANES, F32)], [VMEM] * 3, 1_000_000_000, 3_000_000, 12,
     )(queries, keys, values)
     (partial,) = call(
-        far_kernel, [jax.ShapeDtypeStruct((8, 24, WIDTH + LANES), BF16)], [SMEM] + [VMEM] * 4,
+        far_kernel, [jax.ShapeDtypeStruct((8, 24, WIDTH + LANES), BF16)], [SMEM] + [VMEM] * 5,
         200_000_000, 600_000, 12,
-    )(me, both, both_other, far, far_other)
+    )(me, both, both_other, kv2, kv2_other, far)
     groups = [list(range(first, first + 8)) for first in range(0, count, 8)]
     back = lax.all_to_all(partial, "ctx", 0, 0, axis_index_groups=groups)
     acc01, stat01 = call(

time: 61.5 us -> 57.6 us (0.937)
  local copies, waits for them, and re-layouts: 4.51 us -> 1.44 us
  starting transfers between devices: 30.4 us -> 29.3 us
    all_to_all x0 -> x1, starting transfers between devices: none -> 7.98 us  [program(): lax.all_to_all(far, 'ctx', 0, 0, axis_index_groups=lines)]
    ppermute x8 -> x6, starting transfers between devices: 21.4 us -> 13.7 us  [traded(): lax.ppermute(value, 'ctx', [(source, source ^ mask) for source in range(c...]
    ppermute x8 -> x6, waiting for transfers between devices: 13.2 us -> 9.06 us  [traded(): lax.ppermute(value, 'ctx', [(source, source ^ mask) for source in range(c...]
    all_to_all x0 -> x1, waiting for transfers between devices: none -> 4.01 us  [program(): lax.all_to_all(far, 'ctx', 0, 0, axis_index_groups=lines)]
    unnamed x18 -> x10, local copies, waits for them, and re-layouts: 4.39 us -> 0.72 us
    all_to_all x1, starting transfers between devices: 9.01 us -> 7.62 us  [program(): back = lax.all_to_all(partial, 'ctx', 0, 0, axis_index_groups=groups)]
    broadcast_in_dim x0 -> x1, local copies, waits for them, and re-layouts: none -> 0.69 us  [program(): far = jnp.broadcast_to(far[None], (8, 8, 2 * WIDTH))]
    pallas_call x1, Pallas kernels: 1.21 us -> 1.88 us  [program(): call(select_kernel, [shaped(64, WIDTH, BF16), shaped(80, 2 * WIDTH, BF16)...]
  transfers between devices with their start and end apart: 9 -> 8, of which waited for: 6 -> 5; matrix products, arithmetic and copies ran while one was open for 0% -> 1% of each run, Pallas kernels for 7% -> 8%
where the time goes in v1:
time: 57.6 us; the launch traced here: 57.3 us
  starting transfers between devices  29.3 us (51%)
  waiting for transfers between devices  15.1 us (26%)
  Pallas kernels  11.3 us (20%)
  local copies, waits for them, and re-layouts  1.44 us (2%)
    ppermute x6, starting transfers between devices, traded(): lax.ppermute(value, 'ctx', [(source, source ^ mask) for source in range(c...  13.7 us
    ppermute x6, waiting for transfers between devices, traded(): lax.ppermute(value, 'ctx', [(source, source ^ mask) for source in range(c...  9.06 us
    all_to_all x1, starting transfers between devices, program(): lax.all_to_all(far, 'ctx', 0, 0, axis_index_groups=lines)  7.98 us
    all_to_all x1, starting transfers between devices, program(): back = lax.all_to_all(partial, 'ctx', 0, 0, axis_index_groups=groups)  7.62 us
    all_to_all x1, waiting for transfers between devices, program(): lax.all_to_all(far, 'ctx', 0, 0, axis_index_groups=lines)  4.01 us
    pallas_call x1, Pallas kernels, program(): call(near_kernel, [shaped(TOK, WIDTH, F32), shaped(TOK, LANES, F32)], [SM...  3.23 us
    pallas_call x1, Pallas kernels, program(): call(far_kernel, [jax.ShapeDtypeStruct((8, 24, WIDTH + LANES), BF16)], [S...  2.75 us
    pallas_call x1, Pallas kernels, program(): call(final_kernel, [shaped(TOK, WIDTH, BF16)], [SMEM, VMEM, VMEM, VMEM],...  2.16 us
  transfers between devices with their start and end apart: 8, of which 5 were waited for; matrix products, arithmetic and copies ran while one was open for 1% of the time, Pallas kernels for 8%

profile of v1, /device:TPU:1, one launch (start us, length us, event | category | flops | bytes accessed | tf_op | source)
XLA Modules:
  0.0 57.3 jit_solution(5610000279038291262)
XLA Ops:
  0.0 1.9 %shard_map.46 = (bf16[64,768]{1,0:T(8,128)(2,1)S(1)}, bf16[80,1536]{1,0:T(8,128)(2,1)S(1)}, bf16[16,1536]{1,0:T(8,128)(2,1)S(1)}, bf16[4,1536]{1,0:T(4,128)(2,1)S(1)}, bf16[1,1536]{1,0:T(2,128)(2,1)S(1)}) custom-call(s32[5,12]{1,0:T(8,128)} %off_ref.3, bf16[256,768]{1,0:T(8,128)(2,1)} %q_ref.1, bf16[256,768]{1,0:T(8,128)(2,1)} %k_ref.1, bf16[256,768]{1,0:T(8,128)(2,1)} %v_ref.1), custom_call_target="tpu_custom_call" | custom-call | flops 200000000 | bytes 2000000 | tf_op jit(solution)/shard_map/pallas_call | solution.py:343
  1.9 2.1 %collective-permute-start = (bf16[80,1536]{1,0:T(8,128)(2,1)S(1)}, bf16[80,1536]{1,0:T(8,128)(2,1)S(1)}, u32[]{:S(2)}, u32[]{:S(2)}) collective-permute-start(bf16[80,1536]{1,0:T(8,128)(2,1)S(1)} %get-tuple-element.15), channel_id=1, source_target_pairs={{0,2},{1,3},{2,0},{3,1},{4,6},{5,7},{6,4},{7,5},{8,10},{9,11},{10,... | collective-permute-start | bytes 737288 | tf_op jit(solution)/shard_map/ppermute | solution.py:333
  4.0 4.4 %collective-permute-done = bf16[80,1536]{1,0:T(8,128)(2,1)S(1)} collective-permute-done((bf16[80,1536]{1,0:T(8,128)(2,1)S(1)}, bf16[80,1536]{1,0:T(8,128)(2,1)S(1)}, u32[]{:S(2)}, u32[]{:S(2)}) %collective-permute-start) | collective-permute-done | bytes 245792 | tf_op jit(solution)/shard_map/ppermute | solution.py:333
  8.5 3.8 %collective-permute-start.1 = (bf16[32,1536]{1,0:T(8,128)(2,1)S(1)}, bf16[32,1536]{1,0:T(8,128)(2,1)S(1)}, u32[]{:S(2)}, u32[]{:S(2)}) collective-permute-start(bf16[32,1536]{1,0:T(8,128)(2,1)S(1)} %pad_maximum_fusion), channel_id=1, source_target_pairs={{0,6},{1,7},{2,4},{3,5},{4,2},{5,3},{6,0},{7,1},{8,14},{9,15},{10,... | collective-permute-start | bytes 294920 | tf_op jit(solution)/shard_map/ppermute | solution.py:333
  12.3 2.7 %collective-permute-start.4 = (bf16[1,1536]{1,0:T(2,128)(2,1)S(1)}, bf16[1,1536]{1,0:T(2,128)(2,1)S(1)}, u32[]{:S(2)}, u32[]{:S(2)}) collective-permute-start(bf16[1,1536]{1,0:T(2,128)(2,1)S(1)} %get-tuple-element.22), channel_id=1, source_target_pairs={{0,192},{1,193},{2,194},{3,195},{4,196},{5,197},{6,198},{7,199},{8... | collective-permute-start | bytes 9224 | tf_op jit(solution)/shard_map/ppermute | solution.py:333
  15.0 0.0 collective-permute-done.1
  15.0 2.4 %collective-permute-start.2 = (bf16[192,1536]{1,0:T(8,128)(2,1)S(1)}, bf16[192,1536]{1,0:T(8,128)(2,1)S(1)}, u32[]{:S(2)}, u32[]{:S(2)}) collective-permute-start(bf16[192,1536]{1,0:T(8,128)(2,1)S(1)} %constant_dynamic-update-slice_fusion.a1_ref.qa_ref), channel_id=1, source_target_pairs={{0,1},{1,0},{2,3},{3,2},{4,5},{5,4},{6,7},{7,6},{8,9},{9,8},{10,11... | collective-permute-start | bytes 1769480 | tf_op jit(solution)/shard_map/ppermute | solution.py:333
  17.5 0.0 collective-permute-done.4
  17.5 1.2 %collective-permute-start.5 = (bf16[2,1536]{1,0:T(2,128)(2,1)S(1)}, bf16[2,1536]{1,0:T(2,128)(2,1)S(1)}, u32[]{:S(2)}, u32[]{:S(2)}) collective-permute-start(bf16[2,1536]{1,0:T(2,128)(2,1)S(1)} %pad_maximum_fusion.2), channel_id=1, source_target_pairs={{0,64},{1,65},{2,66},{3,67},{4,68},{5,69},{6,70},{7,71},{8,72},{9,... | collective-permute-start | bytes 18440 | tf_op jit(solution)/shard_map/ppermute | solution.py:333
  18.7 1.4 %collective-permute-done.5 = bf16[2,1536]{1,0:T(2,128)(2,1)S(1)} collective-permute-done((bf16[2,1536]{1,0:T(2,128)(2,1)S(1)}, bf16[2,1536]{1,0:T(2,128)(2,1)S(1)}, u32[]{:S(2)}, u32[]{:S(2)}) %collective-permute-start.5) | collective-permute-done | bytes 6176 | tf_op jit(solution)/shard_map/ppermute | solution.py:333
  20.1 0.7 %broadcast_in_dim.2 = bf16[8,8,1536]{2,1,0:T(8,128)(2,1)} broadcast(bf16[8,1536]{1,0:T(8,128)(2,1)S(1)} %pad_maximum_fusion.1), dimensions={1,2} | broadcast | bytes 221184 | tf_op jit(solution)/shard_map/broadcast_in_dim | solution.py:354
  20.8 8.0 %all-to-all-start = ((bf16[8,8,1536]{2,1,0:T(8,128)(2,1)}), bf16[8,8,1536]{2,1,0:T(8,128)(2,1)S(1)}, u32[]{:S(2)}, u32[]{:S(2)}) async-start(bf16[8,8,1536]{2,1,0:T(8,128)(2,1)} %broadcast_in_dim.2), calls=%async_computation | async-start | bytes 393216 | tf_op jit(solution)/shard_map/all_to_all | solution.py:355
  28.8 1.5 %collective-permute-start.3 = (bf16[16,1536]{1,0:T(8,128)(2,1)S(1)}, bf16[16,1536]{1,0:T(8,128)(2,1)S(1)}, u32[]{:S(2)}, u32[]{:S(2)}) collective-permute-start(bf16[16,1536]{1,0:T(8,128)(2,1)S(1)} %get-tuple-element.20.ka_ref), channel_id=1, source_target_pairs={{0,8},{1,9},{2,10},{3,11},{4,12},{5,13},{6,14},{7,15},{8,0},{9,1},... | collective-permute-start | bytes 147464 | tf_op jit(solution)/shard_map/ppermute | solution.py:333
  30.2 3.3 %collective-permute-done.3.kb_ref = bf16[16,1536]{1,0:T(8,128)(2,1)S(1)} collective-permute-done((bf16[16,1536]{1,0:T(8,128)(2,1)S(1)}, bf16[16,1536]{1,0:T(8,128)(2,1)S(1)}, u32[]{:S(2)}, u32[]{:S(2)}) %collective-permute-start.3) | collective-permute-done | bytes 49184 | tf_op jit(solution)/shard_map/ppermute | solution.py:333
  33.5 4.0 %all-to-all-done = bf16[8,8,1536]{2,1,0:T(8,128)(2,1)S(1)} async-done(((bf16[8,8,1536]{2,1,0:T(8,128)(2,1)}), bf16[8,8,1536]{2,1,0:T(8,128)(2,1)S(1)}, u32[]{:S(2)}, u32[]{:S(2)}) %all-to-all-start) | async-done | bytes 196640 | tf_op jit(solution)/shard_map/all_to_all | solution.py:355
  37.5 0.0 collective-permute-done.2.b1_ref.qb_ref
  37.5 0.0 copy-start.1
  37.5 0.0 copy-start.2
  37.5 2.7 %shard_map.49 = bf16[8,24,896]{2,1,0:T(8,128)(2,1)} custom-call(s32[1]{0:T(128)} %bitcast.pos_ref, bf16[192,1536]{1,0:T(8,128)(2,1)S(1)} %constant_dynamic-update-slice_fusion.a1_ref.qa_ref, bf16[192,1536]{1,0:T(8,128)(2,1)S(1)} %collective-permute-done.2.b1_ref.qb_ref, bf16[16,1536]{1,0:T(8,128)(2,1)S(1)} %get-tuple-element.20.ka_ref, ...), custom_call_target="tpu_custom_call" | custom-call | flops 200000000 | bytes 600000 | tf_op jit(solution)/shard_map/pallas_call | solution.py:365
  40.2 0.0 copy-start
  40.2 7.6 %all-to-all-start.1 = ((bf16[8,24,896]{2,1,0:T(8,128)(2,1)}), bf16[8,24,896]{2,1,0:T(8,128)(2,1)S(1)}, u32[]{:S(2)}, u32[]{:S(2)}) async-start(bf16[8,24,896]{2,1,0:T(8,128)(2,1)} %shard_map.49), calls=%async_computation.1 | async-start | bytes 688128 | tf_op jit(solution)/shard_map/all_to_all | solution.py:370
  47.9 0.0 copy-done.1
  47.9 0.0 copy-done.2
  47.9 0.0 copy-done
  47.9 1.3 %shard_map.47 = (f32[256,768]{1,0:T(8,128)S(1)}, f32[256,128]{1,0:T(8,128)S(1)}) custom-call(bf16[256,768]{1,0:T(8,128)(2,1)S(1)} %copy-done, bf16[256,768]{1,0:T(8,128)(2,1)S(1)} %copy-done.1, bf16[256,768]{1,0:T(8,128)(2,1)S(1)} %copy-done.2), custom_call_target="tpu_custom_call" | custom-call | flops 1000000000 | bytes 3000000 | tf_op jit(solution)/shard_map/pallas_call | solution.py:362
  49.2 0.0 copy-start.3
  49.2 0.7 %copy-done.3 = s32[5,12]{1,0:T(8,128)S(1)} copy-done((s32[5,12]{1,0:T(8,128)S(1)}, s32[5,12]{1,0:T(8,128)}, u32[]{:S(2)}) %copy-start.3) | copy-done | bytes 264
  49.9 3.2 %shard_map.48 = (f32[256,768]{1,0:T(8,128)S(1)}, f32[256,128]{1,0:T(8,128)S(1)}) custom-call(s32[5,12]{1,0:T(8,128)S(1)} %copy-done.3, s32[1]{0:T(128)} %bitcast.pos_ref, bf16[64,768]{1,0:T(8,128)(2,1)S(1)} %get-tuple-element.14.q1_ref, bf16[192,1536]{1,0:T(8,128)(2,1)S(1)} %constant_dynamic-update-slice_fusion.a1_ref.qa_ref, ...), custom_call_target="tpu_custom_call" | custom-call | flops 600000000 | bytes 2000000 | tf_op jit(solution)/shard_map/pallas_call | solution.py:371
  53.1 2.0 %all-to-all-done.1.ret_ref = bf16[8,24,896]{2,1,0:T(8,128)(2,1)S(1)} async-done(((bf16[8,24,896]{2,1,0:T(8,128)(2,1)}), bf16[8,24,896]{2,1,0:T(8,128)(2,1)S(1)}, u32[]{:S(2)}, u32[]{:S(2)}) %all-to-all-start.1) | async-done | bytes 344096 | tf_op jit(solution)/shard_map/all_to_all | solution.py:370
  55.1 2.2 %shard_map.50 = bf16[256,768]{1,0:T(8,128)(2,1)} custom-call(s32[5,12]{1,0:T(8,128)S(1)} %copy-done.3, f32[256,768]{1,0:T(8,128)S(1)} %get-tuple-element.18.acc_ref, f32[256,128]{1,0:T(8,128)S(1)} %get-tuple-element.19.stat_ref, bf16[8,24,896]{2,1,0:T(8,128)(2,1)S(1)} %all-to-all-done.1.ret_ref), custom_call_target="tpu_custom_call" | custom-call | flops 1000000000 | bytes 3000000 | tf_op jit(solution)/shard_map/pallas_call | solution.py:375
  (8 shorter events, 0.1 us)
Async XLA Ops:
  1.9 6.5 %collective-permute-start = (bf16[80,1536]{1,0:T(8,128)(2,1)S(1)}, bf16[80,1536]{1,0:T(8,128)(2,1)S(1)}, u32[]{:S(2)}, u32[]{:S(2)}) collective-permute-start(bf16[80,1536]{1,0:T(8,128)(2,1)S(1)} %get-tuple-element.15), channel_id=1, source_target_pairs={{0,2},{1,3},{2,0},{3,1},{4,6},{5,7},{6,4},{7,5},{8,10},{9,11},{10,... | collective-permute-start | bytes 737288 | tf_op jit(solution)/shard_map/ppermute | solution.py:333
  8.5 6.5 %collective-permute-start.1 = (bf16[32,1536]{1,0:T(8,128)(2,1)S(1)}, bf16[32,1536]{1,0:T(8,128)(2,1)S(1)}, u32[]{:S(2)}, u32[]{:S(2)}) collective-permute-start(bf16[32,1536]{1,0:T(8,128)(2,1)S(1)} %pad_maximum_fusion), channel_id=1, source_target_pairs={{0,6},{1,7},{2,4},{3,5},{4,2},{5,3},{6,0},{7,1},{8,14},{9,15},{10,... | collective-permute-start | bytes 294920 | tf_op jit(solution)/shard_map/ppermute | solution.py:333
  12.3 5.2 %collective-permute-start.4 = (bf16[1,1536]{1,0:T(2,128)(2,1)S(1)}, bf16[1,1536]{1,0:T(2,128)(2,1)S(1)}, u32[]{:S(2)}, u32[]{:S(2)}) collective-permute-start(bf16[1,1536]{1,0:T(2,128)(2,1)S(1)} %get-tuple-element.22), channel_id=1, source_target_pairs={{0,192},{1,193},{2,194},{3,195},{4,196},{5,197},{6,198},{7,199},{8... | collective-permute-start | bytes 9224 | tf_op jit(solution)/shard_map/ppermute | solution.py:333
  15.0 22.5 %collective-permute-start.2 = (bf16[192,1536]{1,0:T(8,128)(2,1)S(1)}, bf16[192,1536]{1,0:T(8,128)(2,1)S(1)}, u32[]{:S(2)}, u32[]{:S(2)}) collective-permute-start(bf16[192,1536]{1,0:T(8,128)(2,1)S(1)} %constant_dynamic-update-slice_fusion.a1_ref.qa_ref), channel_id=1, source_target_pairs={{0,1},{1,0},{2,3},{3,2},{4,5},{5,4},{6,7},{7,6},{8,9},{9,8},{10,11... | collective-permute-start | bytes 1769480 | tf_op jit(solution)/shard_map/ppermute | solution.py:333
  17.5 2.6 %collective-permute-start.5 = (bf16[2,1536]{1,0:T(2,128)(2,1)S(1)}, bf16[2,1536]{1,0:T(2,128)(2,1)S(1)}, u32[]{:S(2)}, u32[]{:S(2)}) collective-permute-start(bf16[2,1536]{1,0:T(2,128)(2,1)S(1)} %pad_maximum_fusion.2), channel_id=1, source_target_pairs={{0,64},{1,65},{2,66},{3,67},{4,68},{5,69},{6,70},{7,71},{8,72},{9,... | collective-permute-start | bytes 18440 | tf_op jit(solution)/shard_map/ppermute | solution.py:333
  20.8 16.7 %all-to-all-start = ((bf16[8,8,1536]{2,1,0:T(8,128)(2,1)}), bf16[8,8,1536]{2,1,0:T(8,128)(2,1)S(1)}, u32[]{:S(2)}, u32[]{:S(2)}) async-start(bf16[8,8,1536]{2,1,0:T(8,128)(2,1)} %broadcast_in_dim.2), calls=%async_computation | async-start | bytes 393216 | tf_op jit(solution)/shard_map/all_to_all | solution.py:355
  28.8 4.7 %collective-permute-start.3 = (bf16[16,1536]{1,0:T(8,128)(2,1)S(1)}, bf16[16,1536]{1,0:T(8,128)(2,1)S(1)}, u32[]{:S(2)}, u32[]{:S(2)}) collective-permute-start(bf16[16,1536]{1,0:T(8,128)(2,1)S(1)} %get-tuple-element.20.ka_ref), channel_id=1, source_target_pairs={{0,8},{1,9},{2,10},{3,11},{4,12},{5,13},{6,14},{7,15},{8,0},{9,1},... | collective-permute-start | bytes 147464 | tf_op jit(solution)/shard_map/ppermute | solution.py:333
  37.5 10.4 %copy-start.1 = (bf16[256,768]{1,0:T(8,128)(2,1)S(1)}, bf16[256,768]{1,0:T(8,128)(2,1)}, u32[]{:S(2)}) copy-start(bf16[256,768]{1,0:T(8,128)(2,1)} %k_ref.1) | copy-start | bytes 1179652
  37.5 10.4 %copy-start.2 = (bf16[256,768]{1,0:T(8,128)(2,1)S(1)}, bf16[256,768]{1,0:T(8,128)(2,1)}, u32[]{:S(2)}) copy-start(bf16[256,768]{1,0:T(8,128)(2,1)} %v_ref.1) | copy-start | bytes 1179652
  40.2 7.6 %copy-start = (bf16[256,768]{1,0:T(8,128)(2,1)S(1)}, bf16[256,768]{1,0:T(8,128)(2,1)}, u32[]{:S(2)}) copy-start(bf16[256,768]{1,0:T(8,128)(2,1)} %q_ref.1) | copy-start | bytes 1179652
  40.2 14.9 %all-to-all-start.1 = ((bf16[8,24,896]{2,1,0:T(8,128)(2,1)}), bf16[8,24,896]{2,1,0:T(8,128)(2,1)S(1)}, u32[]{:S(2)}, u32[]{:S(2)}) async-start(bf16[8,24,896]{2,1,0:T(8,128)(2,1)} %shard_map.49), calls=%async_computation.1 | async-start | bytes 688128 | tf_op jit(solution)/shard_map/all_to_all | solution.py:370
  49.2 0.7 %copy-start.3 = (s32[5,12]{1,0:T(8,128)S(1)}, s32[5,12]{1,0:T(8,128)}, u32[]{:S(2)}) copy-start(s32[5,12]{1,0:T(8,128)} %off_ref.3) | copy-start | bytes 724

commit v2 on v1

v2 whole, which is shorter than its diff:
```python
import functools

import jax
import jax.numpy as jnp
from jax import lax
from jax.experimental import pallas as pl
from jax.experimental.pallas import tpu as pltpu
from jax.sharding import PartitionSpec as P

HEADS = 12
PAIRS = 6
LANES = 128
HALF = 64
TOK = 256
WIDTH = 768
NEG = -1e30
SCALE = 0.125
F32 = jnp.float32
BF16 = jnp.bfloat16
SEL = 96
STAT = 16
VMEM = pl.BlockSpec(memory_space=pltpu.VMEM)
SMEM = pl.BlockSpec(memory_space=pltpu.SMEM)


def iota(shape, dim):
    return lax.broadcasted_iota(jnp.int32, shape, dim)


def dot_nt(a, b):
    return lax.dot_general(a, b, (((1,), (1,)), ((), ())), preferred_element_type=F32)


def dot_nn(a, b):
    return jnp.dot(a, b, preferred_element_type=F32)


def lanes_of(pair):
    return slice(pair * LANES, (pair + 1) * LANES)


def split_heads(rows):
    low = iota(rows.shape, 1) < HALF
    zero = jnp.zeros_like(rows)
    return jnp.concatenate([jnp.where(low, rows, zero), jnp.where(low, zero, rows)], 0)


def join_heads(stacked):
    n = stacked.shape[0] // 2
    low = iota((n, LANES), 1) < HALF
    return jnp.where(low, stacked[:n], stacked[n:])


def put_stats(stats, pair, peak, total):
    n = stats.shape[0]
    lane = iota(stats.shape, 1)
    for side in range(2):
        head = 2 * pair + side
        stats = jnp.where(lane == head, peak[side * n:(side + 1) * n], stats)
        stats = jnp.where(lane == STAT + head, total[side * n:(side + 1) * n], stats)
    return stats


def call(body, outs, in_specs, flops, nbytes, grant, scratch=()):
    return pl.pallas_call(
        body,
        scratch_shapes=scratch,
        compiler_params=pltpu.CompilerParams(vmem_limit_bytes=grant << 20),
        out_shape=outs,
        in_specs=in_specs,
        out_specs=[VMEM] * len(outs),
        cost_estimate=pl.CostEstimate(flops=flops, bytes_accessed=nbytes, transcendentals=0),
    )


def select_kernel(
    off_hbm, q_hbm, k_hbm, v_hbm, q_ref, k_ref, v_ref, q1_ref, q2_ref, kv1_ref, early_ref, f3_ref, f4_ref, off_ref, sems
):
    pairs = ((off_hbm, off_ref), (q_hbm, q_ref), (k_hbm, k_ref), (v_hbm, v_ref))
    copies = [pltpu.make_async_copy(src, dst, sems.at[n]) for n, (src, dst) in enumerate(pairs)]
    for copy in copies:
        copy.start()
    for copy in copies:
        copy.wait()
    row = iota((SEL, TOK), 0)
    tok = iota((SEL, TOK), 1)
    base = jnp.where(row < 64, row * 4, jnp.where(row < 80, (row - 64) * 16, (row - 80) * 64))
    base = jnp.where(row < 84, base, 0)
    early_ref[16:24, WIDTH:2 * WIDTH] = jnp.zeros((8, WIDTH), BF16)
    for pair in range(PAIRS):
        picks = []
        for side in range(2):
            head = 2 * pair + side
            off = jnp.where(
                row < 64,
                off_ref[1, head],
                jnp.where(row < 80, off_ref[2, head], jnp.where(row < 84, off_ref[3, head], off_ref[4, head])),
            )
            hit = (tok == base + off) & (row < 85)
            picks.append(jnp.where(hit, 1.0, 0.0).astype(BF16))
        pick = jnp.concatenate(picks, 0)
        at = lanes_of(pair)
        after = slice(WIDTH + pair * LANES, WIDTH + (pair + 1) * LANES)
        rows = join_heads(dot_nn(pick, q_ref[:, at]) * SCALE).astype(BF16)
        q1_ref[:, at] = rows[0:64]
        q2_ref[:, at] = rows[64:80]
        early_ref[16:24, at] = rows[80:88]
        for ref, here in ((k_ref, at), (v_ref, after)):
            rows = join_heads(dot_nn(pick, ref[:, at])).astype(BF16)
            kv1_ref[:, here] = rows[0:64]
            early_ref[0:16, here] = rows[64:80]
            f3_ref[:, here] = rows[80:84]
            f4_ref[:, here] = rows[84:85]


def local_kernel(q_ref, k_ref, v_ref, acc_ref):
    half = TOK // 2
    for part in range(2):
        keys = (part + 1) * half
        here = slice(part * half, keys)
        query = iota((2 * half, keys), 0) % half + part * half
        allowed = iota((2 * half, keys), 1) <= query
        stats = jnp.zeros((half, LANES), F32)
        for pair in range(PAIRS):
            at = lanes_of(pair)
            queries = split_heads(q_ref[here, at] * jnp.asarray(SCALE, BF16))
            scores = jnp.where(allowed, dot_nt(queries, k_ref[0:keys, at]), NEG)
            peak = jnp.max(scores, axis=1, keepdims=True)
            weights = jnp.exp(scores - peak)
            total = jnp.sum(weights, axis=1, keepdims=True)
            acc_ref[here, at] = join_heads(dot_nn(weights.astype(BF16), v_ref[0:keys, at]))
            stats = put_stats(stats, pair, peak, total)
        acc_ref[here, WIDTH:WIDTH + LANES] = stats


def far_kernel(pos_ref, qa_ref, qb_ref, kf_ref, out_ref):
    me = pos_ref[0]

    def device_of(block):
        return me ^ ((block & 1) * 2) ^ (((block >> 1) & 1) * 6) ^ (block >> 2)

    col = iota((1, 128), 1) & 63
    asker = device_of(col >> 3)
    q_row = col & 7
    row = iota((64, 1), 0)
    k_row = row & 7
    owner = (me - (me & 56)) + (row >> 3) * 8
    far_owner = owner ^ ((k_row & 1) * 192) ^ (((k_row >> 1) & 1) * 64)
    third = (owner & 63) * 4 + k_row <= jnp.where(q_row < 4, (asker & 63) * 4 + q_row, -1)
    fourth = far_owner <= jnp.where(q_row == 4, asker, -1)
    allowed = jnp.where(k_row < 4, third.astype(jnp.int32), fourth.astype(jnp.int32)) > 0
    stat_row = iota((32, 64), 0)
    stats = jnp.zeros((32, 64), F32)
    accs = []
    for pair in range(PAIRS):
        at = lanes_of(pair)
        vat = slice(WIDTH + pair * LANES, WIDTH + (pair + 1) * LANES)
        queries = split_heads(jnp.concatenate([qa_ref[:, at], qb_ref[:, at]], 0))
        scores = jnp.where(allowed, dot_nt(kf_ref[:, at], queries), NEG)
        peak = jnp.max(scores, axis=0, keepdims=True)
        weights = jnp.where(allowed, jnp.exp(scores - peak), 0.0)
        total = jnp.sum(weights, axis=0, keepdims=True)
        acc = lax.dot_general(
            weights.astype(BF16), kf_ref[:, vat], (((0,), (0,)), ((), ())), preferred_element_type=F32
        )
        accs.append(join_heads(acc).astype(BF16))
        for side in range(2):
            here = slice(64 * side, 64 * side + 64)
            stats = jnp.where(stat_row == 2 * pair + side, peak[:, here], stats)
            stats = jnp.where(stat_row == STAT + 2 * pair + side, total[:, here], stats)
    high = stats.astype(BF16).astype(F32)
    mid = (stats - high).astype(BF16).astype(F32)
    low = stats - high - mid
    stats = jnp.concatenate([high, mid, low, jnp.zeros((32, 64), F32)], 0).T.astype(BF16)
    for number in range(8):
        to = device_of(number) & 7
        here = slice(number * 8, number * 8 + 8)
        for pair in range(PAIRS):
            out_ref[to, :, lanes_of(pair)] = accs[pair][here]
        out_ref[to, :, WIDTH:WIDTH + LANES] = stats[here]


def head_row(off_ref, level, shape, per_lane):
    lane = iota(shape, 1)
    lane = lane if per_lane else lane // HALF
    off = jnp.zeros(shape, jnp.int32)
    for head in range(HEADS):
        off = jnp.where(lane == head, off_ref[level, head], off)
    return off


def gathered(q_ref, parts, rows, allowed):
    stats = jnp.zeros((rows, LANES), F32)
    accs = []
    for pair in range(PAIRS):
        at = lanes_of(pair)
        vat = slice(WIDTH + pair * LANES, WIDTH + (pair + 1) * LANES)
        queries = split_heads(q_ref[:, at])
        scores = jnp.concatenate([dot_nt(queries, ref[:, at]) for ref in parts], 1)
        scores = jnp.where(allowed, scores, NEG)
        peak = jnp.max(scores, axis=1, keepdims=True)
        weights = jnp.exp(scores - peak)
        total = jnp.sum(weights, axis=1, keepdims=True)
        weights = weights.astype(BF16)
        acc = dot_nn(weights[:, 0:128], parts[0][:, vat]) + dot_nn(weights[:, 128:256], parts[1][:, vat])
        accs.append(join_heads(acc))
        stats = put_stats(stats, pair, peak, total)
    return accs, stats


def absorb(off_ref, level, accs, stats, acc_ref, out_ref):
    group = 4**level
    rows = TOK // group
    lane = iota((TOK, LANES), 1)
    tok = iota((TOK, LANES), 0)
    expand = jnp.where((iota((TOK, rows), 0) >> (2 * level)) == iota((TOK, rows), 1), 1.0, 0.0)
    spread = jnp.dot(expand, stats, precision=lax.Precision.HIGHEST, preferred_element_type=F32)
    kept = ((tok & (group - 1)) == head_row(off_ref, level, (1, LANES), True)) & (lane < HEADS)
    stat = acc_ref[:, WIDTH:WIDTH + LANES]
    peak0 = jnp.where(lane < HEADS, stat, 0.0)
    peak1 = jnp.where(kept, spread, NEG)
    best = jnp.maximum(peak0, peak1)
    share0 = jnp.where(lane < HEADS, jnp.exp(peak0 - best), 0.0)
    share1 = jnp.exp(peak1 - best)
    total = share0 * pltpu.roll(stat, LANES - STAT, 1) + share1 * pltpu.roll(spread, LANES - STAT, 1)
    out_ref[:, WIDTH:WIDTH + LANES] = jnp.where(
        lane < HEADS, best, pltpu.roll(jnp.where(lane < HEADS, total, 0.0), STAT, 1)
    )
    row_share = lax.dot_general(
        expand, share1, (((0,), (0,)), ((), ())), precision=lax.Precision.HIGHEST, preferred_element_type=F32
    )
    scale0 = over_lanes(share0)
    scale1 = over_lanes(row_share)
    twice = jnp.concatenate([expand.astype(BF16)] * 2, 1)
    for pair in range(PAIRS):
        at = lanes_of(pair)
        high, low = split2(accs[pair] * scale1[:, at])
        added = dot_nn(twice, jnp.concatenate([high, low], 0))
        side = iota((1, LANES), 1) >> 6
        off = jnp.where(side == 0, off_ref[level, 2 * pair], off_ref[level, 2 * pair + 1])
        added = jnp.where((iota((TOK, LANES), 0) & (group - 1)) == off, added, 0.0)
        out_ref[:, at] = scale0[:, at] * acc_ref[:, at] + added


def first_kernel(off_ref, pos_ref, q1_ref, a_ref, b_ref, acc_ref, out_ref):
    me = pos_ref[0]
    col = iota((1, TOK), 1)
    device = me ^ (((col >> 6) & 1) * 2) ^ (col >> 7)
    k_pos = (device & 3) * 64 + (col & 63)
    q_pos = (me & 3) * 64 + (iota((128, 1), 0) & 63)
    accs, stats = gathered(q1_ref, (a_ref, b_ref), 64, k_pos <= q_pos)
    absorb(off_ref, 1, accs, stats, acc_ref, out_ref)


def second_kernel(off_ref, pos_ref, q2_ref, a_ref, b_ref, acc_ref, out_ref):
    me = pos_ref[0]
    col = iota((1, TOK), 1)
    block = (col >> 4) & 3
    device = me ^ ((block & 1) * 2) ^ ((block >> 1) * 6) ^ (((col >> 6) & 1) * 8) ^ (col >> 7)
    k_pos = (device & 15) * 16 + (col & 15)
    q_pos = (me & 15) * 16 + (iota((32, 1), 0) & 15)
    accs, stats = gathered(q2_ref, (a_ref, b_ref), 16, k_pos <= q_pos)
    absorb(off_ref, 2, accs, stats, acc_ref, out_ref)


def split2(value):
    high = value.astype(BF16)
    return high, (value - high.astype(F32)).astype(BF16)


def over_lanes(coeff):
    high, low = split2(coeff)
    lane = iota((2 * LANES, WIDTH), 1) // HALF
    spread = jnp.where((iota((2 * LANES, WIDTH), 0) & (LANES - 1)) == lane, 1.0, 0.0).astype(BF16)
    return dot_nn(jnp.concatenate([high, low], 1), spread)


def final_kernel(off_ref, acc_ref, ret_ref, out_ref):
    lane = iota((8, LANES), 1)
    parts = []
    for number in range(8):
        stats = ret_ref[number, :, WIDTH:WIDTH + LANES].astype(F32)
        parts.append(stats + pltpu.roll(stats, 96, 1) + pltpu.roll(stats, 64, 1))
    peaks = [jnp.where(lane < HEADS, part, NEG) for part in parts]
    peak = functools.reduce(jnp.maximum, peaks)
    factors = [jnp.where(lane < HEADS, jnp.exp(part - peak), 0.0) for part in peaks]
    total = sum(factor * pltpu.roll(part, LANES - STAT, 1) for factor, part in zip(factors, parts))
    spread = over_lanes(jnp.concatenate(factors, 0))
    rows = sum(
        spread[8 * number:8 * number + 8] * ret_ref[number, :, 0:WIDTH].astype(F32) for number in range(8)
    )

    def expanded(value, level):
        if level == 3:
            return jnp.concatenate([jnp.broadcast_to(value[r:r + 1], (64, LANES)) for r in range(4)], 0)
        return jnp.broadcast_to(value[4:5], (TOK, LANES))

    lane = iota((TOK, LANES), 1)
    tok = iota((TOK, LANES), 0)
    stat = acc_ref[:, WIDTH:WIDTH + LANES]
    level_peaks = [jnp.where(lane < HEADS, stat, 0.0)]
    level_totals = [pltpu.roll(stat, LANES - STAT, 1)]
    for level in (3, 4):
        kept = ((tok & (4**level - 1)) == head_row(off_ref, level, (1, LANES), True)) & (lane < HEADS)
        level_peaks.append(jnp.where(kept, expanded(peak, level), NEG))
        level_totals.append(expanded(total, level))
    best = functools.reduce(jnp.maximum, level_peaks)
    shares = [jnp.where(lane < HEADS, jnp.exp(value - best), 0.0) for value in level_peaks]
    denom = sum(share * value for share, value in zip(shares, level_totals))
    inverse = 1.0 / jnp.where(lane < HEADS, denom, 1.0)
    shares = [share * inverse for share in shares]
    row_shares = [jnp.sum(shares[1][64 * r:64 * r + 64], axis=0, keepdims=True) for r in range(4)]
    row_shares += [jnp.sum(shares[2], axis=0, keepdims=True), jnp.zeros((3, LANES), F32)]
    rows = rows * over_lanes(jnp.concatenate(row_shares, 0))
    scale = over_lanes(shares[0])
    hits = [
        iota((4**level, WIDTH), 0) == head_row(off_ref, level, (1, WIDTH), False) for level in (3, 4)
    ]
    for r in range(16):
        here = slice(16 * r, 16 * r + 16)
        inner = slice(16 * (r % 4), 16 * (r % 4) + 16)
        merged = scale[here] * acc_ref[here, 0:WIDTH]
        merged = merged + jnp.where(hits[0][inner], rows[r // 4:r // 4 + 1], 0.0)
        merged = merged + jnp.where(hits[1][here], rows[4:5], 0.0)
        out_ref[here, :] = merged.astype(BF16)


def shaped(rows, width, dtype):
    return jax.ShapeDtypeStruct((rows, width), dtype)


def traded(value, mask, count):
    return lax.ppermute(value, "ctx", [(source, source ^ mask) for source in range(count)])


def grown(value, mask, count):
    return jnp.concatenate([value, traded(value, mask, count)], 0)


def program(queries, keys, values, offsets):
    count = lax.axis_size("ctx")
    me = lax.axis_index("ctx").astype(jnp.int32).reshape(1)
    wide = 2 * WIDTH
    inputs = [pltpu.with_memory_space_constraint(a, pltpu.HBM) for a in (offsets, queries, keys, values)]
    q, k, v, q1, q2, kv1, early, third, fourth = call(
        select_kernel,
        [shaped(TOK, WIDTH, BF16)] * 3
        + [shaped(64, WIDTH, BF16), shaped(16, WIDTH, BF16), shaped(64, wide, BF16), shaped(24, wide, BF16),
           shaped(4, wide, BF16), shaped(1, wide, BF16)],
        [pl.BlockSpec(memory_space=pltpu.HBM)] * 4, 200_000_000, 2_000_000, 12,
        [pltpu.SMEM((5, HEADS), jnp.int32), pltpu.SemaphoreType.DMA((4,))],
    )(*inputs)
    fourth = grown(fourth, 192, count)
    fourth = grown(fourth, 64, count)
    far = jnp.broadcast_to(jnp.concatenate([third, fourth], 0)[None], (8, 8, wide))
    lines = [[first + step for step in range(0, 64, 8)] for first in range(count) if not first & 56]
    far = lax.all_to_all(far, "ctx", 0, 0, axis_index_groups=lines).reshape(64, wide)
    early = grown(early, 2, count)
    early = grown(early, 6, count).reshape(4, 24, wide)
    asked = early[:, 16:24, 0:WIDTH].reshape(32, WIDTH)
    asked_other = traded(asked, 1, count)
    kv1 = grown(kv1, 2, count)
    kv1_other = traded(kv1, 1, count)
    kv2 = grown(early[:, 0:16].reshape(64, wide), 8, count)
    kv2_other = traded(kv2, 1, count)
    total = shaped(TOK, WIDTH + LANES, F32)
    (acc,) = call(local_kernel, [total], [VMEM] * 3, 1_000_000_000, 3_000_000, 12)(q, k, v)
    (acc,) = call(first_kernel, [total], [SMEM, SMEM] + [VMEM] * 4, 600_000_000, 2_000_000, 16)(
        offsets, me, q1, kv1, kv1_other, acc
    )
    (partial,) = call(
        far_kernel, [jax.ShapeDtypeStruct((8, 8, WIDTH + LANES), BF16)], [SMEM] + [VMEM] * 3,
        200_000_000, 600_000, 12,
    )(me, asked, asked_other, far)
    groups = [list(range(first, first + 8)) for first in range(0, count, 8)]
    back = lax.all_to_all(partial, "ctx", 0, 0, axis_index_groups=groups)
    (acc,) = call(second_kernel, [total], [SMEM, SMEM] + [VMEM] * 4, 600_000_000, 2_000_000, 16)(
        offsets, me, q2, kv2, kv2_other, acc
    )
    (merged,) = call(
        final_kernel, [shaped(TOK, WIDTH, BF16)], [SMEM, VMEM, VMEM], 1_000_000_000, 3_000_000, 16
    )(offsets, acc, back)
    return merged


def solution(mesh):
    in_specs = (P("ctx", None), P("ctx", None), P("ctx", None), P())
    return jax.shard_map(program, mesh=mesh, in_specs=in_specs, out_specs=P("ctx", None), check_vma=False)
```

time: 57.6 us -> 48.7 us (0.85)
  waiting for transfers between devices: 15.1 us -> 3.49 us
  Pallas kernels: 11.3 us -> 14.1 us
  local copies, waits for them, and re-layouts: 1.44 us -> 0.76 us
    ppermute x6 -> x9, waiting for transfers between devices: 9.06 us -> 3.48 us  [traded(): lax.ppermute(value, 'ctx', [(source, source ^ mask) for source in range(c...]
    all_to_all x1, waiting for transfers between devices: 4.01 us -> 0.01 us  [program(): lax.all_to_all(far, 'ctx', 0, 0, axis_index_groups=lines).reshape(64, wide)]
    ppermute x6 -> x9, starting transfers between devices: 13.7 us -> 17.7 us  [traded(): lax.ppermute(value, 'ctx', [(source, source ^ mask) for source in range(c...]
    all_to_all x1, starting transfers between devices: 7.62 us -> 3.8 us  [program(): back = lax.all_to_all(partial, 'ctx', 0, 0, axis_index_groups=groups)]
    pallas_call x5 -> x6, Pallas kernels: 11.3 us -> 14.1 us  [the longest x1 3.24 us: program(): call(first_kernel, [total], [SMEM, SMEM] + [VMEM] * 4, 600000000, 2000000...]
    all_to_all x1, waiting for transfers between devices: 1.98 us -> 0.01 us  [program(): back = lax.all_to_all(partial, 'ctx', 0, 0, axis_index_groups=groups)]
    unnamed x10 -> x11, local copies, waits for them, and re-layouts: 0.72 us -> 0.04 us
  transfers between devices with their start and end apart: 8 -> 11, of which waited for: 5 -> 2; matrix products, arithmetic and copies ran while one was open for 1% -> 2% of each run, Pallas kernels for 8% -> 21%
where the time goes in v2:
time: 48.7 us; the launch traced here: 48.4 us
  starting transfers between devices  29.7 us (61%)
  Pallas kernels  14.1 us (29%)
  waiting for transfers between devices  3.49 us (7%)
  local copies, waits for them, and re-layouts  0.76 us (2%)
    ppermute x9, starting transfers between devices, traded(): lax.ppermute(value, 'ctx', [(source, source ^ mask) for source in range(c...  17.7 us
    all_to_all x1, starting transfers between devices, program(): lax.all_to_all(far, 'ctx', 0, 0, axis_index_groups=lines).reshape(64, wide)  8.19 us
    all_to_all x1, starting transfers between devices, program(): back = lax.all_to_all(partial, 'ctx', 0, 0, axis_index_groups=groups)  3.8 us
    ppermute x9, waiting for transfers between devices, traded(): lax.ppermute(value, 'ctx', [(source, source ^ mask) for source in range(c...  3.48 us
    pallas_call x1, Pallas kernels, program(): call(first_kernel, [total], [SMEM, SMEM] + [VMEM] * 4, 600000000, 2000000...  3.24 us
    pallas_call x1, Pallas kernels, program(): call(second_kernel, [total], [SMEM, SMEM] + [VMEM] * 4, 600000000, 200000...  3.18 us
    pallas_call x1, Pallas kernels, program(): call(far_kernel, [jax.ShapeDtypeStruct((8, 8, WIDTH + LANES), BF16)], [SM...  2.44 us
    pallas_call x1, Pallas kernels, program(): call(final_kernel, [shaped(TOK, WIDTH, BF16)], [SMEM, VMEM, VMEM], 100000...  2.03 us
  transfers between devices with their start and end apart: 11, of which 2 were waited for; matrix products, arithmetic and copies ran while one was open for 2% of the time, Pallas kernels for 21%

profile of v2, /device:TPU:1, one launch (start us, length us, event | category | flops | bytes accessed | tf_op | source)
XLA Modules:
  0.0 48.4 jit_solution(2068000466266576513)
XLA Ops:
  0.0 1.9 %shard_map.46 = (bf16[256,768]{1,0:T(8,128)(2,1)S(1)}, bf16[256,768]{1,0:T(8,128)(2,1)S(1)}, bf16[256,768]{1,0:T(8,128)(2,1)S(1)}, bf16[64,768]{1,0:T(8,128)(2,1...) custom-call(s32[5,12]{1,0:T(8,128)} %off_ref.5, ...), custom_call_target="tpu_custom_call" | custom-call | flops 200000000 | bytes 2000000 | tf_op jit(solution)/shard_map/pallas_call | solution.py:345
  1.9 0.0 copy-start.1
  1.9 3.6 %collective-permute-start.7 = (bf16[1,1536]{1,0:T(2,128)(2,1)S(1)}, bf16[1,1536]{1,0:T(2,128)(2,1)S(1)}, u32[]{:S(2)}, u32[]{:S(2)}) collective-permute-start(bf16[1,1536]{1,0:T(2,128)(2,1)S(1)} %get-tuple-element.22), channel_id=1, source_target_pairs={{0,192},{1,193},{2,194},{3,195},{4,196},{5,197},{6,198},{7,199},{8... | collective-permute-start | bytes 9224 | tf_op jit(solution)/shard_map/ppermute | solution.py:333
  5.6 1.2 %collective-permute-start = (bf16[24,1536]{1,0:T(8,128)(2,1)S(1)}, bf16[24,1536]{1,0:T(8,128)(2,1)S(1)}, u32[]{:S(2)}, u32[]{:S(2)}) collective-permute-start(bf16[24,1536]{1,0:T(8,128)(2,1)S(1)} %get-tuple-element.15), channel_id=1, source_target_pairs={{0,2},{1,3},{2,0},{3,1},{4,6},{5,7},{6,4},{7,5},{8,10},{9,11},{10,... | collective-permute-start | bytes 221192 | tf_op jit(solution)/shard_map/ppermute | solution.py:333
  6.8 0.2 collective-permute-start.4
  7.1 0.0 collective-permute-done.7
  7.1 0.1 collective-permute-start.8
  7.2 1.9 %collective-permute-done = bf16[24,1536]{1,0:T(8,128)(2,1)S(1)} collective-permute-done((bf16[24,1536]{1,0:T(8,128)(2,1)S(1)}, bf16[24,1536]{1,0:T(8,128)(2,1)S(1)}, u32[]{:S(2)}, u32[]{:S(2)}) %collective-permute-start) | collective-permute-done | bytes 73760 | tf_op jit(solution)/shard_map/ppermute | solution.py:333
  9.1 2.3 %collective-permute-start.1 = (bf16[48,1536]{1,0:T(8,128)(2,1)S(1)}, bf16[48,1536]{1,0:T(8,128)(2,1)S(1)}, u32[]{:S(2)}, u32[]{:S(2)}) collective-permute-start(bf16[48,1536]{1,0:T(8,128)(2,1)S(1)} %pad_maximum_fusion.2), channel_id=1, source_target_pairs={{0,6},{1,7},{2,4},{3,5},{4,2},{5,3},{6,0},{7,1},{8,14},{9,15},{10,... | collective-permute-start | bytes 442376 | tf_op jit(solution)/shard_map/ppermute | solution.py:333
  11.3 0.0 collective-permute-done.8
  11.4 0.7 %broadcast_in_dim.2 = bf16[8,8,1536]{2,1,0:T(8,128)(2,1)} broadcast(bf16[8,1536]{1,0:T(8,128)(2,1)S(1)} %pad_maximum_fusion.3), dimensions={1,2} | broadcast | bytes 221184 | tf_op jit(solution)/shard_map/broadcast_in_dim | solution.py:355
  12.1 8.2 %all-to-all-start = ((bf16[8,8,1536]{2,1,0:T(8,128)(2,1)}), bf16[8,8,1536]{2,1,0:T(8,128)(2,1)S(1)}, u32[]{:S(2)}, u32[]{:S(2)}) async-start(bf16[8,8,1536]{2,1,0:T(8,128)(2,1)} %broadcast_in_dim.2), calls=%async_computation | async-start | bytes 393216 | tf_op jit(solution)/shard_map/all_to_all | solution.py:357
  20.3 0.0 collective-permute-done.1
  20.3 1.5 %collective-permute-start.2 = (bf16[64,1536]{1,0:T(8,128)(2,1)S(1)}, bf16[64,1536]{1,0:T(8,128)(2,1)S(1)}, u32[]{:S(2)}, u32[]{:S(2)}) collective-permute-start(bf16[64,1536]{1,0:T(8,128)(2,1)S(1)} %bitcast.9), channel_id=1, source_target_pairs={{0,8},{1,9},{2,10},{3,11},{4,12},{5,13},{6,14},{7,15},{8,0},{9,1},... | collective-permute-start | bytes 589832 | tf_op jit(solution)/shard_map/ppermute | solution.py:333
  21.9 0.0 collective-permute-done.4
  21.9 0.0 copy-start.2
  21.9 0.0 copy-start.4
  21.9 4.1 %collective-permute-start.5 = (bf16[128,1536]{1,0:T(8,128)(2,1)S(1)}, bf16[128,1536]{1,0:T(8,128)(2,1)S(1)}, u32[]{:S(2)}, u32[]{:S(2)}) collective-permute-start(bf16[128,1536]{1,0:T(8,128)(2,1)S(1)} %constant_dynamic-update-slice_fusion.a_ref), channel_id=1, source_target_pairs={{0,1},{1,0},{2,3},{3,2},{4,5},{5,4},{6,7},{7,6},{8,9},{9,8},{10,11... | collective-permute-start | bytes 1179656 | tf_op jit(solution)/shard_map/ppermute | solution.py:333
  26.0 1.6 %collective-permute-done.2 = bf16[64,1536]{1,0:T(8,128)(2,1)S(1)} collective-permute-done((bf16[64,1536]{1,0:T(8,128)(2,1)S(1)}, bf16[64,1536]{1,0:T(8,128)(2,1)S(1)}, u32[]{:S(2)}, u32[]{:S(2)}) %collective-permute-start.2) | collective-permute-done | bytes 196640 | tf_op jit(solution)/shard_map/ppermute | solution.py:333
  27.6 4.5 %collective-permute-start.3 = (bf16[128,1536]{1,0:T(8,128)(2,1)S(1)}, bf16[128,1536]{1,0:T(8,128)(2,1)S(1)}, u32[]{:S(2)}, u32[]{:S(2)}) collective-permute-start(bf16[128,1536]{1,0:T(8,128)(2,1)S(1)} %pad_maximum_fusion.a_ref), channel_id=1, source_target_pairs={{0,1},{1,0},{2,3},{3,2},{4,5},{5,4},{6,7},{7,6},{8,9},{9,8},{10,11... | collective-permute-start | bytes 1179656 | tf_op jit(solution)/shard_map/ppermute | solution.py:333
  32.1 0.1 collective-permute-start.6
  32.2 1.4 %shard_map.47.acc_ref = f32[256,896]{1,0:T(8,128)S(1)} custom-call(bf16[256,768]{1,0:T(8,128)(2,1)S(1)} %get-tuple-element.18.q_ref, bf16[256,768]{1,0:T(8,128)(2,1)S(1)} %copy-done.2, bf16[256,768]{1,0:T(8,128)(2,1)S(1)} %copy-done.4), custom_call_target="tpu_custom_call" | custom-call | flops 1000000000 | bytes 3000000 | tf_op jit(solution)/shard_map/pallas_call | solution.py:367
  33.6 0.0 collective-permute-done.6.qb_ref
  33.6 0.0 all-to-all-done
  33.6 2.4 %shard_map.50 = bf16[8,8,896]{2,1,0:T(8,128)(2,1)} custom-call(s32[1]{0:T(128)} %bitcast.pos_ref, bf16[32,768]{1,0:T(8,128)(2,1)S(1)} %slice_bitcast_fusion.qa_ref, bf16[32,768]{1,0:T(8,128)(2,1)S(1)} %collective-permute-done.6.qb_ref, bf16[64,1536]{1,0:T(8,128)(2,1)S(1)} %bitcast.6), custom_call_target="tpu_custom_call" | custom-call | flops 200000000 | bytes 600000 | tf_op jit(solution)/shard_map/pallas_call | solution.py:371
  36.1 3.8 %all-to-all-start.1 = ((bf16[8,8,896]{2,1,0:T(8,128)(2,1)}), bf16[8,8,896]{2,1,0:T(8,128)(2,1)S(1)}, u32[]{:S(2)}, u32[]{:S(2)}) async-start(bf16[8,8,896]{2,1,0:T(8,128)(2,1)} %shard_map.50), calls=%async_computation.1 | async-start | bytes 229376 | tf_op jit(solution)/shard_map/all_to_all | solution.py:376
  39.9 0.0 collective-permute-done.5.b_ref
  39.9 3.2 %shard_map.48.acc_ref = f32[256,896]{1,0:T(8,128)S(1)} custom-call(s32[5,12]{1,0:T(8,128)S(1)} %copy-done, s32[1]{0:T(128)} %bitcast.pos_ref, bf16[64,768]{1,0:T(8,128)(2,1)S(1)} %get-tuple-element.16.q1_ref, bf16[128,1536]{1,0:T(8,128)(2,1)S(1)} %constant_dynamic-update-slice_fusion.a_ref, bf16[128,1536]{1,0:T(8,128)(2,1)S(1)} %collective-permute-done.5.b_ref, ...), custom_call_target="tpu_custom_call" | custom-call | flops 600000000 | bytes 2000000 | tf_op jit(solution)/shard_map/pallas_call | solution.py:368
  43.1 0.0 collective-permute-done.3.b_ref
  43.1 3.2 %shard_map.49.acc_ref = f32[256,896]{1,0:T(8,128)S(1)} custom-call(s32[5,12]{1,0:T(8,128)S(1)} %copy-done, s32[1]{0:T(128)} %bitcast.pos_ref, bf16[16,768]{1,0:T(8,128)(2,1)S(1)} %get-tuple-element.14.q2_ref, bf16[128,1536]{1,0:T(8,128)(2,1)S(1)} %pad_maximum_fusion.a_ref, bf16[128,1536]{1,0:T(8,128)(2,1)S(1)} %collective-permute-done.3.b_ref, ...), custom_call_target="tpu_custom_call" | custom-call | flops 600000000 | bytes 2000000 | tf_op jit(solution)/shard_map/pallas_call | solution.py:377
  46.3 0.0 all-to-all-done.1.ret_ref
  46.3 2.0 %shard_map.51 = bf16[256,768]{1,0:T(8,128)(2,1)} custom-call(s32[5,12]{1,0:T(8,128)S(1)} %copy-done, f32[256,896]{1,0:T(8,128)S(1)} %shard_map.49.acc_ref, bf16[8,8,896]{2,1,0:T(8,128)(2,1)S(1)} %all-to-all-done.1.ret_ref), custom_call_target="tpu_custom_call" | custom-call | flops 1000000000 | bytes 3000000 | tf_op jit(solution)/shard_map/pallas_call | solution.py:380
  (16 shorter events, 0.2 us)
Async XLA Ops:
  1.9 5.1 %copy-start.1 = (bf16[256,768]{1,0:T(8,128)(2,1)}, bf16[256,768]{1,0:T(8,128)(2,1)S(1)}, u32[]{:S(2)}) copy-start(bf16[256,768]{1,0:T(8,128)(2,1)S(1)} %get-tuple-element.19.k_ref) | copy-start | bytes 1179652
  1.9 10.2 %copy-start.3 = (bf16[256,768]{1,0:T(8,128)(2,1)}, bf16[256,768]{1,0:T(8,128)(2,1)S(1)}, u32[]{:S(2)}) copy-start(bf16[256,768]{1,0:T(8,128)(2,1)S(1)} %get-tuple-element.20.v_ref) | copy-start | bytes 1179652
  1.9 5.1 %collective-permute-start.7 = (bf16[1,1536]{1,0:T(2,128)(2,1)S(1)}, bf16[1,1536]{1,0:T(2,128)(2,1)S(1)}, u32[]{:S(2)}, u32[]{:S(2)}) collective-permute-start(bf16[1,1536]{1,0:T(2,128)(2,1)S(1)} %get-tuple-element.22), channel_id=1, source_target_pairs={{0,192},{1,193},{2,194},{3,195},{4,196},{5,197},{6,198},{7,199},{8... | collective-permute-start | bytes 9224 | tf_op jit(solution)/shard_map/ppermute | solution.py:333
  5.6 3.5 %collective-permute-start = (bf16[24,1536]{1,0:T(8,128)(2,1)S(1)}, bf16[24,1536]{1,0:T(8,128)(2,1)S(1)}, u32[]{:S(2)}, u32[]{:S(2)}) collective-permute-start(bf16[24,1536]{1,0:T(8,128)(2,1)S(1)} %get-tuple-element.15), channel_id=1, source_target_pairs={{0,2},{1,3},{2,0},{3,1},{4,6},{5,7},{6,4},{7,5},{8,10},{9,11},{10,... | collective-permute-start | bytes 221192 | tf_op jit(solution)/shard_map/ppermute | solution.py:333
  6.8 15.1 %collective-permute-start.4 = (bf16[64,1536]{1,0:T(8,128)(2,1)S(1)}, bf16[64,1536]{1,0:T(8,128)(2,1)S(1)}, u32[]{:S(2)}, u32[]{:S(2)}) collective-permute-start(bf16[64,1536]{1,0:T(8,128)(2,1)S(1)} %get-tuple-element.17), channel_id=1, source_target_pairs={{0,2},{1,3},{2,0},{3,1},{4,6},{5,7},{6,4},{7,5},{8,10},{9,11},{10,... | collective-permute-start | bytes 589832 | tf_op jit(solution)/shard_map/ppermute | solution.py:333
  7.1 4.2 %collective-permute-start.8 = (bf16[2,1536]{1,0:T(2,128)(2,1)S(1)}, bf16[2,1536]{1,0:T(2,128)(2,1)S(1)}, u32[]{:S(2)}, u32[]{:S(2)}) collective-permute-start(bf16[2,1536]{1,0:T(2,128)(2,1)S(1)} %pad_maximum_fusion.4), channel_id=1, source_target_pairs={{0,64},{1,65},{2,66},{3,67},{4,68},{5,69},{6,70},{7,71},{8,72},{9,... | collective-permute-start | bytes 18440 | tf_op jit(solution)/shard_map/ppermute | solution.py:333
  9.1 11.2 %collective-permute-start.1 = (bf16[48,1536]{1,0:T(8,128)(2,1)S(1)}, bf16[48,1536]{1,0:T(8,128)(2,1)S(1)}, u32[]{:S(2)}, u32[]{:S(2)}) collective-permute-start(bf16[48,1536]{1,0:T(8,128)(2,1)S(1)} %pad_maximum_fusion.2), channel_id=1, source_target_pairs={{0,6},{1,7},{2,4},{3,5},{4,2},{5,3},{6,0},{7,1},{8,14},{9,15},{10,... | collective-permute-start | bytes 442376 | tf_op jit(solution)/shard_map/ppermute | solution.py:333
  12.1 21.5 %all-to-all-start = ((bf16[8,8,1536]{2,1,0:T(8,128)(2,1)}), bf16[8,8,1536]{2,1,0:T(8,128)(2,1)S(1)}, u32[]{:S(2)}, u32[]{:S(2)}) async-start(bf16[8,8,1536]{2,1,0:T(8,128)(2,1)} %broadcast_in_dim.2), calls=%async_computation | async-start | bytes 393216 | tf_op jit(solution)/shard_map/all_to_all | solution.py:357
  20.3 7.3 %collective-permute-start.2 = (bf16[64,1536]{1,0:T(8,128)(2,1)S(1)}, bf16[64,1536]{1,0:T(8,128)(2,1)S(1)}, u32[]{:S(2)}, u32[]{:S(2)}) collective-permute-start(bf16[64,1536]{1,0:T(8,128)(2,1)S(1)} %bitcast.9), channel_id=1, source_target_pairs={{0,8},{1,9},{2,10},{3,11},{4,12},{5,13},{6,14},{7,15},{8,0},{9,1},... | collective-permute-start | bytes 589832 | tf_op jit(solution)/shard_map/ppermute | solution.py:333
  21.9 10.3 %copy-start.2 = (bf16[256,768]{1,0:T(8,128)(2,1)S(1)}, bf16[256,768]{1,0:T(8,128)(2,1)}, u32[]{:S(2)}) copy-start(bf16[256,768]{1,0:T(8,128)(2,1)} %copy-done.1) | copy-start | bytes 1179652
  21.9 10.3 %copy-start.4 = (bf16[256,768]{1,0:T(8,128)(2,1)S(1)}, bf16[256,768]{1,0:T(8,128)(2,1)}, u32[]{:S(2)}) copy-start(bf16[256,768]{1,0:T(8,128)(2,1)} %copy-done.3) | copy-start | bytes 1179652
  21.9 18.0 %collective-permute-start.5 = (bf16[128,1536]{1,0:T(8,128)(2,1)S(1)}, bf16[128,1536]{1,0:T(8,128)(2,1)S(1)}, u32[]{:S(2)}, u32[]{:S(2)}) collective-permute-start(bf16[128,1536]{1,0:T(8,128)(2,1)S(1)} %constant_dynamic-update-slice_fusion.a_ref), channel_id=1, source_target_pairs={{0,1},{1,0},{2,3},{3,2},{4,5},{5,4},{6,7},{7,6},{8,9},{9,8},{10,11... | collective-permute-start | bytes 1179656 | tf_op jit(solution)/shard_map/ppermute | solution.py:333
  27.6 15.5 %collective-permute-start.3 = (bf16[128,1536]{1,0:T(8,128)(2,1)S(1)}, bf16[128,1536]{1,0:T(8,128)(2,1)S(1)}, u32[]{:S(2)}, u32[]{:S(2)}) collective-permute-start(bf16[128,1536]{1,0:T(8,128)(2,1)S(1)} %pad_maximum_fusion.a_ref), channel_id=1, source_target_pairs={{0,1},{1,0},{2,3},{3,2},{4,5},{5,4},{6,7},{7,6},{8,9},{9,8},{10,11... | collective-permute-start | bytes 1179656 | tf_op jit(solution)/shard_map/ppermute | solution.py:333
  32.1 1.5 %collective-permute-start.6 = (bf16[32,768]{1,0:T(8,128)(2,1)S(1)}, bf16[32,768]{1,0:T(8,128)(2,1)S(1)}, u32[]{:S(2)}, u32[]{:S(2)}) collective-permute-start(bf16[32,768]{1,0:T(8,128)(2,1)S(1)} %slice_bitcast_fusion.qa_ref), channel_id=1, source_target_pairs={{0,1},{1,0},{2,3},{3,2},{4,5},{5,4},{6,7},{7,6},{8,9},{9,8},{10,11... | collective-permute-start | bytes 147464 | tf_op jit(solution)/shard_map/ppermute | solution.py:333
  36.1 3.8 %copy-start = (s32[5,12]{1,0:T(8,128)S(1)}, s32[5,12]{1,0:T(8,128)}, u32[]{:S(2)}) copy-start(s32[5,12]{1,0:T(8,128)} %off_ref.5) | copy-start | bytes 724
  36.1 10.3 %all-to-all-start.1 = ((bf16[8,8,896]{2,1,0:T(8,128)(2,1)}), bf16[8,8,896]{2,1,0:T(8,128)(2,1)S(1)}, u32[]{:S(2)}, u32[]{:S(2)}) async-start(bf16[8,8,896]{2,1,0:T(8,128)(2,1)} %shard_map.50), calls=%async_computation.1 | async-start | bytes 229376 | tf_op jit(solution)/shard_map/all_to_all | solution.py:376

commit v3 on v2

--- a/solution.py
+++ b/solution.py
@@ -252,7 +252,7 @@
     absorb(off_ref, 1, accs, stats, acc_ref, out_ref)
 
 
-def second_kernel(off_ref, pos_ref, q2_ref, a_ref, b_ref, acc_ref, out_ref):
+def second_kernel(pos_ref, q2_ref, a_ref, b_ref, out_ref):
     me = pos_ref[0]
     col = iota((1, TOK), 1)
     block = (col >> 4) & 3
@@ -260,7 +260,9 @@
     k_pos = (device & 15) * 16 + (col & 15)
     q_pos = (me & 15) * 16 + (iota((32, 1), 0) & 15)
     accs, stats = gathered(q2_ref, (a_ref, b_ref), 16, k_pos <= q_pos)
-    absorb(off_ref, 2, accs, stats, acc_ref, out_ref)
+    for pair in range(PAIRS):
+        out_ref[:, lanes_of(pair)] = accs[pair]
+    out_ref[:, WIDTH:WIDTH + LANES] = stats
 
 
 def split2(value):
@@ -275,7 +277,7 @@
     return dot_nn(jnp.concatenate([high, low], 1), spread)
 
 
-def final_kernel(off_ref, acc_ref, ret_ref, out_ref):
+def final_kernel(off_ref, acc_ref, second_ref, ret_ref, out_ref):
     lane = iota((8, LANES), 1)
     parts = []
     for number in range(8):
@@ -289,18 +291,23 @@
     rows = sum(
         spread[8 * number:8 * number + 8] * ret_ref[number, :, 0:WIDTH].astype(F32) for number in range(8)
     )
+    second = second_ref[:, WIDTH:WIDTH + LANES]
+    rows = jnp.concatenate([second_ref[:, 0:WIDTH], rows], 0)
+    peak = jnp.concatenate([second, peak], 0)
+    total = jnp.concatenate([pltpu.roll(second, LANES - STAT, 1), total], 0)
 
     def expanded(value, level):
-        if level == 3:
-            return jnp.concatenate([jnp.broadcast_to(value[r:r + 1], (64, LANES)) for r in range(4)], 0)
-        return jnp.broadcast_to(value[4:5], (TOK, LANES))
+        first = (0, 16, 20)[level - 2]
+        group = 4**level
+        pieces = [jnp.broadcast_to(value[first + r:first + r + 1], (group, LANES)) for r in range(TOK // group)]
+        return jnp.concatenate(pieces, 0)
 
     lane = iota((TOK, LANES), 1)
     tok = iota((TOK, LANES), 0)
     stat = acc_ref[:, WIDTH:WIDTH + LANES]
     level_peaks = [jnp.where(lane < HEADS, stat, 0.0)]
     level_totals = [pltpu.roll(stat, LANES - STAT, 1)]
-    for level in (3, 4):
+    for level in (2, 3, 4):
         kept = ((tok & (4**level - 1)) == head_row(off_ref, level, (1, LANES), True)) & (lane < HEADS)
         level_peaks.append(jnp.where(kept, expanded(peak, level), NEG))
         level_totals.append(expanded(total, level))
@@ -309,19 +316,21 @@
     denom = sum(share * value for share, value in zip(shares, level_totals))
     inverse = 1.0 / jnp.where(lane < HEADS, denom, 1.0)
     shares = [share * inverse for share in shares]
-    row_shares = [jnp.sum(shares[1][64 * r:64 * r + 64], axis=0, keepdims=True) for r in range(4)]
-    row_shares += [jnp.sum(shares[2], axis=0, keepdims=True), jnp.zeros((3, LANES), F32)]
+    row_shares = [jnp.sum(shares[1][16 * r:16 * r + 16], axis=0, keepdims=True) for r in range(16)]
+    row_shares += [jnp.sum(shares[2][64 * r:64 * r + 64], axis=0, keepdims=True) for r in range(4)]
+    row_shares += [jnp.sum(shares[3], axis=0, keepdims=True), jnp.zeros((3, LANES), F32)]
     rows = rows * over_lanes(jnp.concatenate(row_shares, 0))
     scale = over_lanes(shares[0])
     hits = [
-        iota((4**level, WIDTH), 0) == head_row(off_ref, level, (1, WIDTH), False) for level in (3, 4)
+        iota((4**level, WIDTH), 0) == head_row(off_ref, level, (1, WIDTH), False) for level in (2, 3, 4)
     ]
     for r in range(16):
         here = slice(16 * r, 16 * r + 16)
         inner = slice(16 * (r % 4), 16 * (r % 4) + 16)
         merged = scale[here] * acc_ref[here, 0:WIDTH]
-        merged = merged + jnp.where(hits[0][inner], rows[r // 4:r // 4 + 1], 0.0)
-        merged = merged + jnp.where(hits[1][here], rows[4:5], 0.0)
+        merged = merged + jnp.where(hits[0], rows[r:r + 1], 0.0)
+        merged = merged + jnp.where(hits[1][inner], rows[16 + r // 4:17 + r // 4], 0.0)
+        merged = merged + jnp.where(hits[2][here], rows[20:21], 0.0)
         out_ref[here, :] = merged.astype(BF16)
 
 
@@ -374,12 +383,12 @@
     )(me, asked, asked_other, far)
     groups = [list(range(first, first + 8)) for first in range(0, count, 8)]
     back = lax.all_to_all(partial, "ctx", 0, 0, axis_index_groups=groups)
-    (acc,) = call(second_kernel, [total], [SMEM, SMEM] + [VMEM] * 4, 600_000_000, 2_000_000, 16)(
-        offsets, me, q2, kv2, kv2_other, acc
-    )
+    (second,) = call(
+        second_kernel, [shaped(16, WIDTH + LANES, F32)], [SMEM] + [VMEM] * 3, 100_000_000, 900_000, 12
+    )(me, q2, kv2, kv2_other)
     (merged,) = call(
-        final_kernel, [shaped(TOK, WIDTH, BF16)], [SMEM, VMEM, VMEM], 1_000_000_000, 3_000_000, 16
-    )(offsets, acc, back)
+        final_kernel, [shaped(TOK, WIDTH, BF16)], [SMEM] + [VMEM] * 3, 1_000_000_000, 3_000_000, 16
+    )(offsets, acc, second, back)
     return merged
 
 

time: 48.7 us -> 48.3 us (level)
  Pallas kernels: 14.1 us -> 12.7 us
  waiting for transfers between devices: 3.49 us -> 4.83 us
    pallas_call x2, Pallas kernels: 5.21 us -> 3.77 us  [the longest x1 2.12 us: program(): call(final_kernel, [shaped(TOK, WIDTH, BF16)], [SMEM] + [VMEM] * 3, 10000...]
    ppermute x9, waiting for transfers between devices: 3.48 us -> 4.82 us  [traded(): lax.ppermute(value, 'ctx', [(source, source ^ mask) for source in range(c...]
  transfers between devices with their start and end apart: 11 -> 11, of which waited for: 2 -> 3; matrix products, arithmetic and copies ran while one was open for 2% -> 2% of each run, Pallas kernels for 21% -> 18%
where the time goes in v3:
time: 48.3 us; the launch traced here: 48 us
  starting transfers between devices  29.5 us (61%)
  Pallas kernels  12.7 us (26%)
  waiting for transfers between devices  4.83 us (10%)
  local copies, waits for them, and re-layouts  0.74 us (2%)
    ppermute x9, starting transfers between devices, traded(): lax.ppermute(value, 'ctx', [(source, source ^ mask) for source in range(c...  17.7 us
    all_to_all x1, starting transfers between devices, program(): lax.all_to_all(far, 'ctx', 0, 0, axis_index_groups=lines).reshape(64, wide)  8.19 us
    ppermute x9, waiting for transfers between devices, traded(): lax.ppermute(value, 'ctx', [(source, source ^ mask) for source in range(c...  4.82 us
    all_to_all x1, starting transfers between devices, program(): back = lax.all_to_all(partial, 'ctx', 0, 0, axis_index_groups=groups)  3.64 us
    pallas_call x1, Pallas kernels, program(): call(first_kernel, [total], [SMEM, SMEM] + [VMEM] * 4, 600000000, 2000000...  3.25 us
    pallas_call x1, Pallas kernels, program(): call(far_kernel, [jax.ShapeDtypeStruct((8, 8, WIDTH + LANES), BF16)], [SM...  2.44 us
    pallas_call x1, Pallas kernels, program(): call(final_kernel, [shaped(TOK, WIDTH, BF16)], [SMEM] + [VMEM] * 3, 10000...  2.12 us
    pallas_call x1, Pallas kernels, program(): call(select_kernel, [shaped(TOK, WIDTH, BF16)] * 3 + [shaped(64, WIDTH, B...  1.88 us
  transfers between devices with their start and end apart: 11, of which 3 were waited for; matrix products, arithmetic and copies ran while one was open for 2% of the time, Pallas kernels for 18%

profile of v3, /device:TPU:1, one launch (start us, length us, event | category | flops | bytes accessed | tf_op | source)
XLA Modules:
  0.0 48.0 jit_solution(14974818831678836471)
XLA Ops:
  0.0 1.9 %shard_map.46 = (bf16[256,768]{1,0:T(8,128)(2,1)S(1)}, bf16[256,768]{1,0:T(8,128)(2,1)S(1)}, bf16[256,768]{1,0:T(8,128)(2,1)S(1)}, bf16[64,768]{1,0:T(8,128)(2,1...) custom-call(s32[5,12]{1,0:T(8,128)} %off_ref.3, ...), custom_call_target="tpu_custom_call" | custom-call | flops 200000000 | bytes 2000000 | tf_op jit(solution)/shard_map/pallas_call | solution.py:354
  1.9 3.6 %collective-permute-start.7 = (bf16[1,1536]{1,0:T(2,128)(2,1)S(1)}, bf16[1,1536]{1,0:T(2,128)(2,1)S(1)}, u32[]{:S(2)}, u32[]{:S(2)}) collective-permute-start(bf16[1,1536]{1,0:T(2,128)(2,1)S(1)} %get-tuple-element.22), channel_id=1, source_target_pairs={{0,192},{1,193},{2,194},{3,195},{4,196},{5,197},{6,198},{7,199},{8... | collective-permute-start | bytes 9224 | tf_op jit(solution)/shard_map/ppermute | solution.py:342
  5.5 1.2 %collective-permute-start.2 = (bf16[24,1536]{1,0:T(8,128)(2,1)S(1)}, bf16[24,1536]{1,0:T(8,128)(2,1)S(1)}, u32[]{:S(2)}, u32[]{:S(2)}) collective-permute-start(bf16[24,1536]{1,0:T(8,128)(2,1)S(1)} %get-tuple-element.20), channel_id=1, source_target_pairs={{0,2},{1,3},{2,0},{3,1},{4,6},{5,7},{6,4},{7,5},{8,10},{9,11},{10,... | collective-permute-start | bytes 221192 | tf_op jit(solution)/shard_map/ppermute | solution.py:342
  6.7 0.2 collective-permute-start
  7.0 0.0 collective-permute-done.7
  7.1 0.1 collective-permute-start.8
  7.2 1.9 %collective-permute-done.2 = bf16[24,1536]{1,0:T(8,128)(2,1)S(1)} collective-permute-done((bf16[24,1536]{1,0:T(8,128)(2,1)S(1)}, bf16[24,1536]{1,0:T(8,128)(2,1)S(1)}, u32[]{:S(2)}, u32[]{:S(2)}) %collective-permute-start.2) | collective-permute-done | bytes 73760 | tf_op jit(solution)/shard_map/ppermute | solution.py:342
  9.0 2.3 %collective-permute-start.3 = (bf16[48,1536]{1,0:T(8,128)(2,1)S(1)}, bf16[48,1536]{1,0:T(8,128)(2,1)S(1)}, u32[]{:S(2)}, u32[]{:S(2)}) collective-permute-start(bf16[48,1536]{1,0:T(8,128)(2,1)S(1)} %pad_maximum_fusion.2), channel_id=1, source_target_pairs={{0,6},{1,7},{2,4},{3,5},{4,2},{5,3},{6,0},{7,1},{8,14},{9,15},{10,... | collective-permute-start | bytes 442376 | tf_op jit(solution)/shard_map/ppermute | solution.py:342
  11.3 0.0 collective-permute-done.8
  11.4 0.7 %broadcast_in_dim.2 = bf16[8,8,1536]{2,1,0:T(8,128)(2,1)} broadcast(bf16[8,1536]{1,0:T(8,128)(2,1)S(1)} %pad_maximum_fusion.3), dimensions={1,2} | broadcast | bytes 221184 | tf_op jit(solution)/shard_map/broadcast_in_dim | solution.py:364
  12.0 8.2 %all-to-all-start = ((bf16[8,8,1536]{2,1,0:T(8,128)(2,1)}), bf16[8,8,1536]{2,1,0:T(8,128)(2,1)S(1)}, u32[]{:S(2)}, u32[]{:S(2)}) async-start(bf16[8,8,1536]{2,1,0:T(8,128)(2,1)} %broadcast_in_dim.2), calls=%async_computation | async-start | bytes 393216 | tf_op jit(solution)/shard_map/all_to_all | solution.py:366
  20.2 0.0 collective-permute-done.3
  20.3 1.5 %collective-permute-start.4 = (bf16[64,1536]{1,0:T(8,128)(2,1)S(1)}, bf16[64,1536]{1,0:T(8,128)(2,1)S(1)}, u32[]{:S(2)}, u32[]{:S(2)}) collective-permute-start(bf16[64,1536]{1,0:T(8,128)(2,1)S(1)} %bitcast.9), channel_id=1, source_target_pairs={{0,8},{1,9},{2,10},{3,11},{4,12},{5,13},{6,14},{7,15},{8,0},{9,1},... | collective-permute-start | bytes 589832 | tf_op jit(solution)/shard_map/ppermute | solution.py:342
  21.8 0.0 collective-permute-done
  21.9 4.1 %collective-permute-start.1 = (bf16[128,1536]{1,0:T(8,128)(2,1)S(1)}, bf16[128,1536]{1,0:T(8,128)(2,1)S(1)}, u32[]{:S(2)}, u32[]{:S(2)}) collective-permute-start(bf16[128,1536]{1,0:T(8,128)(2,1)S(1)} %constant_dynamic-update-slice_fusion.a_ref), channel_id=1, source_target_pairs={{0,1},{1,0},{2,3},{3,2},{4,5},{5,4},{6,7},{7,6},{8,9},{9,8},{10,11... | collective-permute-start | bytes 1179656 | tf_op jit(solution)/shard_map/ppermute | solution.py:342
  26.0 1.6 %collective-permute-done.4 = bf16[64,1536]{1,0:T(8,128)(2,1)S(1)} collective-permute-done((bf16[64,1536]{1,0:T(8,128)(2,1)S(1)}, bf16[64,1536]{1,0:T(8,128)(2,1)S(1)}, u32[]{:S(2)}, u32[]{:S(2)}) %collective-permute-start.4) | collective-permute-done | bytes 196640 | tf_op jit(solution)/shard_map/ppermute | solution.py:342
  27.6 4.5 %collective-permute-start.5 = (bf16[128,1536]{1,0:T(8,128)(2,1)S(1)}, bf16[128,1536]{1,0:T(8,128)(2,1)S(1)}, u32[]{:S(2)}, u32[]{:S(2)}) collective-permute-start(bf16[128,1536]{1,0:T(8,128)(2,1)S(1)} %pad_maximum_fusion.a_ref), channel_id=1, source_target_pairs={{0,1},{1,0},{2,3},{3,2},{4,5},{5,4},{6,7},{7,6},{8,9},{9,8},{10,11... | collective-permute-start | bytes 1179656 | tf_op jit(solution)/shard_map/ppermute | solution.py:342
  32.1 0.1 collective-permute-start.6
  32.2 1.3 %collective-permute-done.6.qb_ref = bf16[32,768]{1,0:T(8,128)(2,1)S(1)} collective-permute-done((bf16[32,768]{1,0:T(8,128)(2,1)S(1)}, bf16[32,768]{1,0:T(8,128)(2,1)S(1)}, u32[]{:S(2)}, u32[]{:S(2)}) %collective-permute-start.6) | collective-permute-done | bytes 49184 | tf_op jit(solution)/shard_map/ppermute | solution.py:342
  33.5 0.0 all-to-all-done
  33.5 2.4 %shard_map.50 = bf16[8,8,896]{2,1,0:T(8,128)(2,1)} custom-call(s32[1]{0:T(128)} %bitcast.pos_ref, bf16[32,768]{1,0:T(8,128)(2,1)S(1)} %slice_bitcast_fusion.qa_ref, bf16[32,768]{1,0:T(8,128)(2,1)S(1)} %collective-permute-done.6.qb_ref, bf16[64,1536]{1,0:T(8,128)(2,1)S(1)} %bitcast.6), custom_call_target="tpu_custom_call" | custom-call | flops 200000000 | bytes 600000 | tf_op jit(solution)/shard_map/pallas_call | solution.py:380
  36.0 3.6 %all-to-all-start.1 = ((bf16[8,8,896]{2,1,0:T(8,128)(2,1)}), bf16[8,8,896]{2,1,0:T(8,128)(2,1)S(1)}, u32[]{:S(2)}, u32[]{:S(2)}) async-start(bf16[8,8,896]{2,1,0:T(8,128)(2,1)} %shard_map.50), calls=%async_computation.1 | async-start | bytes 229376 | tf_op jit(solution)/shard_map/all_to_all | solution.py:385
  39.6 0.0 copy-start
  39.6 1.3 %shard_map.47.acc_ref = f32[256,896]{1,0:T(8,128)S(1)} custom-call(bf16[256,768]{1,0:T(8,128)(2,1)S(1)} %get-tuple-element.16.q_ref, bf16[256,768]{1,0:T(8,128)(2,1)S(1)} %get-tuple-element.17.k_ref, bf16[256,768]{1,0:T(8,128)(2,1)S(1)} %get-tuple-element.18.v_ref), custom_call_target="tpu_custom_call" | custom-call | flops 1000000000 | bytes 3000000 | tf_op jit(solution)/shard_map/pallas_call | solution.py:376
  41.0 0.0 collective-permute-done.1.b_ref
  41.0 0.0 copy-done
  41.0 3.3 %shard_map.48.acc_ref = f32[256,896]{1,0:T(8,128)S(1)} custom-call(s32[5,12]{1,0:T(8,128)S(1)} %copy-done, s32[1]{0:T(128)} %bitcast.pos_ref, bf16[64,768]{1,0:T(8,128)(2,1)S(1)} %get-tuple-element.14.q1_ref, bf16[128,1536]{1,0:T(8,128)(2,1)S(1)} %constant_dynamic-update-slice_fusion.a_ref, bf16[128,1536]{1,0:T(8,128)(2,1)S(1)} %collective-permute-done.1.b_ref, ...), custom_call_target="tpu_custom_call" | custom-call | flops 600000000 | bytes 2000000 | tf_op jit(solution)/shard_map/pallas_call | solution.py:377
  44.2 0.0 collective-permute-done.5.b_ref
  44.2 1.6 %shard_map.49.second_ref = f32[16,896]{1,0:T(8,128)S(1)} custom-call(s32[1]{0:T(128)} %bitcast.pos_ref, bf16[16,768]{1,0:T(8,128)(2,1)S(1)} %get-tuple-element.19.q2_ref, bf16[128,1536]{1,0:T(8,128)(2,1)S(1)} %pad_maximum_fusion.a_ref, bf16[128,1536]{1,0:T(8,128)(2,1)S(1)} %collective-permute-done.5.b_ref), custom_call_target="tpu_custom_call" | custom-call | flops 100000000 | bytes 900000 | tf_op jit(solution)/shard_map/pallas_call | solution.py:386
  45.9 0.0 all-to-all-done.1.ret_ref
  45.9 2.1 %shard_map.51 = bf16[256,768]{1,0:T(8,128)(2,1)} custom-call(s32[5,12]{1,0:T(8,128)S(1)} %copy-done, f32[256,896]{1,0:T(8,128)S(1)} %shard_map.48.acc_ref, f32[16,896]{1,0:T(8,128)S(1)} %shard_map.49.second_ref, bf16[8,8,896]{2,1,0:T(8,128)(2,1)S(1)} %all-to-all-done.1.ret_ref), custom_call_target="tpu_custom_call" | custom-call | flops 1000000000 | bytes 3000000 | tf_op jit(solution)/shard_map/pallas_call | solution.py:389
  (9 shorter events, 0.2 us)
Async XLA Ops:
  1.9 5.1 %collective-permute-start.7 = (bf16[1,1536]{1,0:T(2,128)(2,1)S(1)}, bf16[1,1536]{1,0:T(2,128)(2,1)S(1)}, u32[]{:S(2)}, u32[]{:S(2)}) collective-permute-start(bf16[1,1536]{1,0:T(2,128)(2,1)S(1)} %get-tuple-element.22), channel_id=1, source_target_pairs={{0,192},{1,193},{2,194},{3,195},{4,196},{5,197},{6,198},{7,199},{8... | collective-permute-start | bytes 9224 | tf_op jit(solution)/shard_map/ppermute | solution.py:342
  5.5 3.5 %collective-permute-start.2 = (bf16[24,1536]{1,0:T(8,128)(2,1)S(1)}, bf16[24,1536]{1,0:T(8,128)(2,1)S(1)}, u32[]{:S(2)}, u32[]{:S(2)}) collective-permute-start(bf16[24,1536]{1,0:T(8,128)(2,1)S(1)} %get-tuple-element.20), channel_id=1, source_target_pairs={{0,2},{1,3},{2,0},{3,1},{4,6},{5,7},{6,4},{7,5},{8,10},{9,11},{10,... | collective-permute-start | bytes 221192 | tf_op jit(solution)/shard_map/ppermute | solution.py:342
  6.7 15.1 %collective-permute-start = (bf16[64,1536]{1,0:T(8,128)(2,1)S(1)}, bf16[64,1536]{1,0:T(8,128)(2,1)S(1)}, u32[]{:S(2)}, u32[]{:S(2)}) collective-permute-start(bf16[64,1536]{1,0:T(8,128)(2,1)S(1)} %get-tuple-element.15), channel_id=1, source_target_pairs={{0,2},{1,3},{2,0},{3,1},{4,6},{5,7},{6,4},{7,5},{8,10},{9,11},{10,... | collective-permute-start | bytes 589832 | tf_op jit(solution)/shard_map/ppermute | solution.py:342
  7.1 4.3 %collective-permute-start.8 = (bf16[2,1536]{1,0:T(2,128)(2,1)S(1)}, bf16[2,1536]{1,0:T(2,128)(2,1)S(1)}, u32[]{:S(2)}, u32[]{:S(2)}) collective-permute-start(bf16[2,1536]{1,0:T(2,128)(2,1)S(1)} %pad_maximum_fusion.4), channel_id=1, source_target_pairs={{0,64},{1,65},{2,66},{3,67},{4,68},{5,69},{6,70},{7,71},{8,72},{9,... | collective-permute-start | bytes 18440 | tf_op jit(solution)/shard_map/ppermute | solution.py:342
  9.0 11.2 %collective-permute-start.3 = (bf16[48,1536]{1,0:T(8,128)(2,1)S(1)}, bf16[48,1536]{1,0:T(8,128)(2,1)S(1)}, u32[]{:S(2)}, u32[]{:S(2)}) collective-permute-start(bf16[48,1536]{1,0:T(8,128)(2,1)S(1)} %pad_maximum_fusion.2), channel_id=1, source_target_pairs={{0,6},{1,7},{2,4},{3,5},{4,2},{5,3},{6,0},{7,1},{8,14},{9,15},{10,... | collective-permute-start | bytes 442376 | tf_op jit(solution)/shard_map/ppermute | solution.py:342
  12.0 21.5 %all-to-all-start = ((bf16[8,8,1536]{2,1,0:T(8,128)(2,1)}), bf16[8,8,1536]{2,1,0:T(8,128)(2,1)S(1)}, u32[]{:S(2)}, u32[]{:S(2)}) async-start(bf16[8,8,1536]{2,1,0:T(8,128)(2,1)} %broadcast_in_dim.2), calls=%async_computation | async-start | bytes 393216 | tf_op jit(solution)/shard_map/all_to_all | solution.py:366
  20.3 7.3 %collective-permute-start.4 = (bf16[64,1536]{1,0:T(8,128)(2,1)S(1)}, bf16[64,1536]{1,0:T(8,128)(2,1)S(1)}, u32[]{:S(2)}, u32[]{:S(2)}) collective-permute-start(bf16[64,1536]{1,0:T(8,128)(2,1)S(1)} %bitcast.9), channel_id=1, source_target_pairs={{0,8},{1,9},{2,10},{3,11},{4,12},{5,13},{6,14},{7,15},{8,0},{9,1},... | collective-permute-start | bytes 589832 | tf_op jit(solution)/shard_map/ppermute | solution.py:342
  21.9 19.1 %collective-permute-start.1 = (bf16[128,1536]{1,0:T(8,128)(2,1)S(1)}, bf16[128,1536]{1,0:T(8,128)(2,1)S(1)}, u32[]{:S(2)}, u32[]{:S(2)}) collective-permute-start(bf16[128,1536]{1,0:T(8,128)(2,1)S(1)} %constant_dynamic-update-slice_fusion.a_ref), channel_id=1, source_target_pairs={{0,1},{1,0},{2,3},{3,2},{4,5},{5,4},{6,7},{7,6},{8,9},{9,8},{10,11... | collective-permute-start | bytes 1179656 | tf_op jit(solution)/shard_map/ppermute | solution.py:342
  27.6 16.6 %collective-permute-start.5 = (bf16[128,1536]{1,0:T(8,128)(2,1)S(1)}, bf16[128,1536]{1,0:T(8,128)(2,1)S(1)}, u32[]{:S(2)}, u32[]{:S(2)}) collective-permute-start(bf16[128,1536]{1,0:T(8,128)(2,1)S(1)} %pad_maximum_fusion.a_ref), channel_id=1, source_target_pairs={{0,1},{1,0},{2,3},{3,2},{4,5},{5,4},{6,7},{7,6},{8,9},{9,8},{10,11... | collective-permute-start | bytes 1179656 | tf_op jit(solution)/shard_map/ppermute | solution.py:342
  32.1 1.4 %collective-permute-start.6 = (bf16[32,768]{1,0:T(8,128)(2,1)S(1)}, bf16[32,768]{1,0:T(8,128)(2,1)S(1)}, u32[]{:S(2)}, u32[]{:S(2)}) collective-permute-start(bf16[32,768]{1,0:T(8,128)(2,1)S(1)} %slice_bitcast_fusion.qa_ref), channel_id=1, source_target_pairs={{0,1},{1,0},{2,3},{3,2},{4,5},{5,4},{6,7},{7,6},{8,9},{9,8},{10,11... | collective-permute-start | bytes 147464 | tf_op jit(solution)/shard_map/ppermute | solution.py:342
  36.0 9.9 %all-to-all-start.1 = ((bf16[8,8,896]{2,1,0:T(8,128)(2,1)}), bf16[8,8,896]{2,1,0:T(8,128)(2,1)S(1)}, u32[]{:S(2)}, u32[]{:S(2)}) async-start(bf16[8,8,896]{2,1,0:T(8,128)(2,1)} %shard_map.50), calls=%async_computation.1 | async-start | bytes 229376 | tf_op jit(solution)/shard_map/all_to_all | solution.py:385
  39.6 1.4 %copy-start = (s32[5,12]{1,0:T(8,128)S(1)}, s32[5,12]{1,0:T(8,128)}, u32[]{:S(2)}) copy-start(s32[5,12]{1,0:T(8,128)} %off_ref.3) | copy-start | bytes 724

commit v4 on v3

--- a/solution.py
+++ b/solution.py
@@ -87,6 +87,8 @@
     base = jnp.where(row < 64, row * 4, jnp.where(row < 80, (row - 64) * 16, (row - 80) * 64))
     base = jnp.where(row < 84, base, 0)
     early_ref[16:24, WIDTH:2 * WIDTH] = jnp.zeros((8, WIDTH), BF16)
+    tile_row = iota((16, LANES), 0)
+    tile = jnp.zeros((16, LANES), F32)
     for pair in range(PAIRS):
         picks = []
         for side in range(2):
@@ -105,12 +107,16 @@
         q1_ref[:, at] = rows[0:64]
         q2_ref[:, at] = rows[64:80]
         early_ref[16:24, at] = rows[80:88]
-        for ref, here in ((k_ref, at), (v_ref, after)):
-            rows = join_heads(dot_nn(pick, ref[:, at])).astype(BF16)
+        for ref, here, number in ((k_ref, at, pair), (v_ref, after, PAIRS + pair)):
+            rows = join_heads(dot_nn(pick, ref[:, at]))
+            tile = jnp.where(tile_row == number, rows[84:85], tile)
+            rows = rows.astype(BF16)
             kv1_ref[:, here] = rows[0:64]
             early_ref[0:16, here] = rows[64:80]
             f3_ref[:, here] = rows[80:84]
-            f4_ref[:, here] = rows[84:85]
+    tile = tile.astype(BF16)
+    for number in range(32):
+        f4_ref[number] = tile
 
 
 def local_kernel(q_ref, k_ref, v_ref, acc_ref):
@@ -133,7 +139,7 @@
         acc_ref[here, WIDTH:WIDTH + LANES] = stats
 
 
-def far_kernel(pos_ref, qa_ref, qb_ref, kf_ref, out_ref):
+def far_kernel(pos_ref, qa_ref, qb_ref, ka_ref, kb_ref, k4_ref, out_ref, tiles_ref):
     me = pos_ref[0]
 
     def device_of(block):
@@ -143,12 +149,12 @@
     asker = device_of(col >> 3)
     q_row = col & 7
     row = iota((64, 1), 0)
-    k_row = row & 7
-    owner = (me - (me & 56)) + (row >> 3) * 8
-    far_owner = owner ^ ((k_row & 1) * 192) ^ (((k_row >> 1) & 1) * 64)
-    third = (owner & 63) * 4 + k_row <= jnp.where(q_row < 4, (asker & 63) * 4 + q_row, -1)
-    fourth = far_owner <= jnp.where(q_row == 4, asker, -1)
-    allowed = jnp.where(k_row < 4, third.astype(jnp.int32), fourth.astype(jnp.int32)) > 0
+    owner = me ^ (((row >> 2) & 1) * 32) ^ (((row >> 3) & 1) * 16) ^ (((row >> 4) & 1) * 8)
+    third = (owner & 63) * 4 + (row & 3) <= jnp.where(q_row < 4, (asker & 63) * 4 + q_row, -1)
+    owner = ((row >> 3) & 3) * 64 + (row & 7) * 8 + (me & 7)
+    fourth = owner <= jnp.where(q_row == 4, asker, -1)
+    allowed = jnp.where(row < 32, third.astype(jnp.int32), fourth.astype(jnp.int32)) > 0
+    tiles_ref[...] = k4_ref[...].astype(F32).reshape(512, LANES)
     stat_row = iota((32, 64), 0)
     stats = jnp.zeros((32, 64), F32)
     accs = []
@@ -156,12 +162,16 @@
         at = lanes_of(pair)
         vat = slice(WIDTH + pair * LANES, WIDTH + (pair + 1) * LANES)
         queries = split_heads(jnp.concatenate([qa_ref[:, at], qb_ref[:, at]], 0))
-        scores = jnp.where(allowed, dot_nt(kf_ref[:, at], queries), NEG)
+        keys = tiles_ref[pl.ds(pair, 32, stride=16), :].astype(BF16)
+        keys = jnp.concatenate([ka_ref[:, at], kb_ref[:, at], keys], 0)
+        values = tiles_ref[pl.ds(PAIRS + pair, 32, stride=16), :].astype(BF16)
+        values = jnp.concatenate([ka_ref[:, vat], kb_ref[:, vat], values], 0)
+        scores = jnp.where(allowed, dot_nt(keys, queries), NEG)
         peak = jnp.max(scores, axis=0, keepdims=True)
         weights = jnp.where(allowed, jnp.exp(scores - peak), 0.0)
         total = jnp.sum(weights, axis=0, keepdims=True)
         acc = lax.dot_general(
-            weights.astype(BF16), kf_ref[:, vat], (((0,), (0,)), ((), ())), preferred_element_type=F32
+            weights.astype(BF16), values, (((0,), (0,)), ((), ())), preferred_element_type=F32
         )
         accs.append(join_heads(acc).astype(BF16))
         for side in range(2):
@@ -355,15 +365,17 @@
         select_kernel,
         [shaped(TOK, WIDTH, BF16)] * 3
         + [shaped(64, WIDTH, BF16), shaped(16, WIDTH, BF16), shaped(64, wide, BF16), shaped(24, wide, BF16),
-           shaped(4, wide, BF16), shaped(1, wide, BF16)],
+           shaped(4, wide, BF16), jax.ShapeDtypeStruct((32, 16, LANES), BF16)],
         [pl.BlockSpec(memory_space=pltpu.HBM)] * 4, 200_000_000, 2_000_000, 12,
         [pltpu.SMEM((5, HEADS), jnp.int32), pltpu.SemaphoreType.DMA((4,))],
     )(*inputs)
-    fourth = grown(fourth, 192, count)
-    fourth = grown(fourth, 64, count)
-    far = jnp.broadcast_to(jnp.concatenate([third, fourth], 0)[None], (8, 8, wide))
-    lines = [[first + step for step in range(0, 64, 8)] for first in range(count) if not first & 56]
-    far = lax.all_to_all(far, "ctx", 0, 0, axis_index_groups=lines).reshape(64, wide)
+    planes = [
+        [first + step * 64 + line * 8 for step in range(4) for line in range(8)] for first in range(8)
+    ]
+    fourth = lax.all_to_all(fourth, "ctx", 0, 0, axis_index_groups=planes)
+    third = grown(third, 32, count)
+    third = grown(third, 16, count)
+    third_other = traded(third, 8, count)
     early = grown(early, 2, count)
     early = grown(early, 6, count).reshape(4, 24, wide)
     asked = early[:, 16:24, 0:WIDTH].reshape(32, WIDTH)
@@ -378,9 +390,9 @@
         offsets, me, q1, kv1, kv1_other, acc
     )
     (partial,) = call(
-        far_kernel, [jax.ShapeDtypeStruct((8, 8, WIDTH + LANES), BF16)], [SMEM] + [VMEM] * 3,
-        200_000_000, 600_000, 12,
-    )(me, asked, asked_other, far)
+        far_kernel, [jax.ShapeDtypeStruct((8, 8, WIDTH + LANES), BF16)], [SMEM] + [VMEM] * 5,
+        200_000_000, 600_000, 12, [pltpu.VMEM((512, LANES), F32)],
+    )(me, asked, asked_other, third, third_other, fourth)
     groups = [list(range(first, first + 8)) for first in range(0, count, 8)]
     back = lax.all_to_all(partial, "ctx", 0, 0, axis_index_groups=groups)
     (second,) = call(

time: 48.3 us -> 51.9 us (1.075)
  starting transfers between devices: 29.5 us -> 34.6 us
  waiting for transfers between devices: 4.83 us -> 3.32 us
  local copies, waits for them, and re-layouts: 0.74 us -> 0.05 us
  Pallas kernels: 12.7 us -> 13.3 us
    ppermute x9 -> x10, starting transfers between devices: 17.7 us -> 24.3 us  [traded(): lax.ppermute(value, 'ctx', [(source, source ^ mask) for source in range(c...]
    all_to_all x1, starting transfers between devices: 8.19 us -> 5.94 us  [program(): fourth = lax.all_to_all(fourth, 'ctx', 0, 0, axis_index_groups=planes)]
    ppermute x9 -> x10, waiting for transfers between devices: 4.82 us -> 3.31 us  [traded(): lax.ppermute(value, 'ctx', [(source, source ^ mask) for source in range(c...]
    all_to_all x1, starting transfers between devices: 3.64 us -> 4.41 us  [program(): back = lax.all_to_all(partial, 'ctx', 0, 0, axis_index_groups=groups)]
    broadcast_in_dim x1 -> x0, local copies, waits for them, and re-layouts: 0.69 us -> none  [program(): jnp.broadcast_to(jnp.concatenate([third, fourth], 0)[None], (8, 8, wide))]
    pallas_call x1, Pallas kernels: 1.88 us -> 2.54 us  [program(): call(select_kernel, [shaped(TOK, WIDTH, BF16)] * 3 + [shaped(64, WIDTH, B...]
  transfers between devices with their start and end apart: 11 -> 12, of which waited for: 3 -> 3; matrix products, arithmetic and copies ran while one was open for 2% -> 0% of each run, Pallas kernels for 18% -> 17%
where the time goes in v4:
time: 51.9 us; the launch traced here: 51.6 us
  starting transfers between devices  34.6 us (67%)
  Pallas kernels  13.3 us (26%)
  waiting for transfers between devices  3.32 us (6%)
    ppermute x10, starting transfers between devices, traded(): lax.ppermute(value, 'ctx', [(source, source ^ mask) for source in range(c...  24.3 us
    all_to_all x1, starting transfers between devices, program(): fourth = lax.all_to_all(fourth, 'ctx', 0, 0, axis_index_groups=planes)  5.94 us
    all_to_all x1, starting transfers between devices, program(): back = lax.all_to_all(partial, 'ctx', 0, 0, axis_index_groups=groups)  4.41 us
    ppermute x10, waiting for transfers between devices, traded(): lax.ppermute(value, 'ctx', [(source, source ^ mask) for source in range(c...  3.31 us
    pallas_call x1, Pallas kernels, program(): call(first_kernel, [total], [SMEM, SMEM] + [VMEM] * 4, 600000000, 2000000...  3.25 us
    pallas_call x1, Pallas kernels, program(): call(select_kernel, [shaped(TOK, WIDTH, BF16)] * 3 + [shaped(64, WIDTH, B...  2.54 us
    pallas_call x1, Pallas kernels, program(): call(far_kernel, [jax.ShapeDtypeStruct((8, 8, WIDTH + LANES), BF16)], [SM...  2.44 us
    pallas_call x1, Pallas kernels, program(): call(final_kernel, [shaped(TOK, WIDTH, BF16)], [SMEM] + [VMEM] * 3, 10000...  2.12 us
  transfers between devices with their start and end apart: 12, of which 3 were waited for; matrix products, arithmetic and copies ran while one was open for 0% of the time, Pallas kernels for 17%

profile of v4, /device:TPU:1, one launch (start us, length us, event | category | flops | bytes accessed | tf_op | source)
XLA Modules:
  0.0 51.6 jit_solution(15860990938024182033)
XLA Ops:
  0.0 2.5 %shard_map.46 = (bf16[256,768]{1,0:T(8,128)(2,1)S(1)}, bf16[256,768]{1,0:T(8,128)(2,1)S(1)}, bf16[256,768]{1,0:T(8,128)(2,1)S(1)}, bf16[64,768]{1,0:T(8,128)(2,1...) custom-call(s32[5,12]{1,0:T(8,128)} %off_ref.3, ...), custom_call_target="tpu_custom_call" | custom-call | flops 200000000 | bytes 2000000 | tf_op jit(solution)/shard_map/pallas_call | solution.py:364
  2.5 2.1 %collective-permute-start.2 = (bf16[24,1536]{1,0:T(8,128)(2,1)S(1)}, bf16[24,1536]{1,0:T(8,128)(2,1)S(1)}, u32[]{:S(2)}, u32[]{:S(2)}) collective-permute-start(bf16[24,1536]{1,0:T(8,128)(2,1)S(1)} %get-tuple-element.20), channel_id=1, source_target_pairs={{0,2},{1,3},{2,0},{3,1},{4,6},{5,7},{6,4},{7,5},{8,10},{9,11},{10,... | collective-permute-start | bytes 221192 | tf_op jit(solution)/shard_map/ppermute | solution.py:352
  4.7 6.9 %collective-permute-start.7 = (bf16[4,1536]{1,0:T(4,128)(2,1)S(1)}, bf16[4,1536]{1,0:T(4,128)(2,1)S(1)}, u32[]{:S(2)}, u32[]{:S(2)}) collective-permute-start(bf16[4,1536]{1,0:T(4,128)(2,1)S(1)} %get-tuple-element.21), channel_id=1, source_target_pairs={{0,32},{1,33},{2,34},{3,35},{4,36},{5,37},{6,38},{7,39},{8,40},{9,... | collective-permute-start | bytes 36872 | tf_op jit(solution)/shard_map/ppermute | solution.py:352
  11.6 5.9 %all-to-all-start = ((bf16[32,16,128]{2,1,0:T(8,128)(2,1)}), bf16[32,16,128]{2,1,0:T(8,128)(2,1)S(1)}, u32[]{:S(2)}, u32[]{:S(2)}) async-start(bf16[32,16,128]{2,1,0:T(8,128)(2,1)} %get-tuple-element.22), calls=%async_computation | async-start | bytes 262144 | tf_op jit(solution)/shard_map/all_to_all | solution.py:375
  17.5 0.3 collective-permute-start
  17.9 0.0 collective-permute-done.7
  17.9 2.2 %collective-permute-start.8 = (bf16[8,1536]{1,0:T(8,128)(2,1)S(1)}, bf16[8,1536]{1,0:T(8,128)(2,1)S(1)}, u32[]{:S(2)}, u32[]{:S(2)}) collective-permute-start(bf16[8,1536]{1,0:T(8,128)(2,1)S(1)} %pad_maximum_fusion.4), channel_id=1, source_target_pairs={{0,16},{1,17},{2,18},{3,19},{4,20},{5,21},{6,22},{7,23},{8,24},{9,... | collective-permute-start | bytes 73736 | tf_op jit(solution)/shard_map/ppermute | solution.py:352
  20.1 0.0 collective-permute-done.2
  20.2 2.6 %collective-permute-start.3 = (bf16[48,1536]{1,0:T(8,128)(2,1)S(1)}, bf16[48,1536]{1,0:T(8,128)(2,1)S(1)}, u32[]{:S(2)}, u32[]{:S(2)}) collective-permute-start(bf16[48,1536]{1,0:T(8,128)(2,1)S(1)} %pad_maximum_fusion.2), channel_id=1, source_target_pairs={{0,6},{1,7},{2,4},{3,5},{4,2},{5,3},{6,0},{7,1},{8,14},{9,15},{10,... | collective-permute-start | bytes 442376 | tf_op jit(solution)/shard_map/ppermute | solution.py:352
  22.7 0.0 collective-permute-done.8
  22.8 1.3 %collective-permute-start.9 = (bf16[16,1536]{1,0:T(8,128)(2,1)S(1)}, bf16[16,1536]{1,0:T(8,128)(2,1)S(1)}, u32[]{:S(2)}, u32[]{:S(2)}) collective-permute-start(bf16[16,1536]{1,0:T(8,128)(2,1)S(1)} %pad_maximum_fusion.3.ka_ref), channel_id=1, source_target_pairs={{0,8},{1,9},{2,10},{3,11},{4,12},{5,13},{6,14},{7,15},{8,0},{9,1},... | collective-permute-start | bytes 147464 | tf_op jit(solution)/shard_map/ppermute | solution.py:352
  24.0 1.7 %collective-permute-done.3 = bf16[48,1536]{1,0:T(8,128)(2,1)S(1)} collective-permute-done((bf16[48,1536]{1,0:T(8,128)(2,1)S(1)}, bf16[48,1536]{1,0:T(8,128)(2,1)S(1)}, u32[]{:S(2)}, u32[]{:S(2)}) %collective-permute-start.3) | collective-permute-done | bytes 147488 | tf_op jit(solution)/shard_map/ppermute | solution.py:352
  25.8 1.3 %collective-permute-start.4 = (bf16[64,1536]{1,0:T(8,128)(2,1)S(1)}, bf16[64,1536]{1,0:T(8,128)(2,1)S(1)}, u32[]{:S(2)}, u32[]{:S(2)}) collective-permute-start(bf16[64,1536]{1,0:T(8,128)(2,1)S(1)} %bitcast.7), channel_id=1, source_target_pairs={{0,8},{1,9},{2,10},{3,11},{4,12},{5,13},{6,14},{7,15},{8,0},{9,1},... | collective-permute-start | bytes 589832 | tf_op jit(solution)/shard_map/ppermute | solution.py:352
  27.1 0.0 collective-permute-done
  27.1 3.6 %collective-permute-start.1 = (bf16[128,1536]{1,0:T(8,128)(2,1)S(1)}, bf16[128,1536]{1,0:T(8,128)(2,1)S(1)}, u32[]{:S(2)}, u32[]{:S(2)}) collective-permute-start(bf16[128,1536]{1,0:T(8,128)(2,1)S(1)} %constant_dynamic-update-slice_fusion.a_ref), channel_id=1, source_target_pairs={{0,1},{1,0},{2,3},{3,2},{4,5},{5,4},{6,7},{7,6},{8,9},{9,8},{10,11... | collective-permute-start | bytes 1179656 | tf_op jit(solution)/shard_map/ppermute | solution.py:352
  30.7 0.3 collective-permute-done.4
  31.0 3.9 %collective-permute-start.5 = (bf16[128,1536]{1,0:T(8,128)(2,1)S(1)}, bf16[128,1536]{1,0:T(8,128)(2,1)S(1)}, u32[]{:S(2)}, u32[]{:S(2)}) collective-permute-start(bf16[128,1536]{1,0:T(8,128)(2,1)S(1)} %pad_maximum_fusion.a_ref), channel_id=1, source_target_pairs={{0,1},{1,0},{2,3},{3,2},{4,5},{5,4},{6,7},{7,6},{8,9},{9,8},{10,11... | collective-permute-start | bytes 1179656 | tf_op jit(solution)/shard_map/ppermute | solution.py:352
  34.9 0.1 collective-permute-start.6
  35.0 0.0 collective-permute-done.9.kb_ref
  35.0 0.0 all-to-all-done.k4_ref
  35.0 1.3 %collective-permute-done.6.qb_ref = bf16[32,768]{1,0:T(8,128)(2,1)S(1)} collective-permute-done((bf16[32,768]{1,0:T(8,128)(2,1)S(1)}, bf16[32,768]{1,0:T(8,128)(2,1)S(1)}, u32[]{:S(2)}, u32[]{:S(2)}) %collective-permute-start.6) | collective-permute-done | bytes 49184 | tf_op jit(solution)/shard_map/ppermute | solution.py:352
  36.3 2.4 %shard_map.50 = bf16[8,8,896]{2,1,0:T(8,128)(2,1)} custom-call(s32[1]{0:T(128)} %bitcast.pos_ref, bf16[32,768]{1,0:T(8,128)(2,1)S(1)} %slice_bitcast_fusion.qa_ref, bf16[32,768]{1,0:T(8,128)(2,1)S(1)} %collective-permute-done.6.qb_ref, bf16[16,1536]{1,0:T(8,128)(2,1)S(1)} %pad_maximum_fusion.3.ka_ref, bf16[16,1536]{1,0:T(8,128)(2,1)S(1)} %collective-permute-done.9.kb_ref, ...), custom_call_target="tpu_custom_call" | custom-call | flops 200000000 | bytes 600000 | tf_op jit(solution)/shard_map/pallas_call | solution.py:392
  38.7 4.4 %all-to-all-start.1 = ((bf16[8,8,896]{2,1,0:T(8,128)(2,1)}), bf16[8,8,896]{2,1,0:T(8,128)(2,1)S(1)}, u32[]{:S(2)}, u32[]{:S(2)}) async-start(bf16[8,8,896]{2,1,0:T(8,128)(2,1)} %shard_map.50), calls=%async_computation.1 | async-start | bytes 229376 | tf_op jit(solution)/shard_map/all_to_all | solution.py:397
  43.1 0.0 copy-start
  43.2 1.3 %shard_map.47.acc_ref = f32[256,896]{1,0:T(8,128)S(1)} custom-call(bf16[256,768]{1,0:T(8,128)(2,1)S(1)} %get-tuple-element.16.q_ref, bf16[256,768]{1,0:T(8,128)(2,1)S(1)} %get-tuple-element.17.k_ref, bf16[256,768]{1,0:T(8,128)(2,1)S(1)} %get-tuple-element.18.v_ref), custom_call_target="tpu_custom_call" | custom-call | flops 1000000000 | bytes 3000000 | tf_op jit(solution)/shard_map/pallas_call | solution.py:388
  44.5 0.0 collective-permute-done.1.b_ref
  44.5 0.0 copy-done
  44.5 3.3 %shard_map.48.acc_ref = f32[256,896]{1,0:T(8,128)S(1)} custom-call(s32[5,12]{1,0:T(8,128)S(1)} %copy-done, s32[1]{0:T(128)} %bitcast.pos_ref, bf16[64,768]{1,0:T(8,128)(2,1)S(1)} %get-tuple-element.14.q1_ref, bf16[128,1536]{1,0:T(8,128)(2,1)S(1)} %constant_dynamic-update-slice_fusion.a_ref, bf16[128,1536]{1,0:T(8,128)(2,1)S(1)} %collective-permute-done.1.b_ref, ...), custom_call_target="tpu_custom_call" | custom-call | flops 600000000 | bytes 2000000 | tf_op jit(solution)/shard_map/pallas_call | solution.py:389
  47.8 0.0 collective-permute-done.5.b_ref
  47.8 1.6 %shard_map.49.second_ref = f32[16,896]{1,0:T(8,128)S(1)} custom-call(s32[1]{0:T(128)} %bitcast.pos_ref, bf16[16,768]{1,0:T(8,128)(2,1)S(1)} %get-tuple-element.19.q2_ref, bf16[128,1536]{1,0:T(8,128)(2,1)S(1)} %pad_maximum_fusion.a_ref, bf16[128,1536]{1,0:T(8,128)(2,1)S(1)} %collective-permute-done.5.b_ref), custom_call_target="tpu_custom_call" | custom-call | flops 100000000 | bytes 900000 | tf_op jit(solution)/shard_map/pallas_call | solution.py:398
  49.4 0.0 all-to-all-done.1.ret_ref
  49.4 2.1 %shard_map.51 = bf16[256,768]{1,0:T(8,128)(2,1)} custom-call(s32[5,12]{1,0:T(8,128)S(1)} %copy-done, f32[256,896]{1,0:T(8,128)S(1)} %shard_map.48.acc_ref, f32[16,896]{1,0:T(8,128)S(1)} %shard_map.49.second_ref, bf16[8,8,896]{2,1,0:T(8,128)(2,1)S(1)} %all-to-all-done.1.ret_ref), custom_call_target="tpu_custom_call" | custom-call | flops 1000000000 | bytes 3000000 | tf_op jit(solution)/shard_map/pallas_call | solution.py:401
  (9 shorter events, 0.2 us)
Async XLA Ops:
  2.5 17.6 %collective-permute-start.2 = (bf16[24,1536]{1,0:T(8,128)(2,1)S(1)}, bf16[24,1536]{1,0:T(8,128)(2,1)S(1)}, u32[]{:S(2)}, u32[]{:S(2)}) collective-permute-start(bf16[24,1536]{1,0:T(8,128)(2,1)S(1)} %get-tuple-element.20), channel_id=1, source_target_pairs={{0,2},{1,3},{2,0},{3,1},{4,6},{5,7},{6,4},{7,5},{8,10},{9,11},{10,... | collective-permute-start | bytes 221192 | tf_op jit(solution)/shard_map/ppermute | solution.py:352
  4.7 13.2 %collective-permute-start.7 = (bf16[4,1536]{1,0:T(4,128)(2,1)S(1)}, bf16[4,1536]{1,0:T(4,128)(2,1)S(1)}, u32[]{:S(2)}, u32[]{:S(2)}) collective-permute-start(bf16[4,1536]{1,0:T(4,128)(2,1)S(1)} %get-tuple-element.21), channel_id=1, source_target_pairs={{0,32},{1,33},{2,34},{3,35},{4,36},{5,37},{6,38},{7,39},{8,40},{9,... | collective-permute-start | bytes 36872 | tf_op jit(solution)/shard_map/ppermute | solution.py:352
  11.6 23.4 %all-to-all-start = ((bf16[32,16,128]{2,1,0:T(8,128)(2,1)}), bf16[32,16,128]{2,1,0:T(8,128)(2,1)S(1)}, u32[]{:S(2)}, u32[]{:S(2)}) async-start(bf16[32,16,128]{2,1,0:T(8,128)(2,1)} %get-tuple-element.22), calls=%async_computation | async-start | bytes 262144 | tf_op jit(solution)/shard_map/all_to_all | solution.py:375
  17.5 9.5 %collective-permute-start = (bf16[64,1536]{1,0:T(8,128)(2,1)S(1)}, bf16[64,1536]{1,0:T(8,128)(2,1)S(1)}, u32[]{:S(2)}, u32[]{:S(2)}) collective-permute-start(bf16[64,1536]{1,0:T(8,128)(2,1)S(1)} %get-tuple-element.15), channel_id=1, source_target_pairs={{0,2},{1,3},{2,0},{3,1},{4,6},{5,7},{6,4},{7,5},{8,10},{9,11},{10,... | collective-permute-start | bytes 589832 | tf_op jit(solution)/shard_map/ppermute | solution.py:352
  17.9 4.8 %collective-permute-start.8 = (bf16[8,1536]{1,0:T(8,128)(2,1)S(1)}, bf16[8,1536]{1,0:T(8,128)(2,1)S(1)}, u32[]{:S(2)}, u32[]{:S(2)}) collective-permute-start(bf16[8,1536]{1,0:T(8,128)(2,1)S(1)} %pad_maximum_fusion.4), channel_id=1, source_target_pairs={{0,16},{1,17},{2,18},{3,19},{4,20},{5,21},{6,22},{7,23},{8,24},{9,... | collective-permute-start | bytes 73736 | tf_op jit(solution)/shard_map/ppermute | solution.py:352
  20.2 5.6 %collective-permute-start.3 = (bf16[48,1536]{1,0:T(8,128)(2,1)S(1)}, bf16[48,1536]{1,0:T(8,128)(2,1)S(1)}, u32[]{:S(2)}, u32[]{:S(2)}) collective-permute-start(bf16[48,1536]{1,0:T(8,128)(2,1)S(1)} %pad_maximum_fusion.2), channel_id=1, source_target_pairs={{0,6},{1,7},{2,4},{3,5},{4,2},{5,3},{6,0},{7,1},{8,14},{9,15},{10,... | collective-permute-start | bytes 442376 | tf_op jit(solution)/shard_map/ppermute | solution.py:352
  22.8 12.2 %collective-permute-start.9 = (bf16[16,1536]{1,0:T(8,128)(2,1)S(1)}, bf16[16,1536]{1,0:T(8,128)(2,1)S(1)}, u32[]{:S(2)}, u32[]{:S(2)}) collective-permute-start(bf16[16,1536]{1,0:T(8,128)(2,1)S(1)} %pad_maximum_fusion.3.ka_ref), channel_id=1, source_target_pairs={{0,8},{1,9},{2,10},{3,11},{4,12},{5,13},{6,14},{7,15},{8,0},{9,1},... | collective-permute-start | bytes 147464 | tf_op jit(solution)/shard_map/ppermute | solution.py:352
  25.8 5.1 %collective-permute-start.4 = (bf16[64,1536]{1,0:T(8,128)(2,1)S(1)}, bf16[64,1536]{1,0:T(8,128)(2,1)S(1)}, u32[]{:S(2)}, u32[]{:S(2)}) collective-permute-start(bf16[64,1536]{1,0:T(8,128)(2,1)S(1)} %bitcast.7), channel_id=1, source_target_pairs={{0,8},{1,9},{2,10},{3,11},{4,12},{5,13},{6,14},{7,15},{8,0},{9,1},... | collective-permute-start | bytes 589832 | tf_op jit(solution)/shard_map/ppermute | solution.py:352
  27.1 17.4 %collective-permute-start.1 = (bf16[128,1536]{1,0:T(8,128)(2,1)S(1)}, bf16[128,1536]{1,0:T(8,128)(2,1)S(1)}, u32[]{:S(2)}, u32[]{:S(2)}) collective-permute-start(bf16[128,1536]{1,0:T(8,128)(2,1)S(1)} %constant_dynamic-update-slice_fusion.a_ref), channel_id=1, source_target_pairs={{0,1},{1,0},{2,3},{3,2},{4,5},{5,4},{6,7},{7,6},{8,9},{9,8},{10,11... | collective-permute-start | bytes 1179656 | tf_op jit(solution)/shard_map/ppermute | solution.py:352
  31.0 16.8 %collective-permute-start.5 = (bf16[128,1536]{1,0:T(8,128)(2,1)S(1)}, bf16[128,1536]{1,0:T(8,128)(2,1)S(1)}, u32[]{:S(2)}, u32[]{:S(2)}) collective-permute-start(bf16[128,1536]{1,0:T(8,128)(2,1)S(1)} %pad_maximum_fusion.a_ref), channel_id=1, source_target_pairs={{0,1},{1,0},{2,3},{3,2},{4,5},{5,4},{6,7},{7,6},{8,9},{9,8},{10,11... | collective-permute-start | bytes 1179656 | tf_op jit(solution)/shard_map/ppermute | solution.py:352
  34.9 1.4 %collective-permute-start.6 = (bf16[32,768]{1,0:T(8,128)(2,1)S(1)}, bf16[32,768]{1,0:T(8,128)(2,1)S(1)}, u32[]{:S(2)}, u32[]{:S(2)}) collective-permute-start(bf16[32,768]{1,0:T(8,128)(2,1)S(1)} %slice_bitcast_fusion.qa_ref), channel_id=1, source_target_pairs={{0,1},{1,0},{2,3},{3,2},{4,5},{5,4},{6,7},{7,6},{8,9},{9,8},{10,11... | collective-permute-start | bytes 147464 | tf_op jit(solution)/shard_map/ppermute | solution.py:352
  38.7 10.7 %all-to-all-start.1 = ((bf16[8,8,896]{2,1,0:T(8,128)(2,1)}), bf16[8,8,896]{2,1,0:T(8,128)(2,1)S(1)}, u32[]{:S(2)}, u32[]{:S(2)}) async-start(bf16[8,8,896]{2,1,0:T(8,128)(2,1)} %shard_map.50), calls=%async_computation.1 | async-start | bytes 229376 | tf_op jit(solution)/shard_map/all_to_all | solution.py:397
  43.1 1.4 %copy-start = (s32[5,12]{1,0:T(8,128)S(1)}, s32[5,12]{1,0:T(8,128)}, u32[]{:S(2)}) copy-start(s32[5,12]{1,0:T(8,128)} %off_ref.3) | copy-start | bytes 724

commit v5 on v3

--- a/solution.py
+++ b/solution.py
@@ -61,44 +61,44 @@
     return stats
 
 
-def call(body, outs, in_specs, flops, nbytes, grant, scratch=()):
+def call(body, outs, in_specs, flops, nbytes, grant, scratch=(), space=pltpu.VMEM):
     return pl.pallas_call(
         body,
         scratch_shapes=scratch,
         compiler_params=pltpu.CompilerParams(vmem_limit_bytes=grant << 20),
         out_shape=outs,
         in_specs=in_specs,
-        out_specs=[VMEM] * len(outs),
+        out_specs=[pl.BlockSpec(memory_space=space)] * len(outs),
         cost_estimate=pl.CostEstimate(flops=flops, bytes_accessed=nbytes, transcendentals=0),
     )
 
 
 def select_kernel(
-    off_hbm, q_hbm, k_hbm, v_hbm, q_ref, k_ref, v_ref, q1_ref, q2_ref, kv1_ref, early_ref, f3_ref, f4_ref, off_ref, sems
+    off_hbm, q_hbm, k_hbm, v_hbm, q_ref, k_ref, v_ref, q1_ref, q2_ref, kv1_ref, early_ref, f3_ref, f4_ref, off_ref, pick_ref, sems
 ):
     pairs = ((off_hbm, off_ref), (q_hbm, q_ref), (k_hbm, k_ref), (v_hbm, v_ref))
     copies = [pltpu.make_async_copy(src, dst, sems.at[n]) for n, (src, dst) in enumerate(pairs)]
     for copy in copies:
         copy.start()
-    for copy in copies:
+    row = iota((SEL, LANES), 0)
+    tok = iota((SEL, LANES), 1)
+    base = jnp.where(row < 64, row * 4, jnp.where(row < 80, (row - 64) * 16, (row - 80) * 64))
+    base = jnp.where(row < 84, base, jnp.where(row < 85, 0, -4096))
+    early_ref[16:24, WIDTH:2 * WIDTH] = jnp.zeros((8, WIDTH), BF16)
+    copies[0].wait()
+    for head in range(HEADS):
+        off = jnp.where(
+            row < 64,
+            off_ref[1, head],
+            jnp.where(row < 80, off_ref[2, head], jnp.where(row < 84, off_ref[3, head], off_ref[4, head])),
+        )
+        place = base + off
+        pick = jnp.concatenate([jnp.where(tok == place, 1.0, 0.0), jnp.where(tok + LANES == place, 1.0, 0.0)], 1)
+        pick_ref[SEL * head:SEL * head + SEL, :] = pick.astype(BF16)
+    for copy in copies[1:]:
         copy.wait()
-    row = iota((SEL, TOK), 0)
-    tok = iota((SEL, TOK), 1)
-    base = jnp.where(row < 64, row * 4, jnp.where(row < 80, (row - 64) * 16, (row - 80) * 64))
-    base = jnp.where(row < 84, base, 0)
-    early_ref[16:24, WIDTH:2 * WIDTH] = jnp.zeros((8, WIDTH), BF16)
     for pair in range(PAIRS):
-        picks = []
-        for side in range(2):
-            head = 2 * pair + side
-            off = jnp.where(
-                row < 64,
-                off_ref[1, head],
-                jnp.where(row < 80, off_ref[2, head], jnp.where(row < 84, off_ref[3, head], off_ref[4, head])),
-            )
-            hit = (tok == base + off) & (row < 85)
-            picks.append(jnp.where(hit, 1.0, 0.0).astype(BF16))
-        pick = jnp.concatenate(picks, 0)
+        pick = pick_ref[2 * SEL * pair:2 * SEL * pair + 2 * SEL, :]
         at = lanes_of(pair)
         after = slice(WIDTH + pair * LANES, WIDTH + (pair + 1) * LANES)
         rows = join_heads(dot_nn(pick, q_ref[:, at]) * SCALE).astype(BF16)
@@ -133,8 +133,8 @@
         acc_ref[here, WIDTH:WIDTH + LANES] = stats
 
 
-def far_kernel(pos_ref, qa_ref, qb_ref, kf_ref, out_ref):
-    me = pos_ref[0]
+def far_kernel(qa_ref, qb_ref, kf_ref, out_ref):
+    me = lax.axis_index("ctx").astype(jnp.int32)
 
     def device_of(block):
         return me ^ ((block & 1) * 2) ^ (((block >> 1) & 1) * 6) ^ (block >> 2)
@@ -242,18 +242,22 @@
         out_ref[:, at] = scale0[:, at] * acc_ref[:, at] + added
 
 
-def first_kernel(off_ref, pos_ref, q1_ref, a_ref, b_ref, acc_ref, out_ref):
-    me = pos_ref[0]
+def first_kernel(off_ref, q1_ref, a_ref, b_ref, acc_ref, out_ref, offs_ref):
+    me = lax.axis_index("ctx").astype(jnp.int32)
     col = iota((1, TOK), 1)
     device = me ^ (((col >> 6) & 1) * 2) ^ (col >> 7)
     k_pos = (device & 3) * 64 + (col & 63)
     q_pos = (me & 3) * 64 + (iota((128, 1), 0) & 63)
     accs, stats = gathered(q1_ref, (a_ref, b_ref), 64, k_pos <= q_pos)
     absorb(off_ref, 1, accs, stats, acc_ref, out_ref)
-
-
-def second_kernel(pos_ref, q2_ref, a_ref, b_ref, out_ref):
-    me = pos_ref[0]
+    offs_ref[...] = jnp.zeros((8, WIDTH + LANES), jnp.int32)
+    for level in (2, 3, 4):
+        offs_ref[level:level + 1, 0:WIDTH] = head_row(off_ref, level, (1, WIDTH), False)
+        offs_ref[level:level + 1, WIDTH:WIDTH + LANES] = head_row(off_ref, level, (1, LANES), True)
+
+
+def second_kernel(q2_ref, a_ref, b_ref, out_ref):
+    me = lax.axis_index("ctx").astype(jnp.int32)
     col = iota((1, TOK), 1)
     block = (col >> 4) & 3
     device = me ^ ((block & 1) * 2) ^ ((block >> 1) * 6) ^ (((col >> 6) & 1) * 8) ^ (col >> 7)
@@ -277,7 +281,7 @@
     return dot_nn(jnp.concatenate([high, low], 1), spread)
 
 
-def final_kernel(off_ref, acc_ref, second_ref, ret_ref, out_ref):
+def final_kernel(offs_ref, acc_ref, second_ref, ret_ref, out_hbm, out_ref, sems):
     lane = iota((8, LANES), 1)
     parts = []
     for number in range(8):
@@ -308,7 +312,7 @@
     level_peaks = [jnp.where(lane < HEADS, stat, 0.0)]
     level_totals = [pltpu.roll(stat, LANES - STAT, 1)]
     for level in (2, 3, 4):
-        kept = ((tok & (4**level - 1)) == head_row(off_ref, level, (1, LANES), True)) & (lane < HEADS)
+        kept = ((tok & (4**level - 1)) == offs_ref[level:level + 1, WIDTH:WIDTH + LANES]) & (lane < HEADS)
         level_peaks.append(jnp.where(kept, expanded(peak, level), NEG))
         level_totals.append(expanded(total, level))
     best = functools.reduce(jnp.maximum, level_peaks)
@@ -322,8 +326,9 @@
     rows = rows * over_lanes(jnp.concatenate(row_shares, 0))
     scale = over_lanes(shares[0])
     hits = [
-        iota((4**level, WIDTH), 0) == head_row(off_ref, level, (1, WIDTH), False) for level in (2, 3, 4)
+        iota((4**level, WIDTH), 0) == offs_ref[level:level + 1, 0:WIDTH] for level in (2, 3, 4)
     ]
+    copies = []
     for r in range(16):
         here = slice(16 * r, 16 * r + 16)
         inner = slice(16 * (r % 4), 16 * (r % 4) + 16)
@@ -332,6 +337,12 @@
         merged = merged + jnp.where(hits[1][inner], rows[16 + r // 4:17 + r // 4], 0.0)
         merged = merged + jnp.where(hits[2][here], rows[20:21], 0.0)
         out_ref[here, :] = merged.astype(BF16)
+        if r % 4 == 3:
+            done = slice(64 * (r // 4), 64 * (r // 4) + 64)
+            copies.append(pltpu.make_async_copy(out_ref.at[done], out_hbm.at[done], sems.at[r // 4]))
+            copies[-1].start()
+    for copy in copies:
+        copy.wait()
 
 
 def shaped(rows, width, dtype):
@@ -348,7 +359,6 @@
 
 def program(queries, keys, values, offsets):
     count = lax.axis_size("ctx")
-    me = lax.axis_index("ctx").astype(jnp.int32).reshape(1)
     wide = 2 * WIDTH
     inputs = [pltpu.with_memory_space_constraint(a, pltpu.HBM) for a in (offsets, queries, keys, values)]
     q, k, v, q1, q2, kv1, early, third, fourth = call(
@@ -357,7 +367,7 @@
         + [shaped(64, WIDTH, BF16), shaped(16, WIDTH, BF16), shaped(64, wide, BF16), shaped(24, wide, BF16),
            shaped(4, wide, BF16), shaped(1, wide, BF16)],
         [pl.BlockSpec(memory_space=pltpu.HBM)] * 4, 200_000_000, 2_000_000, 12,
-        [pltpu.SMEM((5, HEADS), jnp.int32), pltpu.SemaphoreType.DMA((4,))],
+        [pltpu.SMEM((5, HEADS), jnp.int32), pltpu.VMEM((HEADS * SEL, TOK), BF16), pltpu.SemaphoreType.DMA((4,))],
     )(*inputs)
     fourth = grown(fourth, 192, count)
     fourth = grown(fourth, 64, count)
@@ -374,21 +384,23 @@
     kv2_other = traded(kv2, 1, count)
     total = shaped(TOK, WIDTH + LANES, F32)
     (acc,) = call(local_kernel, [total], [VMEM] * 3, 1_000_000_000, 3_000_000, 12)(q, k, v)
-    (acc,) = call(first_kernel, [total], [SMEM, SMEM] + [VMEM] * 4, 600_000_000, 2_000_000, 16)(
-        offsets, me, q1, kv1, kv1_other, acc
-    )
+    acc, places = call(
+        first_kernel, [total, jax.ShapeDtypeStruct((8, WIDTH + LANES), jnp.int32)], [SMEM] + [VMEM] * 4,
+        600_000_000, 2_000_000, 16,
+    )(offsets, q1, kv1, kv1_other, acc)
     (partial,) = call(
-        far_kernel, [jax.ShapeDtypeStruct((8, 8, WIDTH + LANES), BF16)], [SMEM] + [VMEM] * 3,
+        far_kernel, [jax.ShapeDtypeStruct((8, 8, WIDTH + LANES), BF16)], [VMEM] * 3,
         200_000_000, 600_000, 12,
-    )(me, asked, asked_other, far)
+    )(asked, asked_other, far)
     groups = [list(range(first, first + 8)) for first in range(0, count, 8)]
     back = lax.all_to_all(partial, "ctx", 0, 0, axis_index_groups=groups)
     (second,) = call(
-        second_kernel, [shaped(16, WIDTH + LANES, F32)], [SMEM] + [VMEM] * 3, 100_000_000, 900_000, 12
-    )(me, q2, kv2, kv2_other)
+        second_kernel, [shaped(16, WIDTH + LANES, F32)], [VMEM] * 3, 100_000_000, 900_000, 12
+    )(q2, kv2, kv2_other)
     (merged,) = call(
-        final_kernel, [shaped(TOK, WIDTH, BF16)], [SMEM] + [VMEM] * 3, 1_000_000_000, 3_000_000, 16
-    )(offsets, acc, second, back)
+        final_kernel, [shaped(TOK, WIDTH, BF16)], [VMEM] * 4, 1_000_000_000, 3_000_000, 16,
+        [pltpu.VMEM((TOK, WIDTH), BF16), pltpu.SemaphoreType.DMA((4,))], pltpu.HBM,
+    )(places, acc, second, back)
     return merged
 
 

time: 48.3 us -> 47.7 us (0.988)
  Pallas kernels: 12.7 us -> 12.1 us
    pallas_call x4, Pallas kernels: 9.46 us -> 8.86 us  [the longest x1 3.26 us: program(): call(first_kernel, [total, jax.ShapeDtypeStruct((8, WIDTH + LANES), jnp.i...]
where the time goes in v5:
time: 47.7 us; the launch traced here: 47.5 us
  starting transfers between devices  29.5 us (62%)
  Pallas kernels  12.1 us (25%)
  waiting for transfers between devices  4.83 us (10%)
  local copies, waits for them, and re-layouts  0.74 us (2%)
    ppermute x9, starting transfers between devices, traded(): lax.ppermute(value, 'ctx', [(source, source ^ mask) for source in range(c...  17.7 us
    all_to_all x1, starting transfers between devices, program(): lax.all_to_all(far, 'ctx', 0, 0, axis_index_groups=lines).reshape(64, wide)  8.18 us
    ppermute x9, waiting for transfers between devices, traded(): lax.ppermute(value, 'ctx', [(source, source ^ mask) for source in range(c...  4.82 us
    all_to_all x1, starting transfers between devices, program(): back = lax.all_to_all(partial, 'ctx', 0, 0, axis_index_groups=groups)  3.64 us
    pallas_call x1, Pallas kernels, program(): call(first_kernel, [total, jax.ShapeDtypeStruct((8, WIDTH + LANES), jnp.i...  3.26 us
    pallas_call x1, Pallas kernels, program(): call(far_kernel, [jax.ShapeDtypeStruct((8, 8, WIDTH + LANES), BF16)], [VM...  2.44 us
    pallas_call x1, Pallas kernels, program(): call(select_kernel, [shaped(TOK, WIDTH, BF16)] * 3 + [shaped(64, WIDTH, B...  1.9 us
    pallas_call x1, Pallas kernels, program(): call(second_kernel, [shaped(16, WIDTH + LANES, F32)], [VMEM] * 3, 1000000...  1.65 us
  transfers between devices with their start and end apart: 11, of which 3 were waited for; matrix products, arithmetic and copies ran while one was open for 2% of the time, Pallas kernels for 18%

profile of v5, /device:TPU:1, one launch (start us, length us, event | category | flops | bytes accessed | tf_op | source)
XLA Modules:
  0.0 47.5 jit_solution(13198198917837961100)
XLA Ops:
  0.0 1.9 %shard_map.46 = (bf16[256,768]{1,0:T(8,128)(2,1)S(1)}, bf16[256,768]{1,0:T(8,128)(2,1)S(1)}, bf16[256,768]{1,0:T(8,128)(2,1)S(1)}, bf16[64,768]{1,0:T(8,128)(2,1...) custom-call(s32[5,12]{1,0:T(8,128)} %off_ref.1, ...), custom_call_target="tpu_custom_call" | custom-call | flops 200000000 | bytes 2000000 | tf_op jit(solution)/shard_map/pallas_call | solution.py:364
  1.9 3.6 %collective-permute-start.7 = (bf16[1,1536]{1,0:T(2,128)(2,1)S(1)}, bf16[1,1536]{1,0:T(2,128)(2,1)S(1)}, u32[]{:S(2)}, u32[]{:S(2)}) collective-permute-start(bf16[1,1536]{1,0:T(2,128)(2,1)S(1)} %get-tuple-element.26), channel_id=1, source_target_pairs={{0,192},{1,193},{2,194},{3,195},{4,196},{5,197},{6,198},{7,199},{8... | collective-permute-start | bytes 9224 | tf_op jit(solution)/shard_map/ppermute | solution.py:353
  5.5 1.2 %collective-permute-start.2 = (bf16[24,1536]{1,0:T(8,128)(2,1)S(1)}, bf16[24,1536]{1,0:T(8,128)(2,1)S(1)}, u32[]{:S(2)}, u32[]{:S(2)}) collective-permute-start(bf16[24,1536]{1,0:T(8,128)(2,1)S(1)} %get-tuple-element.24), channel_id=1, source_target_pairs={{0,2},{1,3},{2,0},{3,1},{4,6},{5,7},{6,4},{7,5},{8,10},{9,11},{10,... | collective-permute-start | bytes 221192 | tf_op jit(solution)/shard_map/ppermute | solution.py:353
  6.8 0.3 collective-permute-start
  7.0 0.0 collective-permute-done.7
  7.1 0.1 collective-permute-start.8
  7.2 1.9 %collective-permute-done.2 = bf16[24,1536]{1,0:T(8,128)(2,1)S(1)} collective-permute-done((bf16[24,1536]{1,0:T(8,128)(2,1)S(1)}, bf16[24,1536]{1,0:T(8,128)(2,1)S(1)}, u32[]{:S(2)}, u32[]{:S(2)}) %collective-permute-start.2) | collective-permute-done | bytes 73760 | tf_op jit(solution)/shard_map/ppermute | solution.py:353
  9.1 2.3 %collective-permute-start.3 = (bf16[48,1536]{1,0:T(8,128)(2,1)S(1)}, bf16[48,1536]{1,0:T(8,128)(2,1)S(1)}, u32[]{:S(2)}, u32[]{:S(2)}) collective-permute-start(bf16[48,1536]{1,0:T(8,128)(2,1)S(1)} %pad_maximum_fusion.2), channel_id=1, source_target_pairs={{0,6},{1,7},{2,4},{3,5},{4,2},{5,3},{6,0},{7,1},{8,14},{9,15},{10,... | collective-permute-start | bytes 442376 | tf_op jit(solution)/shard_map/ppermute | solution.py:353
  11.3 0.0 collective-permute-done.8
  11.4 0.7 %broadcast_in_dim.2 = bf16[8,8,1536]{2,1,0:T(8,128)(2,1)} broadcast(bf16[8,1536]{1,0:T(8,128)(2,1)S(1)} %pad_maximum_fusion.3), dimensions={1,2} | broadcast | bytes 221184 | tf_op jit(solution)/shard_map/broadcast_in_dim | solution.py:374
  12.1 8.2 %all-to-all-start = ((bf16[8,8,1536]{2,1,0:T(8,128)(2,1)}), bf16[8,8,1536]{2,1,0:T(8,128)(2,1)S(1)}, u32[]{:S(2)}, u32[]{:S(2)}) async-start(bf16[8,8,1536]{2,1,0:T(8,128)(2,1)} %broadcast_in_dim.2), calls=%async_computation | async-start | bytes 393216 | tf_op jit(solution)/shard_map/all_to_all | solution.py:376
  20.2 0.0 collective-permute-done.3
  20.3 1.5 %collective-permute-start.4 = (bf16[64,1536]{1,0:T(8,128)(2,1)S(1)}, bf16[64,1536]{1,0:T(8,128)(2,1)S(1)}, u32[]{:S(2)}, u32[]{:S(2)}) collective-permute-start(bf16[64,1536]{1,0:T(8,128)(2,1)S(1)} %bitcast.8), channel_id=1, source_target_pairs={{0,8},{1,9},{2,10},{3,11},{4,12},{5,13},{6,14},{7,15},{8,0},{9,1},... | collective-permute-start | bytes 589832 | tf_op jit(solution)/shard_map/ppermute | solution.py:353
  21.8 0.0 collective-permute-done
  21.9 4.1 %collective-permute-start.1 = (bf16[128,1536]{1,0:T(8,128)(2,1)S(1)}, bf16[128,1536]{1,0:T(8,128)(2,1)S(1)}, u32[]{:S(2)}, u32[]{:S(2)}) collective-permute-start(bf16[128,1536]{1,0:T(8,128)(2,1)S(1)} %constant_dynamic-update-slice_fusion.a_ref), channel_id=1, source_target_pairs={{0,1},{1,0},{2,3},{3,2},{4,5},{5,4},{6,7},{7,6},{8,9},{9,8},{10,11... | collective-permute-start | bytes 1179656 | tf_op jit(solution)/shard_map/ppermute | solution.py:353
  26.0 1.6 %collective-permute-done.4 = bf16[64,1536]{1,0:T(8,128)(2,1)S(1)} collective-permute-done((bf16[64,1536]{1,0:T(8,128)(2,1)S(1)}, bf16[64,1536]{1,0:T(8,128)(2,1)S(1)}, u32[]{:S(2)}, u32[]{:S(2)}) %collective-permute-start.4) | collective-permute-done | bytes 196640 | tf_op jit(solution)/shard_map/ppermute | solution.py:353
  27.6 4.5 %collective-permute-start.5 = (bf16[128,1536]{1,0:T(8,128)(2,1)S(1)}, bf16[128,1536]{1,0:T(8,128)(2,1)S(1)}, u32[]{:S(2)}, u32[]{:S(2)}) collective-permute-start(bf16[128,1536]{1,0:T(8,128)(2,1)S(1)} %pad_maximum_fusion.a_ref), channel_id=1, source_target_pairs={{0,1},{1,0},{2,3},{3,2},{4,5},{5,4},{6,7},{7,6},{8,9},{9,8},{10,11... | collective-permute-start | bytes 1179656 | tf_op jit(solution)/shard_map/ppermute | solution.py:353
  32.1 0.1 collective-permute-start.6
  32.2 1.3 %collective-permute-done.6.qb_ref = bf16[32,768]{1,0:T(8,128)(2,1)S(1)} collective-permute-done((bf16[32,768]{1,0:T(8,128)(2,1)S(1)}, bf16[32,768]{1,0:T(8,128)(2,1)S(1)}, u32[]{:S(2)}, u32[]{:S(2)}) %collective-permute-start.6) | collective-permute-done | bytes 49184 | tf_op jit(solution)/shard_map/ppermute | solution.py:353
  33.5 0.0 all-to-all-done
  33.5 2.4 %shard_map.50 = bf16[8,8,896]{2,1,0:T(8,128)(2,1)} custom-call(bf16[32,768]{1,0:T(8,128)(2,1)S(1)} %slice_bitcast_fusion.qa_ref, bf16[32,768]{1,0:T(8,128)(2,1)S(1)} %collective-permute-done.6.qb_ref, bf16[64,1536]{1,0:T(8,128)(2,1)S(1)} %bitcast.5), custom_call_target="tpu_custom_call" | custom-call | flops 200000000 | bytes 600000 | tf_op jit(solution)/shard_map/pallas_call | solution.py:391
  36.0 3.6 %all-to-all-start.1 = ((bf16[8,8,896]{2,1,0:T(8,128)(2,1)}), bf16[8,8,896]{2,1,0:T(8,128)(2,1)S(1)}, u32[]{:S(2)}, u32[]{:S(2)}) async-start(bf16[8,8,896]{2,1,0:T(8,128)(2,1)} %shard_map.50), calls=%async_computation.1 | async-start | bytes 229376 | tf_op jit(solution)/shard_map/all_to_all | solution.py:396
  39.6 0.0 copy-start
  39.6 1.4 %shard_map.47.acc_ref = f32[256,896]{1,0:T(8,128)S(1)} custom-call(bf16[256,768]{1,0:T(8,128)(2,1)S(1)} %get-tuple-element.18.q_ref, bf16[256,768]{1,0:T(8,128)(2,1)S(1)} %get-tuple-element.19.k_ref, bf16[256,768]{1,0:T(8,128)(2,1)S(1)} %get-tuple-element.20.v_ref), custom_call_target="tpu_custom_call" | custom-call | flops 1000000000 | bytes 3000000 | tf_op jit(solution)/shard_map/pallas_call | solution.py:386
  41.0 0.0 collective-permute-done.1.b_ref
  41.0 0.0 copy-done
  41.0 3.3 %shard_map.48 = (f32[256,896]{1,0:T(8,128)S(1)}, s32[8,896]{1,0:T(8,128)S(1)}) custom-call(s32[5,12]{1,0:T(8,128)S(1)} %copy-done, bf16[64,768]{1,0:T(8,128)(2,1)S(1)} %get-tuple-element.16.q1_ref, bf16[128,1536]{1,0:T(8,128)(2,1)S(1)} %constant_dynamic-update-slice_fusion.a_ref, bf16[128,1536]{1,0:T(8,128)(2,1)S(1)} %collective-permute-done.1.b_ref, ...), custom_call_target="tpu_custom_call" | custom-call | flops 600000000 | bytes 2000000 | tf_op jit(solution)/shard_map/pallas_call | solution.py:387
  44.3 0.0 collective-permute-done.5.b_ref
  44.3 1.6 %shard_map.49.second_ref = f32[16,896]{1,0:T(8,128)S(1)} custom-call(bf16[16,768]{1,0:T(8,128)(2,1)S(1)} %get-tuple-element.23.q2_ref, bf16[128,1536]{1,0:T(8,128)(2,1)S(1)} %pad_maximum_fusion.a_ref, bf16[128,1536]{1,0:T(8,128)(2,1)S(1)} %collective-permute-done.5.b_ref), custom_call_target="tpu_custom_call" | custom-call | flops 100000000 | bytes 900000 | tf_op jit(solution)/shard_map/pallas_call | solution.py:397
  45.9 0.0 all-to-all-done.1.ret_ref
  45.9 1.5 %shard_map.51 = bf16[256,768]{1,0:T(8,128)(2,1)} custom-call(s32[8,896]{1,0:T(8,128)S(1)} %get-tuple-element.21.offs_ref, f32[256,896]{1,0:T(8,128)S(1)} %get-tuple-element.22.acc_ref, f32[16,896]{1,0:T(8,128)S(1)} %shard_map.49.second_ref, bf16[8,8,896]{2,1,0:T(8,128)(2,1)S(1)} %all-to-all-done.1.ret_ref), custom_call_target="tpu_custom_call" | custom-call | flops 1000000000 | bytes 3000000 | tf_op jit(solution)/shard_map/pallas_call | solution.py:400
  (9 shorter events, 0.2 us)
Async XLA Ops:
  1.9 5.1 %collective-permute-start.7 = (bf16[1,1536]{1,0:T(2,128)(2,1)S(1)}, bf16[1,1536]{1,0:T(2,128)(2,1)S(1)}, u32[]{:S(2)}, u32[]{:S(2)}) collective-permute-start(bf16[1,1536]{1,0:T(2,128)(2,1)S(1)} %get-tuple-element.26), channel_id=1, source_target_pairs={{0,192},{1,193},{2,194},{3,195},{4,196},{5,197},{6,198},{7,199},{8... | collective-permute-start | bytes 9224 | tf_op jit(solution)/shard_map/ppermute | solution.py:353
  5.5 3.5 %collective-permute-start.2 = (bf16[24,1536]{1,0:T(8,128)(2,1)S(1)}, bf16[24,1536]{1,0:T(8,128)(2,1)S(1)}, u32[]{:S(2)}, u32[]{:S(2)}) collective-permute-start(bf16[24,1536]{1,0:T(8,128)(2,1)S(1)} %get-tuple-element.24), channel_id=1, source_target_pairs={{0,2},{1,3},{2,0},{3,1},{4,6},{5,7},{6,4},{7,5},{8,10},{9,11},{10,... | collective-permute-start | bytes 221192 | tf_op jit(solution)/shard_map/ppermute | solution.py:353
  6.8 15.1 %collective-permute-start = (bf16[64,1536]{1,0:T(8,128)(2,1)S(1)}, bf16[64,1536]{1,0:T(8,128)(2,1)S(1)}, u32[]{:S(2)}, u32[]{:S(2)}) collective-permute-start(bf16[64,1536]{1,0:T(8,128)(2,1)S(1)} %get-tuple-element.17), channel_id=1, source_target_pairs={{0,2},{1,3},{2,0},{3,1},{4,6},{5,7},{6,4},{7,5},{8,10},{9,11},{10,... | collective-permute-start | bytes 589832 | tf_op jit(solution)/shard_map/ppermute | solution.py:353
  7.1 4.3 %collective-permute-start.8 = (bf16[2,1536]{1,0:T(2,128)(2,1)S(1)}, bf16[2,1536]{1,0:T(2,128)(2,1)S(1)}, u32[]{:S(2)}, u32[]{:S(2)}) collective-permute-start(bf16[2,1536]{1,0:T(2,128)(2,1)S(1)} %pad_maximum_fusion.4), channel_id=1, source_target_pairs={{0,64},{1,65},{2,66},{3,67},{4,68},{5,69},{6,70},{7,71},{8,72},{9,... | collective-permute-start | bytes 18440 | tf_op jit(solution)/shard_map/ppermute | solution.py:353
  9.1 11.2 %collective-permute-start.3 = (bf16[48,1536]{1,0:T(8,128)(2,1)S(1)}, bf16[48,1536]{1,0:T(8,128)(2,1)S(1)}, u32[]{:S(2)}, u32[]{:S(2)}) collective-permute-start(bf16[48,1536]{1,0:T(8,128)(2,1)S(1)} %pad_maximum_fusion.2), channel_id=1, source_target_pairs={{0,6},{1,7},{2,4},{3,5},{4,2},{5,3},{6,0},{7,1},{8,14},{9,15},{10,... | collective-permute-start | bytes 442376 | tf_op jit(solution)/shard_map/ppermute | solution.py:353
  12.1 21.5 %all-to-all-start = ((bf16[8,8,1536]{2,1,0:T(8,128)(2,1)}), bf16[8,8,1536]{2,1,0:T(8,128)(2,1)S(1)}, u32[]{:S(2)}, u32[]{:S(2)}) async-start(bf16[8,8,1536]{2,1,0:T(8,128)(2,1)} %broadcast_in_dim.2), calls=%async_computation | async-start | bytes 393216 | tf_op jit(solution)/shard_map/all_to_all | solution.py:376
  20.3 7.3 %collective-permute-start.4 = (bf16[64,1536]{1,0:T(8,128)(2,1)S(1)}, bf16[64,1536]{1,0:T(8,128)(2,1)S(1)}, u32[]{:S(2)}, u32[]{:S(2)}) collective-permute-start(bf16[64,1536]{1,0:T(8,128)(2,1)S(1)} %bitcast.8), channel_id=1, source_target_pairs={{0,8},{1,9},{2,10},{3,11},{4,12},{5,13},{6,14},{7,15},{8,0},{9,1},... | collective-permute-start | bytes 589832 | tf_op jit(solution)/shard_map/ppermute | solution.py:353
  21.9 19.1 %collective-permute-start.1 = (bf16[128,1536]{1,0:T(8,128)(2,1)S(1)}, bf16[128,1536]{1,0:T(8,128)(2,1)S(1)}, u32[]{:S(2)}, u32[]{:S(2)}) collective-permute-start(bf16[128,1536]{1,0:T(8,128)(2,1)S(1)} %constant_dynamic-update-slice_fusion.a_ref), channel_id=1, source_target_pairs={{0,1},{1,0},{2,3},{3,2},{4,5},{5,4},{6,7},{7,6},{8,9},{9,8},{10,11... | collective-permute-start | bytes 1179656 | tf_op jit(solution)/shard_map/ppermute | solution.py:353
  27.6 16.7 %collective-permute-start.5 = (bf16[128,1536]{1,0:T(8,128)(2,1)S(1)}, bf16[128,1536]{1,0:T(8,128)(2,1)S(1)}, u32[]{:S(2)}, u32[]{:S(2)}) collective-permute-start(bf16[128,1536]{1,0:T(8,128)(2,1)S(1)} %pad_maximum_fusion.a_ref), channel_id=1, source_target_pairs={{0,1},{1,0},{2,3},{3,2},{4,5},{5,4},{6,7},{7,6},{8,9},{9,8},{10,11... | collective-permute-start | bytes 1179656 | tf_op jit(solution)/shard_map/ppermute | solution.py:353
  32.1 1.4 %collective-permute-start.6 = (bf16[32,768]{1,0:T(8,128)(2,1)S(1)}, bf16[32,768]{1,0:T(8,128)(2,1)S(1)}, u32[]{:S(2)}, u32[]{:S(2)}) collective-permute-start(bf16[32,768]{1,0:T(8,128)(2,1)S(1)} %slice_bitcast_fusion.qa_ref), channel_id=1, source_target_pairs={{0,1},{1,0},{2,3},{3,2},{4,5},{5,4},{6,7},{7,6},{8,9},{9,8},{10,11... | collective-permute-start | bytes 147464 | tf_op jit(solution)/shard_map/ppermute | solution.py:353
  36.0 10.0 %all-to-all-start.1 = ((bf16[8,8,896]{2,1,0:T(8,128)(2,1)}), bf16[8,8,896]{2,1,0:T(8,128)(2,1)S(1)}, u32[]{:S(2)}, u32[]{:S(2)}) async-start(bf16[8,8,896]{2,1,0:T(8,128)(2,1)} %shard_map.50), calls=%async_computation.1 | async-start | bytes 229376 | tf_op jit(solution)/shard_map/all_to_all | solution.py:396
  39.6 1.4 %copy-start = (s32[5,12]{1,0:T(8,128)S(1)}, s32[5,12]{1,0:T(8,128)}, u32[]{:S(2)}) copy-start(s32[5,12]{1,0:T(8,128)} %off_ref.1) | copy-start | bytes 724
